TPU v7x, 32 devices: a whole 2x2x4 slice. The times are simulated.
32 devices in a mesh: seq: 16 (over z, x, core), rep: 2 (over y).
Axes of the slice: x: 2, y: 2, z: 4, core: 2. Of those that a mesh axis runs over, the one named last changes fastest.
Arguments:
- tokens: bfloat16 [2, 4096, 1024], P(None, 'seq'), may hold values from -6 to 6
- cotangent: bfloat16 [2, 4096, 1024], P(None, 'seq'), may hold values from -6 to 6
- domain_ids: int32 [2, 4096], P(None, 'seq'), may hold values from 0 to 7
- domain_counts: int32 [8], replicated, may hold values from 512 to 2047
- domain_weights: float32 [8], replicated, may hold values from 0.5 to 2
- seq_cuts: int32 [2], replicated, may hold values from 1024 to 4096, as said below
- attn_gain: float32 [2, 1024], replicated, may hold values from 0.1 to 1.9
- query_weight: bfloat16 [2, 1024, 1024], replicated, may hold values from -0.1875 to 0.1875
- latent_weight: bfloat16 [2, 1024, 512], replicated, may hold values from -0.1875 to 0.1875
- latent_up: bfloat16 [2, 256, 2048], replicated, may hold values from -0.375 to 0.375
- out_weight: bfloat16 [2, 1024, 1024], replicated, may hold values from -1.5 to 1.5
- out_bias: float32 [2, 1024], replicated, may hold values from -3 to 3
- mlp_gain: float32 [2, 1024], replicated, may hold values from 0.1 to 1.9
- gate_up_matrix: bfloat16 [2, 1024, 5632], replicated, may hold values from -0.1875 to 0.1875
- down_matrix: bfloat16 [2, 2816, 1024], replicated, may hold values from -0.109375 to 0.109375
Outputs:
- output: bfloat16 [2, 4096, 1024], P(None, 'seq')
- input_grad: bfloat16 [2, 4096, 1024], P(None, 'seq')
- attn_gain_grad: float32 [2, 1024], P(None, ('seq', 'rep'))
- query_weight_grad: float32 [2, 1024, 1024], P(None, ('seq', 'rep'))
- latent_weight_grad: float32 [2, 1024, 512], P(None, ('seq', 'rep'))
- latent_up_grad: float32 [2, 256, 2048], P(None, None, ('seq', 'rep'))
- out_weight_grad: float32 [2, 1024, 1024], P(None, None, ('seq', 'rep'))
- out_bias_grad: float32 [2, 1024], P(None, ('seq', 'rep'))
- mlp_gain_grad: float32 [2, 1024], P(None, ('seq', 'rep'))
- gate_up_grad: float32 [2, 1024, 5632], P(None, ('seq', 'rep'))
- down_weight_grad: float32 [2, 2816, 1024], P(None, None, ('seq', 'rep'))
Inputs may be any that keep to these rules, and one draw needn't show every extreme that they name: `seq_cuts`: each row holds one sequence before its cut and one from it on; in one row, drawn from the seed, the cut is 4096, so that row is a single sequence.
All inputs are finite; a program needn't handle non-finite values.
Results may differ from a plain program's by a relative error of at most 0.024.
Values may be sent and summed in bfloat16 or wider, within the bound.
No kernel may reach another device: no remote copies, remote signals or barrier semaphores. Data moves between devices by JAX's collectives and lax.ppermute only.
A program may use at most 320 MiB of HBM per device.

v0:
```python
import jax
import jax.numpy as jnp
from jax import lax
from jax.sharding import PartitionSpec as P

HD = 64
LAYERS = 2


NEG_FILL = -1e30


def rms_scale(value_rows):
    return lax.rsqrt(jnp.mean(value_rows * value_rows, axis=-1, keepdims=True) + 1e-06)


def norm_back(grad_in, value_rows, scale_rows, gain_vec):
    normed = value_rows * scale_rows
    upstream = grad_in * gain_vec
    return (
        scale_rows * (upstream - normed * jnp.mean(upstream * normed, axis=-1, keepdims=True)),
        grad_in * normed,
    )


def to_heads(value_rows, heads_per):
    seq_rows, loc_len, col_count = value_rows.shape
    head_size = col_count // heads_per
    return (
        value_rows.reshape(seq_rows, loc_len, heads_per, head_size)
        .transpose(0, 2, 1, 3)
        .reshape(seq_rows * heads_per, loc_len, head_size)
    )


def from_heads(value_rows, heads_per):
    piece_count, loc_len, head_size = value_rows.shape
    seq_rows = piece_count // heads_per
    return (
        value_rows.reshape(seq_rows, heads_per, loc_len, head_size)
        .transpose(0, 2, 1, 3)
        .reshape(seq_rows, loc_len, heads_per * head_size)
    )


def shards(
    tokens,
    cotangent,
    domain_ids,
    domain_counts,
    domain_weights,
    seq_cuts,
    attn_gain,
    query_weight,
    latent_weight,
    latent_up,
    out_weight,
    out_bias,
    mlp_gain,
    gate_up_matrix,
    down_matrix,
):
    seq_count = lax.axis_size("seq")
    rep_count = lax.axis_size("rep")
    seq_place = lax.axis_index("seq")
    own_group = lax.axis_index("rep")
    seq_rows, loc_len, width = tokens.shape
    full_len = loc_len * seq_count
    tok_rows = seq_rows * loc_len
    half_rows = tok_rows // rep_count
    half_first = own_group * half_rows
    heads_dim = query_weight.shape[2]
    group_cols = heads_dim // rep_count
    heads_per = group_cols // HD
    latent_size = latent_up.shape[1]
    hidden_size = down_matrix.shape[1]
    att_scale = HD ** (-0.5)
    block_rows = min(512, full_len)
    block_count = full_len // block_rows
    head_global = own_group * heads_per + seq_place % heads_per
    cut_here = seq_cuts[seq_place // heads_per]
    block_firsts = jnp.arange(block_count, dtype=jnp.int32) * block_rows
    col_index = jnp.arange(full_len, dtype=jnp.int32)

    def allowed_rows(first_row):
        row_index = first_row + jnp.arange(block_rows, dtype=jnp.int32)
        causal_ok = col_index[None, :] <= row_index[:, None]
        same_doc = (row_index[:, None] < cut_here) == (col_index[None, :] < cut_here)
        return causal_ok & same_doc

    def flat_all(value_rows):
        return value_rows.reshape(tok_rows, value_rows.shape[-1])

    def own_rows(value_rows):
        return lax.dynamic_slice_in_dim(flat_all(value_rows), half_first, half_rows, 0)

    domain_total = domain_counts.shape[0]
    all_tokens = seq_rows * full_len
    per_domain = domain_weights * (all_tokens / domain_total) / domain_counts.astype(jnp.float32)
    one_hot = (domain_ids[..., None] == jnp.arange(domain_total, dtype=jnp.int32)).astype(
        jnp.float32
    )
    row_scale = jnp.sum(one_hot * per_domain, axis=-1)
    current = tokens.astype(jnp.float32)
    kept = []
    for layer_index in range(LAYERS):
        r_one = rms_scale(current)
        normed_attn = (current * r_one * attn_gain[layer_index]).astype(jnp.bfloat16)
        query_columns = lax.dynamic_slice_in_dim(
            query_weight[layer_index], own_group * group_cols, group_cols, 1
        )
        latent_columns = lax.dynamic_slice_in_dim(
            latent_weight[layer_index], own_group * latent_size, latent_size, 1
        )
        up_layer = latent_up[layer_index]
        key_cols = lax.dynamic_slice_in_dim(up_layer, own_group * group_cols, group_cols, 1)
        val_cols = lax.dynamic_slice_in_dim(
            up_layer, heads_dim + own_group * group_cols, group_cols, 1
        )
        queries = jnp.dot(normed_attn, query_columns, preferred_element_type=jnp.float32).astype(
            jnp.bfloat16
        )
        latents = jnp.dot(normed_attn, latent_columns, preferred_element_type=jnp.float32).astype(
            jnp.bfloat16
        )
        spread_lat = jnp.broadcast_to(
            latents[:, None], (seq_rows, heads_per, loc_len, latent_size)
        ).reshape(seq_rows * heads_per, loc_len, latent_size)
        q_recv, lat_recv = (
            lax.all_to_all(
                to_heads(queries, heads_per), "seq", split_axis=0, concat_axis=1, tiled=True
            ),
            lax.all_to_all(spread_lat, "seq", split_axis=0, concat_axis=1, tiled=True),
        )
        q_seq = q_recv[0]
        head_keys = lax.dynamic_slice_in_dim(up_layer, head_global * HD, HD, 1)
        head_vals = lax.dynamic_slice_in_dim(up_layer, heads_dim + head_global * HD, HD, 1)
        k_seq = jnp.dot(lat_recv[0], head_keys, preferred_element_type=jnp.float32).astype(
            jnp.bfloat16
        )
        v_seq = jnp.dot(lat_recv[0], head_vals, preferred_element_type=jnp.float32).astype(
            jnp.bfloat16
        )

        def forward_block(block_args, k_seq=k_seq, v_seq=v_seq):
            q_block, first_row = block_args
            scores = (
                jnp.einsum("qd,kd->qk", q_block, k_seq, preferred_element_type=jnp.float32)
                * att_scale
            )
            scores = jnp.where(allowed_rows(first_row), scores, NEG_FILL)
            row_max = jnp.max(scores, axis=-1, keepdims=True)
            exp_scores = jnp.exp(scores - row_max)
            row_sum = jnp.sum(exp_scores, axis=-1, keepdims=True)
            probs_low = (exp_scores / row_sum).astype(jnp.bfloat16)
            head_block = jnp.dot(probs_low, v_seq, preferred_element_type=jnp.float32).astype(
                jnp.bfloat16
            )
            return (head_block, (row_max + jnp.log(row_sum))[:, 0])

        q_blocks = q_seq.reshape(block_count, block_rows, HD)
        head_blocks, log_blocks = lax.map(forward_block, (q_blocks, block_firsts))
        head_seq = head_blocks.reshape(full_len, HD)
        back_heads = lax.all_to_all(head_seq[None], "seq", split_axis=1, concat_axis=0, tiled=True)
        own_heads = from_heads(back_heads, heads_per)
        heads_out = lax.all_gather(own_heads, "rep", axis=2, tiled=True)
        attn_branch = (
            jnp.dot(heads_out, out_weight[layer_index], preferred_element_type=jnp.float32)
            + out_bias[layer_index]
        )
        hidden_in = current + attn_branch
        r_two = rms_scale(hidden_in)
        normed_mlp = (hidden_in * r_two * mlp_gain[layer_index]).astype(jnp.bfloat16)
        gate_both = jnp.dot(
            normed_mlp, gate_up_matrix[layer_index], preferred_element_type=jnp.float32
        )
        gate_part = gate_both[..., :hidden_size]
        up_part = gate_both[..., hidden_size:]
        hidden_act = (jax.nn.silu(gate_part) * up_part).astype(jnp.bfloat16)
        next_state = hidden_in + jnp.dot(
            hidden_act, down_matrix[layer_index], preferred_element_type=jnp.float32
        )
        kept.append(
            (
                current,
                r_one,
                normed_attn,
                latents,
                query_columns,
                latent_columns,
                key_cols,
                val_cols,
                q_blocks,
                k_seq,
                v_seq,
                log_blocks,
                heads_out,
                hidden_in,
                r_two,
                normed_mlp,
                gate_part,
                up_part,
                hidden_act,
            )
        )
        current = next_state
    output = current.astype(jnp.bfloat16)
    grad_state = cotangent.astype(jnp.float32) * row_scale[..., None]
    layer_grads = []
    for layer_index in reversed(range(LAYERS)):
        (
            state_in,
            r_one,
            normed_attn,
            latents,
            query_columns,
            latent_columns,
            key_cols,
            val_cols,
            q_blocks,
            k_seq,
            v_seq,
            log_blocks,
            heads_out,
            hidden_in,
            r_two,
            normed_mlp,
            gate_part,
            up_part,
            hidden_act,
        ) = kept[layer_index]
        feedforward_grad = grad_state.astype(jnp.bfloat16)
        g_down = jnp.einsum(
            "tf,td->fd",
            own_rows(hidden_act),
            own_rows(feedforward_grad),
            preferred_element_type=jnp.float32,
        )
        d_hidden = jnp.einsum(
            "kqm,zm->kqz",
            feedforward_grad,
            down_matrix[layer_index],
            preferred_element_type=jnp.float32,
        )
        sig_gate = jax.nn.sigmoid(gate_part)
        d_gate = (d_hidden * up_part * sig_gate * (1.0 + gate_part * (1.0 - sig_gate))).astype(
            jnp.bfloat16
        )
        d_up = (d_hidden * gate_part * sig_gate).astype(jnp.bfloat16)
        gate_up_cotangent = jnp.concatenate([d_gate, d_up], axis=-1)
        g_gate_up = jnp.einsum(
            "td,tf->df",
            own_rows(normed_mlp),
            own_rows(gate_up_cotangent),
            preferred_element_type=jnp.float32,
        )
        d_normed_mlp = jnp.einsum(
            "ouz,tz->out",
            gate_up_cotangent,
            gate_up_matrix[layer_index],
            preferred_element_type=jnp.float32,
        )
        d_norm_two, gain_terms_two = norm_back(
            d_normed_mlp, hidden_in, r_two, mlp_gain[layer_index]
        )
        g_mlp_gain = jnp.sum(own_rows(gain_terms_two), axis=0)
        d_hidden_in = grad_state + d_norm_two
        attention_grad = d_hidden_in.astype(jnp.bfloat16)
        g_out = jnp.einsum(
            "tf,td->fd",
            own_rows(heads_out),
            own_rows(attention_grad),
            preferred_element_type=jnp.float32,
        )
        g_bias = jnp.sum(own_rows(attention_grad).astype(jnp.float32), axis=0)
        output_rows = lax.dynamic_slice_in_dim(
            out_weight[layer_index], own_group * group_cols, group_cols, 0
        )
        d_heads = jnp.einsum(
            "kqm,zm->kqz", attention_grad, output_rows, preferred_element_type=jnp.float32
        ).astype(jnp.bfloat16)
        d_heads_seq = lax.all_to_all(
            to_heads(d_heads, heads_per), "seq", split_axis=0, concat_axis=1, tiled=True
        )[0]
        d_head_blocks = d_heads_seq.reshape(block_count, block_rows, HD)

        def backward_block(carry, block_args, k_seq=k_seq, v_seq=v_seq):
            d_keys_acc, d_vals_acc = carry
            q_block, d_block, log_block, first_row = block_args
            scores = (
                jnp.einsum("qd,kd->qk", q_block, k_seq, preferred_element_type=jnp.float32)
                * att_scale
            )
            scores = jnp.where(allowed_rows(first_row), scores, NEG_FILL)
            probs = jnp.exp(scores - log_block[:, None])
            d_probs = jnp.einsum("qd,kd->qk", d_block, v_seq, preferred_element_type=jnp.float32)
            d_vals_acc = d_vals_acc + jnp.einsum(
                "qk,qd->kd", probs.astype(jnp.bfloat16), d_block, preferred_element_type=jnp.float32
            )
            row_delta = jnp.sum(probs * d_probs, axis=-1, keepdims=True)
            d_scores = (probs * (d_probs - row_delta)).astype(jnp.bfloat16)
            d_query_block = (
                jnp.einsum("qk,kd->qd", d_scores, k_seq, preferred_element_type=jnp.float32)
                * att_scale
            ).astype(jnp.bfloat16)
            d_keys_acc = (
                d_keys_acc
                + jnp.einsum("qk,qd->kd", d_scores, q_block, preferred_element_type=jnp.float32)
                * att_scale
            )
            return ((d_keys_acc, d_vals_acc), d_query_block)

        start_acc = jnp.zeros((full_len, HD), jnp.float32)
        (d_keys_acc, d_vals_acc), d_query_blocks = lax.scan(
            backward_block,
            (start_acc, start_acc),
            (q_blocks, d_head_blocks, log_blocks, block_firsts),
        )
        d_query_seq = d_query_blocks.reshape(full_len, HD)
        dq_recv, dk_recv, dv_recv = (
            lax.all_to_all(d_query_seq[None], "seq", split_axis=1, concat_axis=0, tiled=True),
            lax.all_to_all(
                d_keys_acc.astype(jnp.bfloat16)[None],
                "seq",
                split_axis=1,
                concat_axis=0,
                tiled=True,
            ),
            lax.all_to_all(
                d_vals_acc.astype(jnp.bfloat16)[None],
                "seq",
                split_axis=1,
                concat_axis=0,
                tiled=True,
            ),
        )
        query_cotangent = from_heads(dq_recv, heads_per)
        d_keys = from_heads(dk_recv, heads_per)
        d_vals = from_heads(dv_recv, heads_per)
        latent_cotangent = (
            jnp.einsum("slf,rf->slr", d_keys, key_cols, preferred_element_type=jnp.float32)
            + jnp.einsum("slf,rf->slr", d_vals, val_cols, preferred_element_type=jnp.float32)
        ).astype(jnp.bfloat16)
        flat_lat = flat_all(latents)
        g_up_keys = jnp.einsum(
            "tr,tf->rf", flat_lat, flat_all(d_keys), preferred_element_type=jnp.float32
        )
        g_up_vals = jnp.einsum(
            "tr,tf->rf", flat_lat, flat_all(d_vals), preferred_element_type=jnp.float32
        )
        flat_normed = flat_all(normed_attn)
        g_query_own = jnp.einsum(
            "td,tf->df", flat_normed, flat_all(query_cotangent), preferred_element_type=jnp.float32
        )
        g_latent_own = jnp.einsum(
            "td,tf->df", flat_normed, flat_all(latent_cotangent), preferred_element_type=jnp.float32
        )
        partial_part = jnp.einsum(
            "ouz,tz->out", query_cotangent, query_columns, preferred_element_type=jnp.float32
        ) + jnp.einsum(
            "zxm,om->zxo", latent_cotangent, latent_columns, preferred_element_type=jnp.float32
        )
        d_normed_attn = lax.psum(partial_part.astype(jnp.bfloat16), "rep").astype(jnp.float32)
        d_norm_one, gain_terms_one = norm_back(
            d_normed_attn, state_in, r_one, attn_gain[layer_index]
        )
        g_attn_gain = jnp.sum(own_rows(gain_terms_one), axis=0)
        grad_state = d_hidden_in + d_norm_one
        up_mask = jnp.arange(2 * heads_dim) % heads_dim // group_cols == own_group
        g_up_full = jnp.where(
            up_mask, jnp.concatenate([g_up_keys] * rep_count + [g_up_vals] * rep_count, axis=1), 0.0
        )
        query_mask = jnp.arange(heads_dim) // group_cols == own_group
        latent_mask = jnp.arange(rep_count * latent_size) // latent_size == own_group
        g_query_full = jnp.where(
            query_mask, jnp.concatenate([g_query_own] * rep_count, axis=1), 0.0
        )
        g_latent_full = jnp.where(
            latent_mask, jnp.concatenate([g_latent_own] * rep_count, axis=1), 0.0
        )
        all_sums = (
            lax.psum_scatter(g_attn_gain, ("seq", "rep"), scatter_dimension=0, tiled=True),
            lax.psum_scatter(g_query_full, ("seq", "rep"), scatter_dimension=0, tiled=True),
            lax.psum_scatter(g_latent_full, ("seq", "rep"), scatter_dimension=0, tiled=True),
            lax.psum_scatter(g_up_full, ("seq", "rep"), scatter_dimension=1, tiled=True),
            lax.psum_scatter(g_out, ("seq", "rep"), scatter_dimension=1, tiled=True),
            lax.psum_scatter(g_bias, ("seq", "rep"), scatter_dimension=0, tiled=True),
            lax.psum_scatter(g_mlp_gain, ("seq", "rep"), scatter_dimension=0, tiled=True),
            lax.psum_scatter(g_gate_up, ("seq", "rep"), scatter_dimension=0, tiled=True),
            lax.psum_scatter(g_down, ("seq", "rep"), scatter_dimension=1, tiled=True),
        )
        layer_grads.insert(0, all_sums)
    stacked = [jnp.stack([grads_one[member] for grads_one in layer_grads]) for member in range(9)]
    return (
        output,
        grad_state.astype(jnp.bfloat16),
        stacked[0],
        stacked[1],
        stacked[2],
        stacked[3],
        stacked[4],
        stacked[5],
        stacked[6],
        stacked[7],
        stacked[8],
    )


def solution(mesh):
    return jax.shard_map(
        shards,
        mesh=mesh,
        in_specs=(
            P(None, "seq", None),
            P(None, "seq", None),
            P(None, "seq"),
            P(),
            P(),
            P(),
            P(),
            P(),
            P(),
            P(),
            P(),
            P(),
            P(),
            P(),
            P(),
        ),
        out_specs=(
            P(None, "seq", None),
            P(None, "seq", None),
            P(None, ("seq", "rep")),
            P(None, ("seq", "rep"), None),
            P(None, ("seq", "rep"), None),
            P(None, None, ("seq", "rep")),
            P(None, None, ("seq", "rep")),
            P(None, ("seq", "rep")),
            P(None, ("seq", "rep")),
            P(None, ("seq", "rep"), None),
            P(None, None, ("seq", "rep")),
        ),
        check_vma=False,
    )
```

profile of v0, /device:TPU:0, one launch (start us, length us, event | category | flops | bytes accessed | tf_op | source)
XLA Modules:
  0.0 4150.9 jit_solution(12987386908798726496)
XLA Ops:
  51.6 35.0 all-to-all-done.1
  93.8 82.5 %while.60 = (s32[]{:T(128)}, bf16[8,512,64]{1,2,0:T(8,128)(2,1)S(1)}, f32[8,512]{1,0:T(8,128)S(1)}, s32[8]{0:T(128)S(1)}, s32[]{:T(128)}, /*index=5*/bf16[8,512,...) while((s32[]{:T(128)}, ...), condition=%wide.region_4.5_spmd.clone.clone, body=%wide.region_1.4_spmd.clone.clone.sunk | while | flops 559977472 | bytes 26969236 | solution.py:162
  208.3 25.9 all_to_all.56
  314.6 39.7 all-to-all-done.4
  362.4 83.0 %while.61 = (s32[]{:T(128)}, bf16[8,512,64]{1,2,0:T(8,128)(2,1)S(1)}, f32[8,512]{1,0:T(8,128)S(1)}, s32[8]{0:T(128)S(1)}, s32[]{:T(128)}, /*index=5*/bf16[8,512,...) while((s32[]{:T(128)}, ...), condition=%wide.region_10.11_spmd.clone.clone, body=%wide.region_7.10_spmd.clone.clone.sunk | while | flops 559977472 | bytes 26969236 | solution.py:162
  476.2 25.9 all_to_all.57
  606.7 261.5 %while.62 = (s32[]{:T(128)}, f32[4096,64]{0,1:T(8,128)S(1)}, f32[4096,64]{0,1:T(8,128)S(1)}, bf16[8,512,64]{1,2,0:T(8,128)(2,1)}, s32[8]{0:T(128)S(1)}, /*index=...) while((s32[]{:T(128)}, f32[4096,64]{0,1:T(8,128)S(1)}, ...), condition=%wide.region_16.17_spmd.clone.clone, body=%wide.region_14.16_spmd.clone.clone.sunk | while | flops 1368724480 | bytes 120151296 | solution.py:314
  872.9 23.7 reduce.2
  1004.8 40.6 all-reduce.10.cloned.1.call-done
  1105.5 268.7 %while.63 = (s32[]{:T(128)}, f32[4096,64]{0,1:T(8,128)S(1)}, f32[4096,64]{0,1:T(8,128)S(1)}, bf16[8,512,64]{1,2,0:T(8,128)(2,1)}, s32[8]{0:T(128)S(1)}, /*index=...) while((s32[]{:T(128)}, f32[4096,64]{0,1:T(8,128)S(1)}, ...), condition=%wide.region_22.23_spmd.clone.clone, body=%wide.region_20.22_spmd.clone.clone.sunk | while | flops 1368724480 | bytes 120151296 | solution.py:314
  1378.8 23.6 reduce.5
  1620.1 40.7 all-reduce.6
  1665.8 25.5 reduce-scatter.43.cloned.1.call-done
  1692.4 134.4 %reduce-scatter.41.cloned.1.call-done = f32[32,512]{1,0:T(8,128)} async-done(((f32[1024,512]{1,0:T(8,128)}), f32[32,512]{1,0:T(8,128)}) %reduce-scatter.41.cloned.1.call-update) | async-done | bytes 65552
  1827.9 134.6 %reduce-scatter.47.cloned.1.call-done = f32[64,256]{1,0:T(8,128)} async-done(((f32[2048,256]{1,0:T(8,128)}), f32[64,256]{1,0:T(8,128)}) %reduce-scatter.47.cloned.1.call-update) | async-done | bytes 65552
  1963.4 134.8 %reduce-scatter.45.cloned.1.call-done = f32[64,256]{1,0:T(8,128)} async-done(((f32[2048,256]{1,0:T(8,128)}), f32[64,256]{1,0:T(8,128)}) %reduce-scatter.45.cloned.1.call-update) | async-done | bytes 65552
  2100.6 138.0 %reduce-scatter.27.cloned.1.call-done = f32[1024,32]{0,1:T(8,128)} async-done(((f32[1024,1024]{0,1:T(8,128)}), f32[1024,32]{0,1:T(8,128)}) %reduce-scatter.27.cloned.1.call-update) | async-done | bytes 131088 | tf_op jit(solution)/shard_map/reduce_scatter | solution.py:386
  2238.6 140.7 %reduce-scatter.25.cloned.1.call-done = f32[1024,32]{0,1:T(8,128)} async-done(((f32[1024,1024]{0,1:T(8,128)}), f32[1024,32]{0,1:T(8,128)}) %reduce-scatter.25.cloned.1.call-update) | async-done | bytes 131088 | tf_op jit(solution)/shard_map/reduce_scatter | solution.py:386
  2381.0 139.2 %reduce-scatter.39.cloned.1.call-done = f32[32,1024]{1,0:T(8,128)} async-done(((f32[1024,1024]{1,0:T(8,128)}), f32[32,1024]{1,0:T(8,128)}) %reduce-scatter.39.cloned.1.call-update) | async-done | bytes 131088
  2521.5 139.1 %reduce-scatter.37.cloned.1.call-done = f32[32,1024]{1,0:T(8,128)} async-done(((f32[1024,1024]{1,0:T(8,128)}), f32[32,1024]{1,0:T(8,128)}) %reduce-scatter.37.cloned.1.call-update) | async-done | bytes 131088
  2662.6 245.7 %reduce-scatter.35.cloned.1.call-done = f32[2816,32]{0,1:T(8,128)} async-done(((f32[2816,1024]{0,1:T(8,128)}), f32[2816,32]{0,1:T(8,128)}) %reduce-scatter.35.cloned.1.call-update) | async-done | bytes 360464 | tf_op jit(solution)/shard_map/reduce_scatter | solution.py:390
  2908.3 251.4 %reduce-scatter.33.cloned.1.call-done = f32[2816,32]{0,1:T(8,128)} async-done(((f32[2816,1024]{0,1:T(8,128)}), f32[2816,32]{0,1:T(8,128)}) %reduce-scatter.33.cloned.1.call-update) | async-done | bytes 360464 | tf_op jit(solution)/shard_map/reduce_scatter | solution.py:390
  3161.7 489.0 %reduce-scatter.31.cloned.1.call-done = f32[32,5632]{1,0:T(8,128)} async-done(((f32[1024,5632]{1,0:T(8,128)}), f32[32,5632]{1,0:T(8,128)}) %reduce-scatter.31.cloned.1.call-update) | async-done | bytes 720912 | tf_op jit(solution)/shard_map/reduce_scatter | solution.py:389
  3650.7 490.9 %reduce-scatter.29.cloned.1.call-done = f32[32,5632]{1,0:T(8,128)} async-done(((f32[1024,5632]{1,0:T(8,128)}), f32[32,5632]{1,0:T(8,128)}) %reduce-scatter.29.cloned.1.call-update) | async-done | bytes 720912 | tf_op jit(solution)/shard_map/reduce_scatter | solution.py:389
  (866 shorter events, 1413.5 us)
Async XLA Ops:
  41.4 45.2 %all-to-all-start.1 = ((bf16[16,256,256]{2,1,0:T(8,128)(2,1)}), bf16[16,256,256]{2,1,0:T(8,128)(2,1)S(1)}, u32[]{:S(2)}, u32[]{:S(2)}) async-start(bf16[16,256,256]{2,1,0:T(8,128)(2,1)} %bitcast.539), calls=%async_computation.1 | async-start | bytes 4194304 | tf_op jit(solution)/shard_map/all_to_all | solution.py:133
  45.5 216.7 %all-gather.3.cloned.1.call-start = ((), (), s32[]{:S(2)}) async-start(), calls=%async_computation.26 | async-start | bytes 1572864 | tf_op jit(solution)/shard_map/all_gather | solution.py:166
  309.1 45.2 %all-to-all-start.4 = ((bf16[16,256,256]{2,1,0:T(8,128)(2,1)}), bf16[16,256,256]{2,1,0:T(8,128)(2,1)S(1)}, u32[]{:S(2)}, u32[]{:S(2)}) async-start(bf16[16,256,256]{2,1,0:T(8,128)(2,1)} %bitcast.540), calls=%async_computation.4 | async-start | bytes 4194304 | tf_op jit(solution)/shard_map/all_to_all | solution.py:133
  313.2 219.1 %all-gather.5.cloned.1.call-start = ((), (), s32[]{:S(2)}) async-start(), calls=%async_computation.27 | async-start | bytes 1572864 | tf_op jit(solution)/shard_map/all_gather | solution.py:166
  898.1 36.9 all-to-all-start.7
  935.0 33.1 all-to-all-start.8
  968.1 26.4 all-to-all-start.9
  974.2 71.2 %all-reduce.10.cloned.1.call-start = ((), (), s32[]{:S(2)}) async-start(), calls=%async_computation.28 | async-start | bytes 2097152 | tf_op jit(solution)/shard_map/psum | solution.py:363
  1404.0 31.9 all-to-all-start.11
  1435.8 35.2 all-to-all-start.12
  1471.1 27.8 all-to-all-start.13
  1477.2 139.9 %all-reduce.12.cloned.1.call-start = ((), (), s32[]{:S(2)}) async-start(), calls=%async_computation.29 | async-start | bytes 2097152 | tf_op jit(solution)/shard_map/psum | solution.py:363
  1511.6 179.6 %reduce-scatter.43.cloned.1.call-start = ((), (), s32[]{:S(2)}) async-start(), calls=%async_computation.39 | async-start | bytes 2162688
  1518.0 308.8 %reduce-scatter.41.cloned.1.call-start = ((), (), s32[]{:S(2)}) async-start(), calls=%async_computation.38 | async-start | bytes 2162688
  1521.2 441.2 %reduce-scatter.47.cloned.1.call-start = ((), (), s32[]{:S(2)}) async-start(), calls=%async_computation.41 | async-start | bytes 2162688
  1530.2 568.0 %reduce-scatter.45.cloned.1.call-start = ((), (), s32[]{:S(2)}) async-start(), calls=%async_computation.40 | async-start | bytes 2162688
  1533.3 705.3 %reduce-scatter.27.cloned.1.call-start = ((), (), s32[]{:S(2)}) async-start(), calls=%async_computation.31 | async-start | bytes 4325376 | tf_op jit(solution)/shard_map/reduce_scatter | solution.py:386
  1537.2 842.1 %reduce-scatter.25.cloned.1.call-start = ((), (), s32[]{:S(2)}) async-start(), calls=%async_computation.30 | async-start | bytes 4325376 | tf_op jit(solution)/shard_map/reduce_scatter | solution.py:386
  1542.3 977.9 %reduce-scatter.39.cloned.1.call-start = ((), (), s32[]{:S(2)}) async-start(), calls=%async_computation.37 | async-start | bytes 4325376
  1556.3 1104.3 %reduce-scatter.37.cloned.1.call-start = ((), (), s32[]{:S(2)}) async-start(), calls=%async_computation.36 | async-start | bytes 4325376
  1561.7 1346.6 %reduce-scatter.35.cloned.1.call-start = ((), (), s32[]{:S(2)}) async-start(), calls=%async_computation.35 | async-start | bytes 11894784 | tf_op jit(solution)/shard_map/reduce_scatter | solution.py:390
  1570.2 1589.5 %reduce-scatter.33.cloned.1.call-start = ((), (), s32[]{:S(2)}) async-start(), calls=%async_computation.34 | async-start | bytes 11894784 | tf_op jit(solution)/shard_map/reduce_scatter | solution.py:390
  1579.0 2071.7 %reduce-scatter.31.cloned.1.call-start = ((), (), s32[]{:S(2)}) async-start(), calls=%async_computation.33 | async-start | bytes 23789568 | tf_op jit(solution)/shard_map/reduce_scatter | solution.py:389
  1592.7 2548.9 %reduce-scatter.29.cloned.1.call-start = ((), (), s32[]{:S(2)}) async-start(), calls=%async_computation.32 | async-start | bytes 23789568 | tf_op jit(solution)/shard_map/reduce_scatter | solution.py:389
  (138 other events, 1458.8 us)
Sparse Core Ops, SparseCore 0:
  241.5 20.7 all-gather.2
  512.5 19.7 all-gather.4
  1004.9 40.4 all-reduce.9
  1511.8 40.3 all-reduce.11
  1554.3 136.9 reduce-scatter.42
  1693.5 133.2 reduce-scatter.40
  1829.1 133.3 reduce-scatter.46
  1964.8 133.3 reduce-scatter.44
  2100.5 138.1 reduce-scatter.26
  2240.7 138.5 reduce-scatter.24
  2381.6 138.5 reduce-scatter.38
  2522.3 138.2 reduce-scatter.36
  2662.9 245.3 reduce-scatter.34
  2910.5 249.1 reduce-scatter.32
  3161.8 488.7 reduce-scatter.30
  3652.8 488.6 reduce-scatter.28
where the time goes:
time: 4160 us; the launch traced here: 4150 us
  waiting for transfers between devices  2670 us (64%)
  matrix products  557 us (13%)
  other arithmetic  499 us (12%)
  local copies, waits for them, and re-layouts  248 us (6%)
  blocking collectives  92.5 us (2%)
  starting transfers between devices  67.5 us (2%)
    reduce_scatter x2, waiting for transfers between devices, shards(): lax.psum_scatter(g_gate_up, ('seq', 'rep'), scatter_dimension=0, tiled=True)  980 us
    unnamed x22, waiting for transfers between devices  708 us
    reduce_scatter x2, waiting for transfers between devices, shards(): lax.psum_scatter(g_down, ('seq', 'rep'), scatter_dimension=1, tiled=True)  497 us
    reduce_scatter x2, waiting for transfers between devices, shards(): lax.psum_scatter(g_out, ('seq', 'rep'), scatter_dimension=1, tiled=True)  279 us
    unnamed x14, other arithmetic  185 us
    convert_element_type x16, other arithmetic, backward_block(): d_scores = (probs * (d_probs - row_delta)).astype(jnp.bfloat16)  159 us
    unnamed x256, local copies, waits for them, and re-layouts  120 us
    dot_general x16, matrix products, backward_block(): jnp.einsum('qd,kd->qk', q_block, k_seq, preferred_element_type=jnp.float32)  106 us
  transfers between devices with their start and end apart: 28, of which 21 were waited for; matrix products, arithmetic and copies ran while one was open for 7% of the time, Pallas kernels for 0%

commit v1 on v0

--- a/solution.py
+++ b/solution.py
@@ -91,6 +91,38 @@
     def flat_all(value_rows):
         return value_rows.reshape(tok_rows, value_rows.shape[-1])
 
+    def own_blocks(value_rows):
+        flat = flat_all(value_rows)
+        cols = flat.shape[1]
+        kept_cols = cols // rep_count
+        block = cols // (seq_count * rep_count)
+        kept_at = jnp.arange(kept_cols, dtype=jnp.int32)
+        source = (kept_at // block * rep_count + own_group) * block + kept_at % block
+        pick = (jnp.arange(cols, dtype=jnp.int32)[:, None] == source[None, :]).astype(flat.dtype)
+        return jnp.dot(flat, pick, preferred_element_type=jnp.float32).astype(flat.dtype)
+
+    def seq_sum(value_rows):
+        return lax.psum_scatter(
+            value_rows.astype(jnp.bfloat16), "seq", scatter_dimension=0, tiled=True
+        ).astype(jnp.float32)
+
+    def own_half(value_rows):
+        both = lax.all_gather(value_rows, "rep", axis=1, tiled=True)
+        rows = both.shape[0] // rep_count
+        return lax.dynamic_slice_in_dim(both, own_group * rows, rows, 0)
+
+    device_count = seq_count * rep_count
+    up_moves = []
+    for seq_at in range(seq_count):
+        for rep_at in range(rep_count):
+            side, inner = divmod(seq_at, seq_count // 2)
+            up_moves.append(
+                (
+                    seq_at * rep_count + rep_at,
+                    side * (device_count // 2) + rep_at * (seq_count // 2) + inner,
+                )
+            )
+
     def own_rows(value_rows):
         return lax.dynamic_slice_in_dim(flat_all(value_rows), half_first, half_rows, 0)
 
@@ -231,9 +263,9 @@
         ) = kept[layer_index]
         feedforward_grad = grad_state.astype(jnp.bfloat16)
         g_down = jnp.einsum(
-            "tf,td->fd",
-            own_rows(hidden_act),
-            own_rows(feedforward_grad),
+            "td,tf->df",
+            own_blocks(feedforward_grad),
+            flat_all(hidden_act),
             preferred_element_type=jnp.float32,
         )
         d_hidden = jnp.einsum(
@@ -250,8 +282,8 @@
         gate_up_cotangent = jnp.concatenate([d_gate, d_up], axis=-1)
         g_gate_up = jnp.einsum(
             "td,tf->df",
-            own_rows(normed_mlp),
-            own_rows(gate_up_cotangent),
+            own_blocks(normed_mlp),
+            flat_all(gate_up_cotangent),
             preferred_element_type=jnp.float32,
         )
         d_normed_mlp = jnp.einsum(
@@ -267,9 +299,9 @@
         d_hidden_in = grad_state + d_norm_two
         attention_grad = d_hidden_in.astype(jnp.bfloat16)
         g_out = jnp.einsum(
-            "tf,td->fd",
-            own_rows(heads_out),
-            own_rows(attention_grad),
+            "td,tf->df",
+            own_blocks(attention_grad),
+            flat_all(heads_out),
             preferred_element_type=jnp.float32,
         )
         g_bias = jnp.sum(own_rows(attention_grad).astype(jnp.float32), axis=0)
@@ -366,28 +398,17 @@
         )
         g_attn_gain = jnp.sum(own_rows(gain_terms_one), axis=0)
         grad_state = d_hidden_in + d_norm_one
-        up_mask = jnp.arange(2 * heads_dim) % heads_dim // group_cols == own_group
-        g_up_full = jnp.where(
-            up_mask, jnp.concatenate([g_up_keys] * rep_count + [g_up_vals] * rep_count, axis=1), 0.0
-        )
-        query_mask = jnp.arange(heads_dim) // group_cols == own_group
-        latent_mask = jnp.arange(rep_count * latent_size) // latent_size == own_group
-        g_query_full = jnp.where(
-            query_mask, jnp.concatenate([g_query_own] * rep_count, axis=1), 0.0
-        )
-        g_latent_full = jnp.where(
-            latent_mask, jnp.concatenate([g_latent_own] * rep_count, axis=1), 0.0
-        )
+        g_up_own = jnp.concatenate([g_up_keys, g_up_vals], axis=1).T
         all_sums = (
             lax.psum_scatter(g_attn_gain, ("seq", "rep"), scatter_dimension=0, tiled=True),
-            lax.psum_scatter(g_query_full, ("seq", "rep"), scatter_dimension=0, tiled=True),
-            lax.psum_scatter(g_latent_full, ("seq", "rep"), scatter_dimension=0, tiled=True),
-            lax.psum_scatter(g_up_full, ("seq", "rep"), scatter_dimension=1, tiled=True),
-            lax.psum_scatter(g_out, ("seq", "rep"), scatter_dimension=1, tiled=True),
+            own_half(seq_sum(g_query_own)),
+            own_half(seq_sum(g_latent_own)),
+            lax.ppermute(seq_sum(g_up_own), ("seq", "rep"), up_moves).T,
+            seq_sum(g_out).T,
             lax.psum_scatter(g_bias, ("seq", "rep"), scatter_dimension=0, tiled=True),
             lax.psum_scatter(g_mlp_gain, ("seq", "rep"), scatter_dimension=0, tiled=True),
-            lax.psum_scatter(g_gate_up, ("seq", "rep"), scatter_dimension=0, tiled=True),
-            lax.psum_scatter(g_down, ("seq", "rep"), scatter_dimension=1, tiled=True),
+            seq_sum(g_gate_up),
+            seq_sum(g_down).T,
         )
         layer_grads.insert(0, all_sums)
     stacked = [jnp.stack([grads_one[member] for grads_one in layer_grads]) for member in range(9)]

time: 4160 us -> 2010 us (0.48)
  waiting for transfers between devices: 2670 us -> 571 us
    reduce_scatter x6 -> x10, waiting for transfers between devices: 1760 us -> 345 us  [seq_sum(): lax.psum_scatter(value_rows.astype(jnp.bfloat16), 'seq', scatter_dimensio...]
    unnamed x22 -> x18, waiting for transfers between devices: 708 us -> 0.26 us
    unnamed x256 -> x210, local copies, waits for them, and re-layouts: 120 us -> 86.8 us
  transfers between devices with their start and end apart: 28 -> 30, of which waited for: 21 -> 17; matrix products, arithmetic and copies ran while one was open for 7% -> 29% of each run, Pallas kernels for 0% -> 0%
where the time goes in v1:
time: 2010 us; the launch traced here: 2000 us
  waiting for transfers between devices  571 us (28%)
  matrix products  542 us (27%)
  other arithmetic  467 us (23%)
  local copies, waits for them, and re-layouts  217 us (11%)
  blocking collectives  115 us (6%)
  starting transfers between devices  69.5 us (3%)
    reduce_scatter x10, waiting for transfers between devices, seq_sum(): lax.psum_scatter(value_rows.astype(jnp.bfloat16), 'seq', scatter_dimensio...  345 us
    unnamed x14, other arithmetic  186 us
    convert_element_type x16, other arithmetic, backward_block(): d_scores = (probs * (d_probs - row_delta)).astype(jnp.bfloat16)  128 us
    dot_general x16, matrix products, backward_block(): jnp.einsum('qd,kd->qk', q_block, k_seq, preferred_element_type=jnp.float32)  107 us
    unnamed x210, local copies, waits for them, and re-layouts  86.8 us
    all_to_all x2, waiting for transfers between devices, shards(): lax.all_to_all(spread_lat, 'seq', split_axis=0, concat_axis=1, tiled=True)  74.5 us
    dot_general x16, matrix products, backward_block(): jnp.einsum('qk,qd->kd', probs.astype(jnp.bfloat16), d_block, preferred_el...  72.4 us
    psum x2, waiting for transfers between devices, shards(): lax.psum(partial_part.astype(jnp.bfloat16), 'rep').astype(jnp.float32)  66 us
  transfers between devices with their start and end apart: 30, of which 17 were waited for; matrix products, arithmetic and copies ran while one was open for 29% of the time, Pallas kernels for 0%

profile of v1, /device:TPU:0, one launch (start us, length us, event | category | flops | bytes accessed | tf_op | source)
XLA Modules:
  0.0 2000.4 jit_solution(13412024002865571701)
XLA Ops:
  52.5 34.9 %all-to-all-done.1 = bf16[16,256,256]{2,1,0:T(8,128)(2,1)S(1)} async-done(((bf16[16,256,256]{2,1,0:T(8,128)(2,1)}), bf16[16,256,256]{2,1,0:T(8,128)(2,1)S(1)}, u32[]{:S(2)}, u32[]{:S(2)}) %all-to-all-start.1) | async-done | bytes 2097184 | tf_op jit(solution)/shard_map/all_to_all | solution.py:165
  96.3 87.0 %while.60 = (s32[]{:T(128)}, bf16[8,512,64]{1,2,0:T(8,128)(2,1)}, f32[8,512]{1,0:T(8,128)S(1)}, s32[8]{0:T(128)S(1)}, s32[]{:T(128)}, /*index=5*/bf16[8,512,64]{...) while((s32[]{:T(128)}, bf16[8,512,64]{1,2,0:T(8,128)(2,1)}, ...), condition=%wide.region_4.5_spmd.clone.clone, body=%wide.region_1.4_spmd.clone.clone.sunk | while | flops 559977472 | bytes 26444948 | solution.py:194
  193.5 24.4 %reduce = bf16[4096,64]{1,0:T(8,128)(2,1)} reduce(bf16[4096,1,64]{2,1,0:T(2,128)(2,1)} %bitcast.565, bf16[]{:T(256)} %broadcast.349), dimensions={1}, to_apply=%bitcast.369.reduce_sub_computation | reduce | bytes 1048578
  221.0 26.0 %all_to_all.56 = bf16[16,2,8192]{2,1,0:T(2,128)(2,1)} all-to-all(bf16[16,2,8192]{2,1,0:T(2,128)(2,1)} %reshape.493), channel_id=1, replica_groups=mesh['seq'=16,'rep'=2] {'seq'}, dimensions={0} | all-to-all | bytes 1048576 | tf_op jit(solution)/shard_map/all_to_all | solution.py:196
  330.6 39.5 %all-to-all-done.4 = bf16[16,256,256]{2,1,0:T(8,128)(2,1)S(1)} async-done(((bf16[16,256,256]{2,1,0:T(8,128)(2,1)}), bf16[16,256,256]{2,1,0:T(8,128)(2,1)S(1)}, u32[]{:S(2)}, u32[]{:S(2)}) %all-to-all-start.4) | async-done | bytes 2097184 | tf_op jit(solution)/shard_map/all_to_all | solution.py:165
  378.9 78.3 %while.61 = (s32[]{:T(128)}, bf16[8,512,64]{1,2,0:T(8,128)(2,1)}, f32[8,512]{1,0:T(8,128)S(1)}, s32[8]{0:T(128)S(1)}, s32[]{:T(128)}, /*index=5*/bf16[8,512,64]{...) while((s32[]{:T(128)}, bf16[8,512,64]{1,2,0:T(8,128)(2,1)}, ...), condition=%wide.region_10.11_spmd.clone.clone, body=%wide.region_7.10_spmd.clone.clone.sunk | while | flops 559977472 | bytes 26969236 | solution.py:194
  463.2 23.4 %reduce.1 = bf16[4096,64]{1,0:T(8,128)(2,1)S(1)} reduce(bf16[4096,1,64]{2,1,0:T(2,128)(2,1)} %bitcast.567, bf16[]{:T(256)} %broadcast.349), dimensions={1}, to_apply=%bitcast.371.reduce_sub_computation | reduce | bytes 1048578
  488.2 25.8 %all_to_all.57 = bf16[16,2,8192]{2,1,0:T(2,128)(2,1)S(1)} all-to-all(bf16[16,2,8192]{2,1,0:T(2,128)(2,1)} %reshape.495), channel_id=1, replica_groups=mesh['seq'=16,'rep'=2] {'seq'}, dimensions={0} | all-to-all | bytes 1048576 | tf_op jit(solution)/shard_map/all_to_all | solution.py:196
  614.0 232.1 %while.62 = (s32[]{:T(128)}, f32[4096,64]{0,1:T(8,128)S(1)}, f32[4096,64]{0,1:T(8,128)S(1)}, bf16[8,512,64]{1,2,0:T(8,128)(2,1)}, s32[8]{0:T(128)S(1)}, /*index=...) while((s32[]{:T(128)}, f32[4096,64]{0,1:T(8,128)S(1)}, ...), condition=%wide.region_16.17_spmd.clone.clone, body=%wide.region_14.16_spmd.clone.clone.sunk | while | flops 1368724480 | bytes 107568416 | solution.py:346
  855.4 24.7 %reduce.2 = bf16[4096,64]{1,0:T(8,128)(2,1)} reduce(bf16[4096,1,64]{2,1,0:T(2,128)(2,1)} %bitcast.568, bf16[]{:T(256)} %broadcast.349), dimensions={1}, to_apply=%bitcast.373.reduce_sub_computation | reduce | bytes 1048578
  891.7 23.4 %reduce.4 = bf16[4096,64]{1,0:T(8,128)(2,1)S(1)} reduce(bf16[4096,1,64]{2,1,0:T(2,128)(2,1)} %bitcast.559, bf16[]{:T(256)} %broadcast.349), dimensions={1}, to_apply=%bitcast.377.reduce_sub_computation | reduce | bytes 1048578
  928.8 22.4 %reduce.3 = bf16[4096,64]{1,0:T(8,128)(2,1)S(1)} reduce(bf16[4096,1,64]{2,1,0:T(2,128)(2,1)S(1)} %bitcast.560, bf16[]{:T(256)} %broadcast.349), dimensions={1}, to_apply=%bitcast.375.reduce_sub_computation | reduce | bytes 1048578
  1002.7 31.2 %all-reduce.10.cloned.1.call-done = bf16[2,256,1024]{2,1,0:T(8,128)(2,1)} async-done(((bf16[2,256,1024]{2,1,0:T(8,128)(2,1)}), bf16[2,256,1024]{2,1,0:T(8,128)(2,1)}) %all-reduce.10.cloned.1.call-update) | async-done | bytes 1048592 | tf_op jit(solution)/shard_map/psum | solution.py:395
  1093.4 239.2 %while.63 = (s32[]{:T(128)}, f32[4096,64]{0,1:T(8,128)S(1)}, f32[4096,64]{0,1:T(8,128)S(1)}, bf16[8,512,64]{1,2,0:T(8,128)(2,1)}, s32[8]{0:T(128)S(1)}, /*index=...) while((s32[]{:T(128)}, f32[4096,64]{0,1:T(8,128)S(1)}, ...), condition=%wide.region_22.23_spmd.clone.clone, body=%wide.region_20.22_spmd.clone.clone.sunk | while | flops 1368724480 | bytes 107568416 | solution.py:346
  1338.6 22.6 %reduce.7 = bf16[4096,64]{1,0:T(8,128)(2,1)S(1)} reduce(bf16[4096,1,64]{2,1,0:T(2,128)(2,1)S(1)} %bitcast.561, bf16[]{:T(256)} %broadcast.349), dimensions={1}, to_apply=%bitcast.383.reduce_sub_computation | reduce | bytes 1048578
  1372.2 22.4 %reduce.6 = bf16[4096,64]{1,0:T(8,128)(2,1)S(1)} reduce(bf16[4096,1,64]{2,1,0:T(2,128)(2,1)S(1)} %bitcast.562, bf16[]{:T(256)} %broadcast.349), dimensions={1}, to_apply=%bitcast.381.reduce_sub_computation | reduce | bytes 1048578
  1407.8 22.4 %reduce.5 = bf16[4096,64]{1,0:T(8,128)(2,1)S(1)} reduce(bf16[4096,1,64]{2,1,0:T(2,128)(2,1)S(1)} %bitcast.566, bf16[]{:T(256)} %broadcast.349), dimensions={1}, to_apply=%bitcast.379.reduce_sub_computation | reduce | bytes 1048578
  1548.1 34.4 %reduce-scatter.21.cloned.1.call-done = bf16[64,256]{1,0:T(8,128)(2,1)} async-done(((bf16[1024,256]{1,0:T(8,128)(2,1)}), bf16[64,256]{1,0:T(8,128)(2,1)}) %reduce-scatter.21.cloned.1.call-update) | async-done | bytes 32784 | tf_op jit(solution)/shard_map/reduce_scatter | solution.py:105
  1589.7 34.8 %all-reduce.12.cloned.1.call-done = bf16[2,256,1024]{2,1,0:T(8,128)(2,1)} async-done(((bf16[2,256,1024]{2,1,0:T(8,128)(2,1)}), bf16[2,256,1024]{2,1,0:T(8,128)(2,1)}) %all-reduce.12.cloned.1.call-update) | async-done | bytes 1048592 | tf_op jit(solution)/shard_map/psum | solution.py:395
  1626.5 39.8 %all-reduce.6 = (f32[1024]{0:T(1024)S(1)}, f32[1024]{0:T(1024)S(1)}, f32[1024]{0:T(1024)S(1)}, f32[1024]{0:T(1024)S(1)}, f32[1024]{0:T(1024)S(1)}, /*index=5*/f32[1024]{0:T(1024)S(1)}) all-reduce(f32[1024]{0:T(1024)S(1)} %copy-done.76, ...), channel_id=3, replica_groups=mesh['seq'=16,'rep'=2] {'seq','rep'}, use_global_device_ids=true, to_apply=%region_28.29.clone | all-reduce | flops 6144 | bytes 49152
  1693.7 60.7 %reduce-scatter.35.cloned.1.call-done = bf16[32,2816]{1,0:T(8,128)(2,1)} async-done(((bf16[512,2816]{1,0:T(8,128)(2,1)}), bf16[32,2816]{1,0:T(8,128)(2,1)}) %reduce-scatter.35.cloned.1.call-update) | async-done | bytes 180240 | tf_op jit(solution)/shard_map/reduce_scatter | solution.py:105
  1754.4 68.2 %reduce-scatter.33.cloned.1.call-done = bf16[32,2816]{1,0:T(8,128)(2,1)} async-done(((bf16[512,2816]{1,0:T(8,128)(2,1)}), bf16[32,2816]{1,0:T(8,128)(2,1)}) %reduce-scatter.33.cloned.1.call-update) | async-done | bytes 180240 | tf_op jit(solution)/shard_map/reduce_scatter | solution.py:105
  1824.6 82.3 %reduce-scatter.31.cloned.1.call-done = bf16[32,5632]{1,0:T(8,128)(2,1)} async-done(((bf16[512,5632]{1,0:T(8,128)(2,1)}), bf16[32,5632]{1,0:T(8,128)(2,1)}) %reduce-scatter.31.cloned.1.call-update) | async-done | bytes 360464 | tf_op jit(solution)/shard_map/reduce_scatter | solution.py:105
  1906.9 84.5 %reduce-scatter.29.cloned.1.call-done = bf16[32,5632]{1,0:T(8,128)(2,1)} async-done(((bf16[512,5632]{1,0:T(8,128)(2,1)}), bf16[32,5632]{1,0:T(8,128)(2,1)}) %reduce-scatter.29.cloned.1.call-update) | async-done | bytes 360464 | tf_op jit(solution)/shard_map/reduce_scatter | solution.py:105
  (863 shorter events, 1233.2 us)
Async XLA Ops:
  42.2 45.2 %all-to-all-start.1 = ((bf16[16,256,256]{2,1,0:T(8,128)(2,1)}), bf16[16,256,256]{2,1,0:T(8,128)(2,1)S(1)}, u32[]{:S(2)}, u32[]{:S(2)}) async-start(bf16[16,256,256]{2,1,0:T(8,128)(2,1)} %bitcast.563), calls=%async_computation.1 | async-start | bytes 4194304 | tf_op jit(solution)/shard_map/all_to_all | solution.py:165
  46.4 231.6 %all-gather.3.cloned.1.call-start = ((), (), s32[]{:S(2)}) async-start(), calls=%async_computation.26 | async-start | bytes 1572864 | tf_op jit(solution)/shard_map/all_gather | solution.py:198
  324.9 45.2 %all-to-all-start.4 = ((bf16[16,256,256]{2,1,0:T(8,128)(2,1)}), bf16[16,256,256]{2,1,0:T(8,128)(2,1)S(1)}, u32[]{:S(2)}, u32[]{:S(2)}) async-start(bf16[16,256,256]{2,1,0:T(8,128)(2,1)} %bitcast.564), calls=%async_computation.4 | async-start | bytes 4194304 | tf_op jit(solution)/shard_map/all_to_all | solution.py:165
  329.0 212.2 %all-gather.5.cloned.1.call-start = ((), (), s32[]{:S(2)}) async-start(), calls=%async_computation.27 | async-start | bytes 1572864 | tf_op jit(solution)/shard_map/all_gather | solution.py:198
  883.1 33.6 %all-to-all-start.7 = ((bf16[16,2,8192]{2,1,0:T(2,128)(2,1)}), bf16[16,2,8192]{2,1,0:T(2,128)(2,1)}, u32[]{:S(2)}, u32[]{:S(2)}) async-start(bf16[16,2,8192]{2,1,0:T(2,128)(2,1)} %reshape.497), calls=%async_computation.7 | async-start | bytes 1048576 | tf_op jit(solution)/shard_map/all_to_all | solution.py:353
  916.7 36.0 %all-to-all-start.9 = ((bf16[16,2,8192]{2,1,0:T(2,128)(2,1)}), bf16[16,2,8192]{2,1,0:T(2,128)(2,1)}, u32[]{:S(2)}, u32[]{:S(2)}) async-start(bf16[16,2,8192]{2,1,0:T(2,128)(2,1)} %reshape.501), calls=%async_computation.9 | async-start | bytes 1048576 | tf_op jit(solution)/shard_map/all_to_all | solution.py:361
  958.9 75.0 %all-reduce.10.cloned.1.call-start = ((), (), s32[]{:S(2)}) async-start(), calls=%async_computation.28 | async-start | bytes 2097152 | tf_op jit(solution)/shard_map/psum | solution.py:395
  993.3 532.7 %reduce-scatter.39.cloned.1.call-start = ((), (), s32[]{:S(2)}) async-start(), calls=%async_computation.41 | async-start | bytes 557056
  996.4 531.2 %reduce-scatter.23.cloned.1.call-start = ((), (), s32[]{:S(2)}) async-start(), calls=%async_computation.33 | async-start | bytes 557056 | tf_op jit(solution)/shard_map/reduce_scatter | solution.py:105
  999.0 539.3 %reduce-scatter.19.cloned.1.call-start = ((), (), s32[]{:S(2)}) async-start(), calls=%async_computation.31 | async-start | bytes 1114112 | tf_op jit(solution)/shard_map/reduce_scatter | solution.py:105
  1076.1 468.8 %reduce-scatter.27.cloned.1.call-start = ((), (), s32[]{:S(2)}) async-start(), calls=%async_computation.35 | async-start | bytes 1114112 | tf_op jit(solution)/shard_map/reduce_scatter | solution.py:105
  1362.7 33.5 %all-to-all-start.13 = ((bf16[16,2,8192]{2,1,0:T(2,128)(2,1)}), bf16[16,2,8192]{2,1,0:T(2,128)(2,1)}, u32[]{:S(2)}, u32[]{:S(2)}) async-start(bf16[16,2,8192]{2,1,0:T(2,128)(2,1)} %reshape.507), calls=%async_computation.13 | async-start | bytes 1048576 | tf_op jit(solution)/shard_map/all_to_all | solution.py:361
  1396.1 43.4 %all-to-all-start.12 = ((bf16[16,2,8192]{2,1,0:T(2,128)(2,1)}), bf16[16,2,8192]{2,1,0:T(2,128)(2,1)}, u32[]{:S(2)}, u32[]{:S(2)}) async-start(bf16[16,2,8192]{2,1,0:T(2,128)(2,1)} %reshape.505), calls=%async_computation.12 | async-start | bytes 1048576 | tf_op jit(solution)/shard_map/all_to_all | solution.py:354
  1402.3 142.7 %reduce-scatter.25.cloned.1.call-start = ((), (), s32[]{:S(2)}) async-start(), calls=%async_computation.34 | async-start | bytes 1114112 | tf_op jit(solution)/shard_map/reduce_scatter | solution.py:105
  1445.5 101.0 %reduce-scatter.37.cloned.1.call-start = ((), (), s32[]{:S(2)}) async-start(), calls=%async_computation.40 | async-start | bytes 557056
  1456.9 125.6 %reduce-scatter.21.cloned.1.call-start = ((), (), s32[]{:S(2)}) async-start(), calls=%async_computation.32 | async-start | bytes 557056 | tf_op jit(solution)/shard_map/reduce_scatter | solution.py:105
  1459.5 165.0 %all-reduce.12.cloned.1.call-start = ((), (), s32[]{:S(2)}) async-start(), calls=%async_computation.29 | async-start | bytes 2097152 | tf_op jit(solution)/shard_map/psum | solution.py:395
  1468.3 218.2 %reduce-scatter.17.cloned.1.call-start = ((), (), s32[]{:S(2)}) async-start(), calls=%async_computation.30 | async-start | bytes 1114112 | tf_op jit(solution)/shard_map/reduce_scatter | solution.py:105
  1470.6 283.8 %reduce-scatter.35.cloned.1.call-start = ((), (), s32[]{:S(2)}) async-start(), calls=%async_computation.39 | async-start | bytes 3063808 | tf_op jit(solution)/shard_map/reduce_scatter | solution.py:105
  1476.7 345.9 %reduce-scatter.33.cloned.1.call-start = ((), (), s32[]{:S(2)}) async-start(), calls=%async_computation.38 | async-start | bytes 3063808 | tf_op jit(solution)/shard_map/reduce_scatter | solution.py:105
  1484.0 422.9 %reduce-scatter.31.cloned.1.call-start = ((), (), s32[]{:S(2)}) async-start(), calls=%async_computation.37 | async-start | bytes 6127616 | tf_op jit(solution)/shard_map/reduce_scatter | solution.py:105
  1499.8 491.5 %reduce-scatter.29.cloned.1.call-start = ((), (), s32[]{:S(2)}) async-start(), calls=%async_computation.36 | async-start | bytes 6127616 | tf_op jit(solution)/shard_map/reduce_scatter | solution.py:105
  1526.9 62.0 %collective-permute-start.1 = (f32[64,256]{0,1:T(8,128)S(1)}, f32[64,256]{0,1:T(8,128)S(1)}, u32[]{:S(2)}, u32[]{:S(2)}) collective-permute-start(f32[64,256]{0,1:T(8,128)S(1)} %convert_element_type.290), channel_id=1, source_target_pairs={{0,0},{1,8},{2,1},{3,9},{4,2},{5,10},{6,3},{7,11},{8,4},{9,12},{10... | collective-permute-start | bytes 196616 | tf_op jit(solution)/shard_map/ppermute | solution.py:406
  1547.4 41.5 %collective-permute-start = (f32[64,256]{0,1:T(8,128)S(1)}, f32[64,256]{0,1:T(8,128)S(1)}, u32[]{:S(2)}, u32[]{:S(2)}) collective-permute-start(f32[64,256]{0,1:T(8,128)S(1)} %convert_element_type.288), channel_id=1, source_target_pairs={{0,0},{1,8},{2,1},{3,9},{4,2},{5,10},{6,3},{7,11},{8,4},{9,12},{10... | collective-permute-start | bytes 196616 | tf_op jit(solution)/shard_map/ppermute | solution.py:406
  (137 other events, 1814.1 us)
Sparse Core Ops, SparseCore 0:
  257.2 20.7 all-gather.2
  521.4 19.7 all-gather.4
  993.4 40.3 all-reduce.9
  1037.7 56.0 reduce-scatter.38
  1097.2 56.2 reduce-scatter.22
  1157.4 56.4 reduce-scatter.18
  1217.5 56.5 reduce-scatter.26
  1407.2 59.3 reduce-scatter.24
  1470.2 53.6 reduce-scatter.36
  1527.7 54.7 reduce-scatter.20
  1585.4 39.0 all-reduce.11
  1629.0 57.4 reduce-scatter.16
  1690.2 64.1 reduce-scatter.34
  1758.5 64.0 reduce-scatter.32
  1826.4 80.4 reduce-scatter.30
  1910.6 80.6 reduce-scatter.28

commit v2 on v0

v2 whole, which is shorter than its diff:
```python
import functools

import jax
import jax.numpy as jnp
from jax import lax
from jax.experimental import pallas as pl
from jax.experimental.pallas import tpu as pltpu
from jax.sharding import PartitionSpec as P

HD = 64
LAYERS = 2
GROUPS = 2
NEG_FILL = -1e30
LOG2E = 1.4426950408889634
ATT_SCALE = HD ** (-0.5)
NT = (((1,), (1,)), ((), ()))
TN = (((0,), (0,)), ((), ()))
F32 = jnp.float32
BF16 = jnp.bfloat16
KEY_BLOCK = 512
QUERY_BLOCK = 1024


def dot_as(left, right, dims):
    return lax.dot_general(left, right, dims, preferred_element_type=F32)


def dot(left, right):
    return jnp.dot(left, right, preferred_element_type=F32)


def slot_of(piece, place, seq_count):
    source = piece // 2 if piece % 2 == 0 else (2 * seq_count - 1 - piece) // 2
    return source ^ place


def order_keys(place, lat_ref, keys, keys_t, seq_count, half):
    for piece in range(2 * seq_count):
        slot = slot_of(piece, place, seq_count)
        keys[pl.ds(piece * half, half), :] = lat_ref[0, slot, pl.ds((piece % 2) * half, half), :]
    for first in range(0, 2 * seq_count * half, 256):
        keys_t[:, first : first + 256] = keys[first : first + 256, :].T


def block_bounds(scalars, row, part, half):
    first = scalars[1 + part]
    cut = scalars[3 + row]
    last = first + half - 1
    low_min = jnp.where(first >= cut, cut, 0)
    low_max = jnp.where(last >= cut, cut, 0)
    return first, cut, low_min // KEY_BLOCK, last // KEY_BLOCK + 1, low_max


def hide(scores, block_at, first, cut, half):
    lanes = lax.broadcasted_iota(jnp.int32, (1, scores.shape[1]), 1)
    query_at = first + lanes % half
    low = jnp.where(query_at >= cut, cut, 0)
    key_at = block_at * KEY_BLOCK + lax.broadcasted_iota(jnp.int32, scores.shape, 0)
    return jnp.where((key_at <= query_at) & (key_at >= low), scores, NEG_FILL)


def over_blocks(bounds, block):
    first, _, start, stop, low_max = bounds

    def body(block_at, carry):
        edge = (block_at * KEY_BLOCK + KEY_BLOCK - 1 > first) | (block_at * KEY_BLOCK < low_max)

        @pl.when(edge)
        def _():
            block(block_at, True)

        @pl.when(jnp.logical_not(edge))
        def _():
            block(block_at, False)

        return carry

    lax.fori_loop(start, stop, body, 0)


def attend_kernel(
    scalars,
    q_ref,
    lat_ref,
    up_k_ref,
    up_v_ref,
    out_ref,
    out_t_ref,
    log_ref,
    query_ref,
    mixed_ref,
    keys,
    keys_t,
    top,
    total,
    acc,
    *,
    seq_count,
    half,
    heads,
):
    row, part = pl.program_id(0), pl.program_id(1)

    @pl.when(part == 0)
    def _():
        order_keys(scalars[0], lat_ref, keys, keys_t, seq_count, half)

    for head in range(heads):
        feats = slice(head * HD, (head + 1) * HD)
        lifted = dot_as(q_ref[0, 0, feats, :], up_k_ref[feats, :], TN)
        query_ref[0, 0, head * half : (head + 1) * half, :] = (lifted * (LOG2E * ATT_SCALE)).astype(
            BF16
        )
    top[...] = jnp.full_like(top, NEG_FILL)
    total[...] = jnp.zeros_like(total)
    acc[...] = jnp.zeros_like(acc)
    bounds = block_bounds(scalars, row, part, half)
    columns = heads * half
    width = min(QUERY_BLOCK, columns)

    def block(block_at, edge):
        at = pl.multiple_of(block_at * KEY_BLOCK, KEY_BLOCK)
        key_rows = keys[pl.ds(at, KEY_BLOCK), :]
        key_cols = keys_t[:, pl.ds(at, KEY_BLOCK)]
        for col in range(0, columns, width):
            cols = slice(col, col + width)
            scores = dot_as(key_rows, query_ref[0, 0, cols, :], NT)
            if edge:
                scores = hide(scores, block_at, bounds[0], bounds[1], half)
            old_top = top[:, cols]
            new_top = jnp.maximum(old_top, jnp.max(scores, axis=0, keepdims=True))
            probs = jnp.exp2(scores - new_top)
            fade = jnp.exp2(old_top - new_top)
            total[:, cols] = total[:, cols] * fade + jnp.sum(probs, axis=0, keepdims=True)
            top[:, cols] = new_top
            acc[:, cols] = acc[:, cols] * fade + dot(key_cols, probs.astype(BF16))

    over_blocks(bounds, block)
    mixed_ref[0, 0, :, :] = (acc[...] * (1.0 / total[...])).astype(BF16)
    log_ref[0, 0, :, :] = top[...] + jnp.log2(total[...])
    for head in range(heads):
        feats = slice(head * HD, (head + 1) * HD)
        out_t = dot(
            up_v_ref[feats, :], mixed_ref[0, 0, :, head * half : (head + 1) * half]
        ).astype(BF16)
        out_t_ref[0, 0, feats, :] = out_t
        out_ref[0, 0, :, feats] = out_t.T


def attend_back_kernel(
    scalars,
    q_ref,
    d_out_ref,
    out_ref,
    lat_ref,
    up_k_ref,
    up_v_ref,
    query_ref,
    mixed_ref,
    log_ref,
    dq_ref,
    d_lat_ref,
    d_up_k_ref,
    d_up_v_ref,
    keys,
    keys_t,
    d_keys,
    query_plain,
    d_mixed,
    delta,
    d_query,
    *,
    seq_count,
    half,
    heads,
):
    row, part = pl.program_id(0), pl.program_id(1)

    @pl.when(part == 0)
    def _():
        order_keys(scalars[0], lat_ref, keys, keys_t, seq_count, half)
        d_keys[...] = jnp.zeros_like(d_keys)

    @pl.when((part == 0) & (row == 0))
    def _():
        d_up_k_ref[...] = jnp.zeros_like(d_up_k_ref)
        d_up_v_ref[...] = jnp.zeros_like(d_up_v_ref)

    for head in range(heads):
        feats = slice(head * HD, (head + 1) * HD)
        cols = slice(head * half, (head + 1) * half)
        d_out = d_out_ref[0, 0, feats, :]
        query_plain[cols, :] = (
            dot_as(q_ref[0, 0, feats, :], up_k_ref[feats, :], TN) * ATT_SCALE
        ).astype(BF16)
        d_mixed[cols, :] = dot_as(d_out, up_v_ref[feats, :], TN).astype(BF16)
        delta[:, cols] = jnp.sum(
            d_out.astype(F32) * out_ref[0, 0, feats, :].astype(F32), axis=0, keepdims=True
        )
    d_query[...] = jnp.zeros_like(d_query)
    bounds = block_bounds(scalars, row, part, half)
    columns = heads * half
    width = min(QUERY_BLOCK, columns)

    def block(block_at, edge):
        at = pl.multiple_of(block_at * KEY_BLOCK, KEY_BLOCK)
        key_rows = keys[pl.ds(at, KEY_BLOCK), :]
        key_cols = keys_t[:, pl.ds(at, KEY_BLOCK)]
        key_total = d_keys[pl.ds(at, KEY_BLOCK), :]
        for col in range(0, columns, width):
            cols = slice(col, col + width)
            scores = dot_as(key_rows, query_ref[0, 0, cols, :], NT)
            if edge:
                scores = hide(scores, block_at, bounds[0], bounds[1], half)
            probs = jnp.exp2(scores - log_ref[0, 0, :, cols])
            d_probs = dot_as(key_rows, d_mixed[cols, :], NT)
            d_scores = (probs * (d_probs - delta[:, cols])).astype(BF16)
            key_total = key_total + (
                dot(d_scores, query_plain[cols, :]) + dot(probs.astype(BF16), d_mixed[cols, :])
            )
            d_query[:, cols] += dot(key_cols, d_scores)
        d_keys[pl.ds(at, KEY_BLOCK), :] = key_total

    over_blocks(bounds, block)
    for head in range(heads):
        feats = slice(head * HD, (head + 1) * HD)
        cols = slice(head * half, (head + 1) * half)
        d_lifted = (d_query[:, cols] * ATT_SCALE).astype(BF16)
        dq_ref[0, 0, :, feats] = dot(up_k_ref[feats, :], d_lifted).astype(BF16).T
        d_up_k_ref[feats, :] += dot_as(q_ref[0, 0, feats, :], d_lifted, NT)
        d_up_v_ref[feats, :] += dot_as(d_out_ref[0, 0, feats, :], mixed_ref[0, 0, :, cols], NT)

    @pl.when(part == 1)
    def _():
        for piece in range(2 * seq_count):
            slot = slot_of(piece, scalars[0], seq_count)
            d_lat_ref[0, slot, pl.ds((piece % 2) * half, half), :] = d_keys[
                pl.ds(piece * half, half), :
            ].astype(BF16)


def attention_sizes(queries_t, lats):
    rows, _, feats, half = queries_t.shape
    group_feats = feats // GROUPS
    heads = group_feats // HD
    seq_count, size = lats.shape[1], lats.shape[3]
    return rows, half, group_feats, heads, heads * half, seq_count, size, seq_count * 2 * half


def head_spec(group_feats, half, group):
    return pl.BlockSpec((1, 1, group_feats, half), lambda row, part, _: (row, part, group, 0))


def plain_spec(*block):
    return pl.BlockSpec((1, 1) + block, lambda row, part, _: (row, part, 0, 0))


def up_spec(group_feats, size, at):
    return pl.BlockSpec((group_feats, size), lambda row, part, _: (at, 0))


def attend(scalars, queries_t, lats, up_t, group):
    rows, half, group_feats, heads, columns, seq_count, size, keys = attention_sizes(
        queries_t, lats
    )
    return pl.pallas_call(
        functools.partial(attend_kernel, seq_count=seq_count, half=half, heads=heads),
        grid_spec=pltpu.PrefetchScalarGridSpec(
            num_scalar_prefetch=1,
            grid=(rows, 2),
            in_specs=[
                head_spec(group_feats, half, group),
                pl.BlockSpec((1,) + lats.shape[1:], lambda row, part, _: (row, 0, 0, 0)),
                up_spec(group_feats, size, group),
                up_spec(group_feats, size, GROUPS + group),
            ],
            out_specs=[
                plain_spec(half, group_feats),
                plain_spec(group_feats, half),
                plain_spec(1, columns),
                plain_spec(columns, size),
                plain_spec(size, columns),
            ],
            scratch_shapes=[
                pltpu.VMEM((keys, size), BF16),
                pltpu.VMEM((size, keys), BF16),
                pltpu.VMEM((1, columns), F32),
                pltpu.VMEM((1, columns), F32),
                pltpu.VMEM((size, columns), F32),
            ],
        ),
        out_shape=[
            jax.ShapeDtypeStruct((rows, 2, half, group_feats), BF16),
            jax.ShapeDtypeStruct((rows, 2, group_feats, half), BF16),
            jax.ShapeDtypeStruct((rows, 2, 1, columns), F32),
            jax.ShapeDtypeStruct((rows, 2, columns, size), BF16),
            jax.ShapeDtypeStruct((rows, 2, size, columns), BF16),
        ],
        compiler_params=pltpu.CompilerParams(
            dimension_semantics=("arbitrary", "arbitrary"), vmem_limit_bytes=40 << 20
        ),
        cost_estimate=pl.CostEstimate(
            flops=rows * 2 * columns * keys * size * 2,
            bytes_accessed=rows * (2 * keys * size + 8 * columns * size),
            transcendentals=rows * columns * keys,
        ),
        name="attend",
    )(scalars, queries_t, lats, up_t, up_t)


def attend_back(scalars, queries_t, d_heads_t, heads_t, lats, up_t, kept, group):
    rows, half, group_feats, heads, columns, seq_count, size, keys = attention_sizes(
        queries_t, lats
    )
    logs, lifted, mixed = kept
    lat_spec = pl.BlockSpec((1,) + lats.shape[1:], lambda row, part, _: (row, 0, 0, 0))
    return pl.pallas_call(
        functools.partial(attend_back_kernel, seq_count=seq_count, half=half, heads=heads),
        grid_spec=pltpu.PrefetchScalarGridSpec(
            num_scalar_prefetch=1,
            grid=(rows, 2),
            in_specs=[
                head_spec(group_feats, half, group),
                head_spec(group_feats, half, group),
                plain_spec(group_feats, half),
                lat_spec,
                up_spec(group_feats, size, group),
                up_spec(group_feats, size, GROUPS + group),
                plain_spec(columns, size),
                plain_spec(size, columns),
                plain_spec(1, columns),
            ],
            out_specs=[
                plain_spec(half, group_feats),
                lat_spec,
                up_spec(group_feats, size, 0),
                up_spec(group_feats, size, 0),
            ],
            scratch_shapes=[
                pltpu.VMEM((keys, size), BF16),
                pltpu.VMEM((size, keys), BF16),
                pltpu.VMEM((keys, size), F32),
                pltpu.VMEM((columns, size), BF16),
                pltpu.VMEM((columns, size), BF16),
                pltpu.VMEM((1, columns), F32),
                pltpu.VMEM((size, columns), F32),
            ],
        ),
        out_shape=[
            jax.ShapeDtypeStruct((rows, 2, half, group_feats), BF16),
            jax.ShapeDtypeStruct(lats.shape, BF16),
            jax.ShapeDtypeStruct((group_feats, size), F32),
            jax.ShapeDtypeStruct((group_feats, size), F32),
        ],
        compiler_params=pltpu.CompilerParams(
            dimension_semantics=("arbitrary", "arbitrary"), vmem_limit_bytes=48 << 20
        ),
        cost_estimate=pl.CostEstimate(
            flops=rows * 5 * columns * keys * size * 2,
            bytes_accessed=rows * (4 * keys * size + 12 * columns * size),
            transcendentals=rows * columns * keys,
        ),
        name="attend_back",
    )(scalars, queries_t, d_heads_t, heads_t, lats, up_t, up_t, lifted, mixed, logs)


def rms_scale(value_rows):
    return lax.rsqrt(jnp.mean(value_rows * value_rows, axis=-1, keepdims=True) + 1e-06)


def norm_back(grad_in, value_rows, scale_rows, gain_vec):
    normed = value_rows * scale_rows
    upstream = grad_in * gain_vec
    return (
        scale_rows * (upstream - normed * jnp.mean(upstream * normed, axis=-1, keepdims=True)),
        jnp.sum(grad_in * normed, axis=0),
    )


def hidden_tile(hidden):
    return 256 if hidden % 256 == 0 else hidden


def feed_kernel(
    heads_a,
    heads_b,
    state,
    w_out,
    bias,
    gain,
    next_gain,
    w_gate,
    w_up,
    w_down,
    hidden_in,
    normed_mlp,
    gate,
    up,
    act,
    following,
    normed_next,
):
    step = pl.program_id(0)
    group_cols = heads_a.shape[1]

    @pl.when(step == 0)
    def _():
        value = state[...] + (
            dot(heads_a[...], w_out[0, :group_cols, :])
            + dot(heads_b[...], w_out[0, group_cols:, :])
            + bias[0]
        )
        hidden_in[...] = value
        normed_mlp[...] = (value * rms_scale(value) * gain[0]).astype(BF16)
        following[...] = value

    gate_part = dot(normed_mlp[...], w_gate[0])
    up_part = dot(normed_mlp[...], w_up[0])
    act_part = (gate_part * jax.nn.sigmoid(gate_part) * up_part).astype(BF16)
    gate[...] = gate_part.astype(BF16)
    up[...] = up_part.astype(BF16)
    act[...] = act_part
    following[...] += dot(act_part, w_down[0])

    @pl.when(step == pl.num_programs(0) - 1)
    def _():
        value = following[...]
        normed_next[...] = (value * rms_scale(value) * next_gain[0]).astype(BF16)


def feed(state, heads, layer, next_layer, weights):
    out_weight, out_bias, mlp_gain, attn_gain, gate_up_matrix, down_matrix = weights
    toks, width = state.shape
    hidden = down_matrix.shape[1]
    tile = hidden_tile(hidden)
    steps = hidden // tile
    whole = lambda value: pl.BlockSpec(value.shape, lambda step: (0,) * value.ndim)
    tokens_full = pl.BlockSpec((toks, width), lambda step: (0, 0))
    tokens_tile = pl.BlockSpec((toks, tile), lambda step: (0, step))
    vector = lambda at: pl.BlockSpec((1, 1, width), lambda step: (at, 0, 0))
    wide = lambda dtype: jax.ShapeDtypeStruct((toks, width), dtype)
    tiled = jax.ShapeDtypeStruct((toks, hidden), BF16)
    return pl.pallas_call(
        feed_kernel,
        grid=(steps,),
        in_specs=[
            whole(heads[0]),
            whole(heads[1]),
            tokens_full,
            pl.BlockSpec((1,) + out_weight.shape[1:], lambda step: (layer, 0, 0)),
            vector(layer),
            vector(layer),
            vector(next_layer),
            pl.BlockSpec((1, width, tile), lambda step: (layer, 0, step)),
            pl.BlockSpec((1, width, tile), lambda step: (layer, 0, steps + step)),
            pl.BlockSpec((1, tile, width), lambda step: (layer, step, 0)),
        ],
        out_specs=[
            tokens_full,
            tokens_full,
            tokens_tile,
            tokens_tile,
            tokens_tile,
            tokens_full,
            tokens_full,
        ],
        out_shape=[wide(F32), wide(BF16), tiled, tiled, tiled, wide(F32), wide(BF16)],
        compiler_params=pltpu.CompilerParams(
            dimension_semantics=("arbitrary",), vmem_limit_bytes=36 << 20
        ),
        cost_estimate=pl.CostEstimate(
            flops=2 * toks * width * (3 * hidden + width),
            bytes_accessed=2 * width * (3 * hidden + width) + 6 * toks * hidden,
            transcendentals=toks * hidden,
        ),
        name="feed",
    )(
        heads[0],
        heads[1],
        state,
        out_weight,
        out_bias[:, None],
        mlp_gain[:, None],
        attn_gain[:, None],
        gate_up_matrix,
        gate_up_matrix,
        down_matrix,
    )


def feed_back_kernel(
    grad,
    hidden_in,
    gain,
    w_out,
    gate,
    up,
    w_gate,
    w_up,
    w_down,
    d_gate,
    d_up,
    d_mlp,
    d_hidden_in,
    d_attn,
    d_heads_t,
    gain_sum,
    bias_sum,
    acc,
    *,
    half,
):
    step = pl.program_id(0)

    @pl.when(step == 0)
    def _():
        d_mlp[...] = grad[...].astype(BF16)
        acc[...] = jnp.zeros_like(acc)

    d_act = dot_as(d_mlp[...], w_down[0], NT)
    gate_part = gate[...].astype(F32)
    up_part = up[...].astype(F32)
    sig_gate = jax.nn.sigmoid(gate_part)
    d_gate_part = (d_act * up_part * sig_gate * (1.0 + gate_part * (1.0 - sig_gate))).astype(BF16)
    d_up_part = (d_act * gate_part * sig_gate).astype(BF16)
    d_gate[...] = d_gate_part
    d_up[...] = d_up_part
    acc[...] += dot_as(d_gate_part, w_gate[0], NT) + dot_as(d_up_part, w_up[0], NT)

    @pl.when(step == pl.num_programs(0) - 1)
    def _():
        value = hidden_in[...]
        scale_rows = rms_scale(value)
        d_norm, gain_terms = norm_back(acc[...], value, scale_rows, gain[0])
        gain_sum[...] = gain_terms[None]
        total = grad[...] + d_norm
        low = total.astype(BF16)
        d_hidden_in[...] = total
        d_attn[...] = low
        bias_sum[...] = jnp.sum(low.astype(F32), axis=0, keepdims=True)
        for piece in range(d_heads_t.shape[0]):
            d_heads_t[piece] = dot_as(w_out[0], low[piece * half : (piece + 1) * half], NT).astype(
                BF16
            )


def feed_back(grad, hidden_in, gate, up, layer, half, weights):
    out_weight, _, mlp_gain, _, gate_up_matrix, down_matrix = weights
    toks, width = grad.shape
    heads_dim = out_weight.shape[1]
    hidden = down_matrix.shape[1]
    tile = hidden_tile(hidden)
    steps = hidden // tile
    tokens_full = pl.BlockSpec((toks, width), lambda step: (0, 0))
    tokens_tile = pl.BlockSpec((toks, tile), lambda step: (0, step))
    vector_out = pl.BlockSpec((1, width), lambda step: (0, 0))
    wide = lambda dtype: jax.ShapeDtypeStruct((toks, width), dtype)
    tiled = jax.ShapeDtypeStruct((toks, hidden), BF16)
    pieces = toks // half
    return pl.pallas_call(
        functools.partial(feed_back_kernel, half=half),
        grid=(steps,),
        in_specs=[
            tokens_full,
            tokens_full,
            pl.BlockSpec((1, 1, width), lambda step: (layer, 0, 0)),
            pl.BlockSpec((1,) + out_weight.shape[1:], lambda step: (layer, 0, 0)),
            tokens_tile,
            tokens_tile,
            pl.BlockSpec((1, width, tile), lambda step: (layer, 0, step)),
            pl.BlockSpec((1, width, tile), lambda step: (layer, 0, steps + step)),
            pl.BlockSpec((1, tile, width), lambda step: (layer, step, 0)),
        ],
        out_specs=[
            tokens_tile,
            tokens_tile,
            tokens_full,
            tokens_full,
            tokens_full,
            pl.BlockSpec((pieces, heads_dim, half), lambda step: (0, 0, 0)),
            vector_out,
            vector_out,
        ],
        out_shape=[
            tiled,
            tiled,
            wide(BF16),
            wide(F32),
            wide(BF16),
            jax.ShapeDtypeStruct((pieces, heads_dim, half), BF16),
            jax.ShapeDtypeStruct((1, width), F32),
            jax.ShapeDtypeStruct((1, width), F32),
        ],
        scratch_shapes=[pltpu.VMEM((toks, width), F32)],
        compiler_params=pltpu.CompilerParams(
            dimension_semantics=("arbitrary",), vmem_limit_bytes=36 << 20
        ),
        cost_estimate=pl.CostEstimate(
            flops=2 * toks * width * (3 * hidden + heads_dim),
            bytes_accessed=2 * width * (3 * hidden + heads_dim) + 8 * toks * hidden,
            transcendentals=toks * hidden,
        ),
        name="feed_back",
    )(
        grad,
        hidden_in,
        mlp_gain[:, None],
        out_weight,
        gate,
        up,
        gate_up_matrix,
        gate_up_matrix,
        down_matrix,
    )


def wide_sum_kernel(left_a, left_b, gate_a, gate_b, up_a, up_b, act_a, act_b, total):
    step = pl.program_id(0)
    third = pl.num_programs(0) // 3

    def add(right_a, right_b):
        total[...] = (dot(left_a[0], right_a[...]) + dot(left_b[0], right_b[...])).astype(BF16)

    @pl.when(step < third)
    def _():
        add(gate_a, gate_b)

    @pl.when((step >= third) & (step < 2 * third))
    def _():
        add(up_a, up_b)

    @pl.when(step >= 2 * third)
    def _():
        add(act_a, act_b)


def wide_sum(lefts, gates, ups, acts, columns):
    rows, toks = lefts[0].shape[1:]
    hidden = gates[0].shape[1]
    tile = hidden // 2 if hidden % 256 == 0 else hidden
    third = hidden // tile
    left_spec = pl.BlockSpec((1, rows, toks), lambda step: (step // (2 * third), 0, 0))

    def right_spec(at):
        return pl.BlockSpec(
            (toks, tile), lambda step: (0, jnp.clip(step - at * third, 0, third - 1))
        )

    return pl.pallas_call(
        wide_sum_kernel,
        grid=(3 * third,),
        in_specs=[left_spec] * 2 + [right_spec(at) for at in range(3) for _ in range(2)],
        out_specs=pl.BlockSpec((rows, tile), lambda step: (0, step)),
        out_shape=jax.ShapeDtypeStruct((rows, columns), BF16),
        compiler_params=pltpu.CompilerParams(
            dimension_semantics=("arbitrary",), vmem_limit_bytes=36 << 20
        ),
        cost_estimate=pl.CostEstimate(
            flops=4 * rows * toks * 3 * hidden,
            bytes_accessed=6 * hidden * (2 * toks + rows),
            transcendentals=0,
        ),
        name="wide_sum",
    )(*lefts, *gates, *ups, *acts)


def fill_kernel(left_a, left_b, a_first, a_second, b_first, b_second, _, total):
    step = pl.program_id(0)
    split = pl.num_programs(0) // 2

    @pl.when(step < split)
    def _():
        total[...] = (dot(left_a[...], a_first[...]) + dot(left_b[...], b_first[...])).astype(BF16)

    @pl.when(step >= split)
    def _():
        total[...] = (dot(left_a[...], a_second[...]) + dot(left_b[...], b_second[...])).astype(
            BF16
        )


def fill(lefts, rights, buffer, at):
    rows, toks = lefts[0].shape
    group_cols = rights[0][0].shape[1]
    tile = 256
    split = group_cols // tile
    first = at // tile
    whole = pl.BlockSpec((rows, toks), lambda step: (0, 0))
    spec_a = pl.BlockSpec((toks, tile), lambda step: (0, jnp.minimum(step, split - 1)))
    spec_b = pl.BlockSpec((toks, tile), lambda step: (0, jnp.maximum(step - split, 0)))
    return pl.pallas_call(
        fill_kernel,
        grid=(2 * split,),
        in_specs=[whole] * 2 + [spec_a, spec_b] * 2 + [pl.BlockSpec(memory_space=pl.ANY)],
        out_specs=pl.BlockSpec((rows, tile), lambda step: (0, first + step)),
        out_shape=jax.ShapeDtypeStruct(buffer.shape, buffer.dtype),
        input_output_aliases={6: 0},
        compiler_params=pltpu.CompilerParams(dimension_semantics=("arbitrary",)),
        cost_estimate=pl.CostEstimate(
            flops=8 * rows * toks * group_cols,
            bytes_accessed=8 * group_cols * toks + 4 * rows * group_cols,
            transcendentals=0,
        ),
        name="fill",
    )(*lefts, *rights[0], *rights[1], buffer)


def small_sum_kernel(*refs, count):
    left_a, left_b = refs[:2]
    rights, extra, total = refs[2 : 2 + 2 * count], refs[2 + 2 * count], refs[3 + 2 * count]
    at = 0
    for one in range(count):
        right_a, right_b = rights[one], rights[count + one]
        cols = right_a.shape[1]
        total[:, at : at + cols] = (
            dot(left_a[...], right_a[...]) + dot(left_b[...], right_b[...])
        ).astype(BF16)
        at += cols
    total[:, at:] = extra[...]


def small_sum(lefts, rights, extra):
    rows, toks = lefts[0].shape
    count = len(rights[0])
    cols = sum(value.shape[1] for value in rights[0])
    return pl.pallas_call(
        functools.partial(small_sum_kernel, count=count),
        out_shape=jax.ShapeDtypeStruct((rows, cols + extra.shape[1]), BF16),
        compiler_params=pltpu.CompilerParams(vmem_limit_bytes=36 << 20),
        cost_estimate=pl.CostEstimate(
            flops=4 * rows * toks * cols,
            bytes_accessed=4 * toks * cols + 2 * rows * cols,
            transcendentals=0,
        ),
        name="small_sum",
    )(*lefts, *rights[0], *rights[1], extra)


def shards(
    tokens,
    cotangent,
    domain_ids,
    domain_counts,
    domain_weights,
    seq_cuts,
    attn_gain,
    query_weight,
    latent_weight,
    latent_up,
    out_weight,
    out_bias,
    mlp_gain,
    gate_up_matrix,
    down_matrix,
):
    seq_count = lax.axis_size("seq")
    rep_count = lax.axis_size("rep")
    place = lax.axis_index("seq").astype(jnp.int32)
    side = lax.axis_index("rep").astype(jnp.int32)
    seq_rows, loc_len, width = tokens.shape
    rows = seq_rows // rep_count
    half = loc_len // 2
    toks = rows * loc_len
    heads_dim = query_weight.shape[2]
    size = latent_up.shape[1]
    hidden = down_matrix.shape[1]
    group_cols = heads_dim // GROUPS
    bits = [1 << at for at in range(seq_count.bit_length() - 1)]
    weights = (out_weight, out_bias, mlp_gain, attn_gain, gate_up_matrix, down_matrix)

    def swap_ends(value):
        moves = [(at, seq_count - 1 - at) for at in range(seq_count)]
        return lax.ppermute(value, "seq", moves)

    def across(value):
        return lax.ppermute(value, "rep", [(at, rep_count - 1 - at) for at in range(rep_count)])

    def trade(value, bit):
        return lax.ppermute(value, "seq", [(at, at ^ bit) for at in range(seq_count)])

    def rows_of(value, owner):
        return lax.dynamic_slice_in_dim(value, owner * rows, rows, 0)

    def zigzag(value, owner):
        mine = rows_of(value, owner)
        mine = mine.reshape((rows, 2, half) + mine.shape[2:])
        return jnp.stack([mine[:, 0], swap_ends(mine[:, 1])], axis=1)

    def zigzag_tokens(value, owner):
        return zigzag(value, owner).reshape(toks, value.shape[-1])

    def spread(value):
        value = value[:, None]
        for bit in reversed(bits):
            held = value.shape[1]
            value = jnp.stack([value, trade(value, bit)], axis=2).reshape(
                (rows, 2 * held) + value.shape[2:]
            )
        return value

    def gather_sum(value):
        for bit in bits:
            left = value.shape[1] // 2
            pairs = value.reshape((rows, left, 2) + value.shape[2:])
            got = trade(pairs[:, :, 1], bit)
            value = (pairs[:, :, 0].astype(F32) + got.astype(F32)).astype(BF16)
        return value[:, 0]

    block = width // (seq_count * rep_count)
    kept_rows = seq_count * block
    row_at = jnp.arange(kept_rows, dtype=jnp.int32)
    step_at = row_at // block
    distance = jnp.zeros_like(row_at)
    for level, bit in enumerate(bits):
        distance = distance + (step_at // (seq_count // 2 >> level)) % 2 * bit
    halving_step = place ^ distance
    col_at = jnp.arange(width, dtype=jnp.int32)

    def picker(steps):
        source = (steps * rep_count + side) * block + row_at % block
        return (source[:, None] == col_at[None, :]).astype(BF16)

    pick = picker(step_at)
    pick_halving = picker(halving_step)
    to_halving = (
        (halving_step * block + row_at % block)[:, None] == row_at[None, :]
    ).astype(BF16)

    def picked(picks, value):
        return dot_as(picks, value, NT).astype(BF16)

    def halving_sum(value):
        kept, sent = value[: kept_rows // 2], value[kept_rows // 2 :]
        for bit in bits:
            got = trade(sent, bit)
            if bit == bits[-1]:
                return kept.astype(F32) + got.astype(F32)
            left = kept.shape[0] // 2
            sent = (kept[left:].astype(F32) + got[left:].astype(F32)).astype(BF16)
            kept = (kept[:left].astype(F32) + got[:left].astype(F32)).astype(BF16)

    domain_total = domain_counts.shape[0]
    all_tokens = seq_rows * loc_len * seq_count
    per_domain = domain_weights * (all_tokens / domain_total) / domain_counts.astype(F32)
    one_hot = (domain_ids[..., None] == jnp.arange(domain_total, dtype=jnp.int32)).astype(F32)
    row_scale = jnp.sum(one_hot * per_domain, axis=-1)
    scalars = jnp.concatenate(
        [
            jnp.stack([place, place * loc_len, (2 * seq_count - 1 - 2 * place) * half]),
            rows_of(seq_cuts, side),
        ]
    )

    def project_back(d_hidden_in, dq, d_lat, state, layer):
        d_normed = 0.0
        for group in range(GROUPS):
            d_normed = d_normed + dot_as(
                dq[group],
                query_weight[layer, :, group * group_cols : (group + 1) * group_cols],
                NT,
            )
            d_normed = d_normed + dot_as(
                d_lat[group], latent_weight[layer, :, group * size : (group + 1) * size], NT
            )
        d_norm, g_gain = norm_back(d_normed, state, rms_scale(state), attn_gain[layer])
        return d_hidden_in + d_norm, g_gain

    def first_normed(state):
        return (state * rms_scale(state) * attn_gain[0]).astype(BF16)

    own = zigzag_tokens(tokens, side).astype(F32)
    other = zigzag_tokens(tokens, rep_count - 1 - side).astype(F32)
    normed_own, normed_other = first_normed(own), first_normed(other)
    saved = []
    for layer in range(LAYERS):
        next_layer = min(layer + 1, LAYERS - 1)
        lats = [
            spread(
                dot(normed_own, latent_weight[layer, :, group * size : (group + 1) * size])
                .astype(BF16)
                .reshape(rows, loc_len, size)
            )
            for group in range(GROUPS)
        ]
        queries_t = jnp.einsum(
            "rpid,df->rpfi",
            normed_own.reshape(rows, 2, half, width),
            query_weight[layer],
            preferred_element_type=F32,
        ).astype(BF16)
        up_t = latent_up[layer].T
        heads, attended = [], []
        for group in range(GROUPS):
            out, *rest = attend(scalars, queries_t, lats[group], up_t, group)
            heads.append(out.reshape(toks, group_cols))
            attended.append(rest)
        other_heads = [across(out) for out in heads]
        hidden_own = feed(own, heads, layer, next_layer, weights)
        hidden_other = feed(other, other_heads, layer, next_layer, weights)
        saved.append(
            (
                (own, normed_own, heads, hidden_own),
                (other, normed_other, other_heads, hidden_other),
                (lats, queries_t, up_t, attended),
            )
        )
        own, normed_own = hidden_own[5:]
        other, normed_other = hidden_other[5:]

    def natural(value):
        value = value.reshape(rows, 2, half, width)
        value = jnp.concatenate([value[:, 0], swap_ends(value[:, 1])], axis=1)
        both = jnp.stack([value, across(value)])
        return jnp.where(side == 0, both, both[::-1]).reshape(seq_rows, loc_len, width)

    output = natural(own.astype(BF16))
    grad_own = zigzag_tokens(cotangent, side).astype(F32) * zigzag(row_scale, side).reshape(toks, 1)
    grad_other = zigzag_tokens(cotangent, rep_count - 1 - side).astype(F32) * zigzag(
        row_scale, rep_count - 1 - side
    ).reshape(toks, 1)
    wide_cols = 3 * hidden + heads_dim
    layer_grads = []
    for layer in reversed(range(LAYERS)):
        kept_own, kept_other, (lats, queries_t, up_t, attended) = saved[layer]
        own, normed_own, heads, hidden_own = kept_own
        other, normed_other, other_heads, hidden_other = kept_other
        back_own, back_other = (
            feed_back(grad, kept[0], kept[2], kept[3], layer, half, weights)
            for grad, kept in ((grad_own, hidden_own), (grad_other, hidden_other))
        )
        d_heads_t = back_own[5].reshape(rows, 2, heads_dim, half)
        dq, d_lat, up_k, up_v = [], [], [], []
        for group in range(GROUPS):
            dq_one, d_lat_one, up_k_one, up_v_one = attend_back(
                scalars,
                queries_t,
                d_heads_t,
                attended[group][0],
                lats[group],
                up_t,
                attended[group][1:],
                group,
            )
            dq.append(dq_one.reshape(toks, group_cols))
            d_lat.append(gather_sum(d_lat_one).reshape(toks, size))
            up_k.append(up_k_one)
            up_v.append(up_v_one)
        dq_other = [across(value) for value in dq]
        d_lat_other = [across(value) for value in d_lat]
        grad_own, attn_gain_own = project_back(back_own[3], dq, d_lat, own, layer)
        grad_other, attn_gain_other = project_back(
            back_other[3], dq_other, d_lat_other, other, layer
        )

        backs = (back_own, back_other)
        hiddens = (hidden_own, hidden_other)
        lefts = [
            jnp.stack([picked(pick, hid[1]), picked(pick, back[2])])
            for hid, back in zip(hiddens, backs)
        ]
        wide = wide_sum(
            lefts,
            [back[0] for back in backs],
            [back[1] for back in backs],
            [hid[4] for hid in hiddens],
            wide_cols,
        )
        wide = fill(
            [picked(pick, back[4]) for back in backs], [heads, other_heads], wide, 3 * hidden
        )
        wide = lax.psum_scatter(wide, "seq", scatter_dimension=0, tiled=True).astype(F32)

        up_rows = jnp.concatenate(up_k + up_v, axis=0)
        up_block = up_rows.shape[0] // (seq_count * rep_count)
        up_rows = up_rows.reshape(seq_count, rep_count, up_block, size)
        up_kept = lax.dynamic_index_in_dim(up_rows, side, 1, False)
        up_sent = lax.dynamic_index_in_dim(up_rows, rep_count - 1 - side, 1, False).astype(BF16)
        up_rows = (up_kept + across(up_sent).astype(F32)).astype(BF16)
        folds = up_block // block
        up_rows = jnp.concatenate(
            [up_rows[:, at * block : (at + 1) * block] for at in range(folds)], axis=2
        ).reshape(kept_rows, folds * size)
        up_rows = dot(to_halving, up_rows).astype(BF16)
        normed = [picked(pick_halving, normed_own), picked(pick_halving, normed_other)]
        g_query = halving_sum(small_sum(normed, [dq, dq_other], up_rows))
        vectors = jnp.concatenate(
            [back_own[6] + back_other[6], back_own[7] + back_other[7]]
            + [(attn_gain_own + attn_gain_other)[None]]
            + [jnp.zeros((125, width), F32)]
        ).astype(BF16)
        g_latent = halving_sum(
            small_sum(normed, [d_lat, d_lat_other], picked(pick_halving, vectors))
        )
        g_vectors = g_latent[:, GROUPS * size :]
        g_up = jnp.concatenate(
            [
                g_query[:, heads_dim + at * size : heads_dim + (at + 1) * size]
                for at in range(folds)
            ]
        )
        layer_grads.insert(
            0,
            (
                g_vectors[:, 2],
                g_query[:, :heads_dim],
                g_latent[:, : GROUPS * size],
                g_up.T,
                wide[:, 3 * hidden :].T,
                g_vectors[:, 1],
                g_vectors[:, 0],
                wide[:, : 2 * hidden],
                wide[:, 2 * hidden : 3 * hidden].T,
            ),
        )
    stacked = [jnp.stack([grads[member] for grads in layer_grads]) for member in range(9)]
    return (output, natural(grad_own.astype(BF16)), *stacked)


def solution(mesh):
    rows = P(None, "seq", None)
    scattered = P(None, ("seq", "rep"))
    first = P(None, ("seq", "rep"), None)
    second = P(None, None, ("seq", "rep"))
    return jax.shard_map(
        shards,
        mesh=mesh,
        in_specs=(rows, rows, P(None, "seq")) + (P(),) * 12,
        out_specs=(
            rows,
            rows,
            scattered,
            first,
            first,
            second,
            second,
            scattered,
            scattered,
            first,
            second,
        ),
        check_vma=False,
    )
```

time: 4160 us -> 818 us (0.20)
  waiting for transfers between devices: 2670 us -> 252 us
  matrix products: 557 us -> 42.9 us
  other arithmetic: 499 us -> 33.8 us
  Pallas kernels: 0 us -> 301 us
  local copies, waits for them, and re-layouts: 248 us -> 75.6 us
  blocking collectives: 92.5 us -> 0 us
    reduce_scatter x6 -> x2, waiting for transfers between devices: 1760 us -> 0.02 us  [shards(): lax.psum_scatter(wide, 'seq', scatter_dimension=0, tiled=True).astype(F32)]
    unnamed x22 -> x2, waiting for transfers between devices: 708 us -> 0.03 us
    dot_general x154 -> x42, matrix products: 557 us -> 42.9 us  [the longest x34 36.6 us: dot_as(): return lax.dot_general(left, right, dims, preferred_element_type=F32)]
    pallas_call x0 -> x24, Pallas kernels: none -> 301 us  [the longest x4 88.1 us: attend_back(): pl.pallas_call(functools.partial(attend_back_kernel, seq_count=seq_count,...]
    ppermute x0 -> x72, waiting for transfers between devices: none -> 252 us  [the longest x48 231 us: trade(): lax.ppermute(value, 'seq', [(at, at ^ bit) for at in range(seq_count)])]
    unnamed x14 -> x0, other arithmetic: 185 us -> none
    convert_element_type x26 -> x29, other arithmetic: 177 us -> 12.3 us  [the longest x8 4.75 us: gather_sum(): value = (pairs[:, :, 0].astype(F32) + got.astype(F32)).astype(BF16)]
    all_to_all x12 -> x0, waiting for transfers between devices: 128 us -> none  [the longest x2 74.7 us: shards(): lax.all_to_all(spread_lat, 'seq', split_axis=0, concat_axis=1, tiled=True)]
  transfers between devices with their start and end apart: 28 -> 74, of which waited for: 21 -> 38; matrix products, arithmetic and copies ran while one was open for 7% -> 11% of each run, Pallas kernels for 0% -> 34%
where the time goes in v2:
time: 818 us; the launch traced here: 807 us
  Pallas kernels  301 us (37%)
  waiting for transfers between devices  252 us (31%)
  starting transfers between devices  83.9 us (10%)
  local copies, waits for them, and re-layouts  75.6 us (9%)
  matrix products  42.9 us (5%)
  other arithmetic  33.8 us (4%)
  between operations  16.9 us (2%)
    ppermute x48, waiting for transfers between devices, trade(): lax.ppermute(value, 'seq', [(at, at ^ bit) for at in range(seq_count)])  231 us
    pallas_call x4, Pallas kernels, attend_back(): pl.pallas_call(functools.partial(attend_back_kernel, seq_count=seq_count,...  88.1 us
    pallas_call x4, Pallas kernels, feed_back(): pl.pallas_call(functools.partial(feed_back_kernel, half=half), grid=(step...  68.8 us
    pallas_call x4, Pallas kernels, feed(): pl.pallas_call(feed_kernel, grid=(steps,), in_specs=[whole(heads[0]), who...  58 us
    ppermute x48, starting transfers between devices, trade(): lax.ppermute(value, 'seq', [(at, at ^ bit) for at in range(seq_count)])  57.3 us
    pallas_call x4, Pallas kernels, attend(): pl.pallas_call(functools.partial(attend_kernel, seq_count=seq_count, half...  57.2 us
    unnamed x300, local copies, waits for them, and re-layouts  56.1 us
    dot_general x34, matrix products, dot_as(): return lax.dot_general(left, right, dims, preferred_element_type=F32)  36.6 us
  transfers between devices with their start and end apart: 74, of which 38 were waited for; matrix products, arithmetic and copies ran while one was open for 11% of the time, Pallas kernels for 34%

profile of v2, /device:TPU:0, one launch (start us, length us, event | category | flops | bytes accessed | tf_op | source)
XLA Modules:
  0.0 806.6 jit_solution(523506248560697031)
XLA Ops:
  47.6 19.7 %collective-permute-start.5 = (bf16[1,1,256,256]{3,2,1,0:T(8,128)(2,1)S(1)}, bf16[1,1,256,256]{3,2,1,0:T(8,128)(2,1)S(1)}, u32[]{:S(2)}, u32[]{:S(2)}) collective-permute-start(bf16[1,1,256,256]{3,2,1,0:T(8,128)(2,1)S(1)} %bitcast.652), channel_id=1, source_target_pairs={{0,16},{2,18},{4,20},{6,22},{8,24},{10,26},{12,28},{14,30},{16,0},... | collective-permute-start | bytes 393224 | tf_op jit(solution)/shard_map/ppermute | solution.py:779
  115.1 14.2 %attend.5 = (bf16[1,2,128,512]{3,2,1,0:T(8,128)(2,1)S(1)}, bf16[1,2,512,128]{3,2,1,0:T(8,128)(2,1)S(1)}, f32[1,2,1,1024]{3,2,1,0:T(1,128)S(1)}, bf16[1,2,1024,25...) custom-call(s32[4]{0:T(128)S(1)} %pad_add_fusion.scalars, bf16[1,2,1024,128]{3,2,1,0:T(8,128)(2,1)S(1)} %fusion.45.q_ref, ...), custom_call_target="tpu_custom_call" | custom-call | flops 4294967296 | bytes 4194304 | tf_op jit(solution)/shard_map/attend/pallas_call | solution.py:266
  131.9 14.4 %attend.4 = (bf16[1,2,128,512]{3,2,1,0:T(8,128)(2,1)S(1)}, bf16[1,2,512,128]{3,2,1,0:T(8,128)(2,1)S(1)}, f32[1,2,1,1024]{3,2,1,0:T(1,128)S(1)}, bf16[1,2,1024,25...) custom-call(s32[4]{0:T(128)S(1)} %pad_add_fusion.scalars, bf16[1,2,1024,128]{3,2,1,0:T(8,128)(2,1)S(1)} %fusion.45.q_ref, ...), custom_call_target="tpu_custom_call" | custom-call | flops 4294967296 | bytes 4194304 | tf_op jit(solution)/shard_map/attend/pallas_call | solution.py:266
  149.1 14.0 %feed.4 = (f32[256,1024]{1,0:T(8,128)S(1)}, bf16[256,1024]{1,0:T(8,128)(2,1)S(1)}, bf16[256,2816]{1,0:T(8,128)(2,1)S(1)}, bf16[256,2816]{1,0:T(8,128)(2,1)S(1)},...) custom-call(bf16[256,512]{1,0:T(8,128)(2,1)S(1)} %bitcast.540, ...), custom_call_target="tpu_custom_call" | custom-call | flops 4966055936 | bytes 23724032 | tf_op jit(solution)/shard_map/feed/pallas_call | solution.py:443
  169.4 10.4 %collective-permute-done.13 = bf16[1,1,256,256]{3,2,1,0:T(8,128)(2,1)S(1)} collective-permute-done((bf16[1,1,256,256]{3,2,1,0:T(8,128)(2,1)S(1)}, bf16[1,1,256,256]{3,2,1,0:T(8,128)(2,1)S(1)}, u32[]{:S(2)}, u32[]{:S(2)}) %collective-permute-start.13) | collective-permute-done | bytes 131104 | tf_op jit(solution)/shard_map/ppermute | solution.py:779
  213.3 14.0 %feed.6 = (f32[256,1024]{1,0:T(8,128)S(1)}, bf16[256,1024]{1,0:T(8,128)(2,1)S(1)}, bf16[256,2816]{1,0:T(8,128)(2,1)S(1)}, bf16[256,2816]{1,0:T(8,128)(2,1)S(1)},...) custom-call(bf16[256,512]{1,0:T(8,128)(2,1)S(1)} %collective-permute-done.46.heads_a.b_first, ...), custom_call_target="tpu_custom_call" | custom-call | flops 4966055936 | bytes 23724032 | tf_op jit(solution)/shard_map/feed/pallas_call | solution.py:443
  232.2 14.6 %attend.7 = (bf16[1,2,128,512]{3,2,1,0:T(8,128)(2,1)S(1)}, bf16[1,2,512,128]{3,2,1,0:T(8,128)(2,1)S(1)}, f32[1,2,1,1024]{3,2,1,0:T(1,128)S(1)}, bf16[1,2,1024,25...) custom-call(s32[4]{0:T(128)S(1)} %pad_add_fusion.scalars, bf16[1,2,1024,128]{3,2,1,0:T(8,128)(2,1)S(1)} %fusion.42.q_ref, ...), custom_call_target="tpu_custom_call" | custom-call | flops 4294967296 | bytes 4194304 | tf_op jit(solution)/shard_map/attend/pallas_call | solution.py:266
  249.5 14.2 %attend.6 = (bf16[1,2,128,512]{3,2,1,0:T(8,128)(2,1)S(1)}, bf16[1,2,512,128]{3,2,1,0:T(8,128)(2,1)S(1)}, f32[1,2,1,1024]{3,2,1,0:T(1,128)S(1)}, bf16[1,2,1024,25...) custom-call(s32[4]{0:T(128)S(1)} %pad_add_fusion.scalars, bf16[1,2,1024,128]{3,2,1,0:T(8,128)(2,1)S(1)} %fusion.42.q_ref, ...), custom_call_target="tpu_custom_call" | custom-call | flops 4294967296 | bytes 4194304 | tf_op jit(solution)/shard_map/attend/pallas_call | solution.py:266
  265.3 15.1 %feed.5 = (f32[256,1024]{1,0:T(8,128)S(1)}, bf16[256,1024]{1,0:T(8,128)(2,1)S(1)}, bf16[256,2816]{1,0:T(8,128)(2,1)S(1)}, bf16[256,2816]{1,0:T(8,128)(2,1)S(1)},...) custom-call(bf16[256,512]{1,0:T(8,128)(2,1)S(1)} %bitcast.546, ...), custom_call_target="tpu_custom_call" | custom-call | flops 4966055936 | bytes 23724032 | tf_op jit(solution)/shard_map/feed/pallas_call | solution.py:443
  282.2 16.6 %feed_back.4 = (bf16[256,2816]{1,0:T(8,128)(2,1)S(1)}, bf16[256,2816]{1,0:T(8,128)(2,1)S(1)}, bf16[256,1024]{1,0:T(8,128)(2,1)S(1)}, f32[256,1024]{1,0:T(8,128)S...) custom-call(f32[256,1024]{1,0:T(8,128)S(1)} %convert_multiply_fusion, ...), custom_call_target="tpu_custom_call" | custom-call | flops 4966055936 | bytes 25165824 | tf_op jit(solution)/shard_map/feed_back/pallas_call | solution.py:560
  310.2 22.1 %attend_back.5 = (bf16[1,2,128,512]{3,2,1,0:T(8,128)(2,1)}, bf16[1,16,256,256]{3,2,1,0:T(8,128)(2,1)}, f32[512,256]{1,0:T(8,128)S(1)}, f32[512,256]{1,0:T(8,128)S(1)}) custom-call(s32[4]{0:T(128)S(1)} %pad_add_fusion.scalars, bf16[1,2,1024,128]{3,2,1,0:T(8,128)(2,1)S(1)} %copy-done.78, bf16[1,2,1024,128]{3,2,1,0:T(8,128)(2,1)S(1)} %bitcast.571, ...), custom_call_target="tpu_custom_call" | custom-call | flops 10737418240 | bytes 7340032 | tf_op jit(solution)/shard_map/attend_back/pallas_call | solution.py:317
  338.2 22.1 %attend_back.4 = (bf16[1,2,128,512]{3,2,1,0:T(8,128)(2,1)}, bf16[1,16,256,256]{3,2,1,0:T(8,128)(2,1)}, f32[512,256]{1,0:T(8,128)S(1)}, f32[512,256]{1,0:T(8,128)S(1)}) custom-call(s32[4]{0:T(128)S(1)} %pad_add_fusion.scalars, bf16[1,2,1024,128]{3,2,1,0:T(8,128)(2,1)S(1)} %copy-done.79, bf16[1,2,1024,128]{3,2,1,0:T(8,128)(2,1)S(1)} %bitcast.572, ...), custom_call_target="tpu_custom_call" | custom-call | flops 10737418240 | bytes 7340032 | tf_op jit(solution)/shard_map/attend_back/pallas_call | solution.py:317
  379.4 14.9 %feed.7 = (f32[256,1024]{1,0:T(8,128)S(1)}, bf16[256,1024]{1,0:T(8,128)(2,1)S(1)}, bf16[256,2816]{1,0:T(8,128)(2,1)S(1)}, bf16[256,2816]{1,0:T(8,128)(2,1)S(1)},...) custom-call(bf16[256,512]{1,0:T(8,128)(2,1)S(1)} %copy-done.39, ...), custom_call_target="tpu_custom_call" | custom-call | flops 4966055936 | bytes 23724032 | tf_op jit(solution)/shard_map/feed/pallas_call | solution.py:443
  394.9 17.3 %feed_back.6 = (bf16[256,2816]{1,0:T(8,128)(2,1)S(1)}, bf16[256,2816]{1,0:T(8,128)(2,1)S(1)}, bf16[256,1024]{1,0:T(8,128)(2,1)S(1)}, f32[256,1024]{1,0:T(8,128)S...) custom-call(f32[256,1024]{1,0:T(8,128)S(1)} %convert_multiply_fusion, ...), custom_call_target="tpu_custom_call" | custom-call | flops 4966055936 | bytes 25165824 | tf_op jit(solution)/shard_map/feed_back/pallas_call | solution.py:560
  450.5 13.9 %collective-permute-done.22 = bf16[1,4,256,256]{3,2,1,0:T(8,128)(2,1)S(1)} collective-permute-done((bf16[1,4,256,256]{3,2,1,0:T(8,128)(2,1)S(1)}, bf16[1,4,256,256]{3,2,1,0:T(8,128)(2,1)S(1)}, u32[]{:S(2)}, u32[]{:S(2)}) %collective-permute-start.22) | collective-permute-done | bytes 524320 | tf_op jit(solution)/shard_map/ppermute | solution.py:779
  464.7 21.6 %collective-permute-done.26 = bf16[1,4,256,256]{3,2,1,0:T(8,128)(2,1)S(1)} collective-permute-done((bf16[1,4,256,256]{3,2,1,0:T(8,128)(2,1)S(1)}, bf16[1,4,256,256]{3,2,1,0:T(8,128)(2,1)S(1)}, u32[]{:S(2)}, u32[]{:S(2)}) %collective-permute-start.26) | collective-permute-done | bytes 524320 | tf_op jit(solution)/shard_map/ppermute | solution.py:779
  495.9 16.9 %collective-permute-done.27 = bf16[1,2,256,256]{3,2,1,0:T(8,128)(2,1)S(1)} collective-permute-done((bf16[1,2,256,256]{3,2,1,0:T(8,128)(2,1)S(1)}, bf16[1,2,256,256]{3,2,1,0:T(8,128)(2,1)S(1)}, u32[]{:S(2)}, u32[]{:S(2)}) %collective-permute-start.27) | collective-permute-done | bytes 262176 | tf_op jit(solution)/shard_map/ppermute | solution.py:779
  536.5 17.2 %feed_back.5 = (bf16[256,2816]{1,0:T(8,128)(2,1)S(1)}, bf16[256,2816]{1,0:T(8,128)(2,1)S(1)}, bf16[256,1024]{1,0:T(8,128)(2,1)S(1)}, f32[256,1024]{1,0:T(8,128)S...) custom-call(f32[256,1024]{1,0:T(8,128)S(1)} %get-tuple-element.263.g, ...), custom_call_target="tpu_custom_call" | custom-call | flops 4966055936 | bytes 25165824 | tf_op jit(solution)/shard_map/feed_back/pallas_call | solution.py:560
  561.0 21.8 %attend_back.7 = (bf16[1,2,128,512]{3,2,1,0:T(8,128)(2,1)S(1)}, bf16[1,16,256,256]{3,2,1,0:T(8,128)(2,1)}, f32[512,256]{1,0:T(8,128)S(1)}, f32[512,256]{1,0:T(8,128)S(1)}) custom-call(s32[4]{0:T(128)S(1)} %pad_add_fusion.scalars, bf16[1,2,1024,128]{3,2,1,0:T(8,128)(2,1)S(1)} %copy-done.81, bf16[1,2,1024,128]{3,2,1,0:T(8,128)(2,1)S(1)} %bitcast.573, ...), custom_call_target="tpu_custom_call" | custom-call | flops 10737418240 | bytes 7340032 | tf_op jit(solution)/shard_map/attend_back/pallas_call | solution.py:317
  587.4 22.1 %attend_back.6 = (bf16[1,2,128,512]{3,2,1,0:T(8,128)(2,1)S(1)}, bf16[1,16,256,256]{3,2,1,0:T(8,128)(2,1)}, f32[512,256]{1,0:T(8,128)S(1)}, f32[512,256]{1,0:T(8,128)S(1)}) custom-call(s32[4]{0:T(128)S(1)} %pad_add_fusion.scalars, bf16[1,2,1024,128]{3,2,1,0:T(8,128)(2,1)S(1)} %copy-done.82, bf16[1,2,1024,128]{3,2,1,0:T(8,128)(2,1)S(1)} %bitcast.574, ...), custom_call_target="tpu_custom_call" | custom-call | flops 10737418240 | bytes 7340032 | tf_op jit(solution)/shard_map/attend_back/pallas_call | solution.py:317
  615.7 17.7 %feed_back.7 = (bf16[256,2816]{1,0:T(8,128)(2,1)S(1)}, bf16[256,2816]{1,0:T(8,128)(2,1)S(1)}, bf16[256,1024]{1,0:T(8,128)(2,1)S(1)}, f32[256,1024]{1,0:T(8,128)}...) custom-call(f32[256,1024]{1,0:T(8,128)S(1)} %get-tuple-element.262.g, ...), custom_call_target="tpu_custom_call" | custom-call | flops 4966055936 | bytes 25165824 | tf_op jit(solution)/shard_map/feed_back/pallas_call | solution.py:560
  677.3 13.3 %collective-permute-done.30 = bf16[1,4,256,256]{3,2,1,0:T(8,128)(2,1)S(1)} collective-permute-done((bf16[1,4,256,256]{3,2,1,0:T(8,128)(2,1)S(1)}, bf16[1,4,256,256]{3,2,1,0:T(8,128)(2,1)S(1)}, u32[]{:S(2)}, u32[]{:S(2)}) %collective-permute-start.30) | collective-permute-done | bytes 524320 | tf_op jit(solution)/shard_map/ppermute | solution.py:779
  691.2 21.9 %collective-permute-done.34 = bf16[1,4,256,256]{3,2,1,0:T(8,128)(2,1)S(1)} collective-permute-done((bf16[1,4,256,256]{3,2,1,0:T(8,128)(2,1)S(1)}, bf16[1,4,256,256]{3,2,1,0:T(8,128)(2,1)S(1)}, u32[]{:S(2)}, u32[]{:S(2)}) %collective-permute-start.34) | collective-permute-done | bytes 524320 | tf_op jit(solution)/shard_map/ppermute | solution.py:779
  721.4 16.4 %collective-permute-done.35 = bf16[1,2,256,256]{3,2,1,0:T(8,128)(2,1)S(1)} collective-permute-done((bf16[1,2,256,256]{3,2,1,0:T(8,128)(2,1)S(1)}, bf16[1,2,256,256]{3,2,1,0:T(8,128)(2,1)S(1)}, u32[]{:S(2)}, u32[]{:S(2)}) %collective-permute-start.35) | collective-permute-done | bytes 262176 | tf_op jit(solution)/shard_map/ppermute | solution.py:779
  (674 shorter events, 383.3 us)
Async XLA Ops:
  7.2 786.8 %reduce-scatter.5.cloned.1.call-start = ((), (), s32[]{:S(2)}) async-start(), calls=%async_computation.3 | async-start | bytes 10305536 | tf_op jit(solution)/shard_map/reduce_scatter | solution.py:971
  16.8 75.7 %collective-permute-start.42 = (bf16[1,128,1024]{2,1,0:T(8,128)(2,1)}, bf16[1,128,1024]{2,1,0:T(8,128)(2,1)}, u32[]{:S(2)}, u32[]{:S(2)}) collective-permute-start(bf16[1,128,1024]{2,1,0:T(8,128)(2,1)} %get-tuple-element.228), channel_id=1, source_target_pairs={{0,30},{2,28},{4,26},{6,24},{8,22},{10,20},{12,18},{14,16},{16,14}... | collective-permute-start | bytes 786440 | tf_op jit(solution)/shard_map/ppermute | solution.py:773
  22.0 87.3 %collective-permute-start.19 = (bf16[1,128,1024]{2,1,0:T(8,128)(2,1)}, bf16[1,128,1024]{2,1,0:T(8,128)(2,1)}, u32[]{:S(2)}, u32[]{:S(2)}) collective-permute-start(bf16[1,128,1024]{2,1,0:T(8,128)(2,1)} %get-tuple-element.236), channel_id=1, source_target_pairs={{0,30},{2,28},{4,26},{6,24},{8,22},{10,20},{12,18},{14,16},{16,14}... | collective-permute-start | bytes 786440 | tf_op jit(solution)/shard_map/ppermute | solution.py:773
  47.6 29.6 %collective-permute-start.5 = (bf16[1,1,256,256]{3,2,1,0:T(8,128)(2,1)S(1)}, bf16[1,1,256,256]{3,2,1,0:T(8,128)(2,1)S(1)}, u32[]{:S(2)}, u32[]{:S(2)}) collective-permute-start(bf16[1,1,256,256]{3,2,1,0:T(8,128)(2,1)S(1)} %bitcast.652), channel_id=1, source_target_pairs={{0,16},{2,18},{4,20},{6,22},{8,24},{10,26},{12,28},{14,30},{16,0},... | collective-permute-start | bytes 393224 | tf_op jit(solution)/shard_map/ppermute | solution.py:779
  131.9 81.4 %collective-permute-start.47 = (bf16[256,512]{1,0:T(8,128)(2,1)S(1)}, bf16[256,512]{1,0:T(8,128)(2,1)S(1)}, u32[]{:S(2)}, u32[]{:S(2)}) collective-permute-start(bf16[256,512]{1,0:T(8,128)(2,1)S(1)} %bitcast.536), channel_id=1, source_target_pairs={{0,1},{1,0},{2,3},{3,2},{4,5},{5,4},{6,7},{7,6},{8,9},{9,8},{10,11... | collective-permute-start | bytes 786440 | tf_op jit(solution)/shard_map/ppermute | solution.py:776
  149.0 64.3 %collective-permute-start.46 = (bf16[256,512]{1,0:T(8,128)(2,1)S(1)}, bf16[256,512]{1,0:T(8,128)(2,1)S(1)}, u32[]{:S(2)}, u32[]{:S(2)}) collective-permute-start(bf16[256,512]{1,0:T(8,128)(2,1)S(1)} %bitcast.539), channel_id=1, source_target_pairs={{0,1},{1,0},{2,3},{3,2},{4,5},{5,4},{6,7},{7,6},{8,9},{9,8},{10,11... | collective-permute-start | bytes 786440 | tf_op jit(solution)/shard_map/ppermute | solution.py:776
  249.5 124.6 %collective-permute-start.45 = (bf16[256,512]{1,0:T(8,128)(2,1)S(1)}, bf16[256,512]{1,0:T(8,128)(2,1)S(1)}, u32[]{:S(2)}, u32[]{:S(2)}) collective-permute-start(bf16[256,512]{1,0:T(8,128)(2,1)S(1)} %bitcast.542), channel_id=1, source_target_pairs={{0,1},{1,0},{2,3},{3,2},{4,5},{5,4},{6,7},{7,6},{8,9},{9,8},{10,11... | collective-permute-start | bytes 786440 | tf_op jit(solution)/shard_map/ppermute | solution.py:776
  265.3 111.0 %collective-permute-start.44 = (bf16[256,512]{1,0:T(8,128)(2,1)S(1)}, bf16[256,512]{1,0:T(8,128)(2,1)S(1)}, u32[]{:S(2)}, u32[]{:S(2)}) collective-permute-start(bf16[256,512]{1,0:T(8,128)(2,1)S(1)} %bitcast.545), channel_id=1, source_target_pairs={{0,1},{1,0},{2,3},{3,2},{4,5},{5,4},{6,7},{7,6},{8,9},{9,8},{10,11... | collective-permute-start | bytes 786440 | tf_op jit(solution)/shard_map/ppermute | solution.py:776
  333.9 95.1 %collective-permute-start.50 = (bf16[256,512]{1,0:T(8,128)(2,1)}, bf16[256,512]{1,0:T(8,128)(2,1)}, u32[]{:S(2)}, u32[]{:S(2)}) collective-permute-start(bf16[256,512]{1,0:T(8,128)(2,1)} %bitcast.122.refs_3_), channel_id=1, source_target_pairs={{0,1},{1,0},{2,3},{3,2},{4,5},{5,4},{6,7},{7,6},{8,9},{9,8},{10,11... | collective-permute-start | bytes 786440 | tf_op jit(solution)/shard_map/ppermute | solution.py:776
  360.3 72.9 %collective-permute-start.48 = (bf16[256,512]{1,0:T(8,128)(2,1)}, bf16[256,512]{1,0:T(8,128)(2,1)}, u32[]{:S(2)}, u32[]{:S(2)}) collective-permute-start(bf16[256,512]{1,0:T(8,128)(2,1)} %bitcast.107.refs_2_), channel_id=1, source_target_pairs={{0,1},{1,0},{2,3},{3,2},{4,5},{5,4},{6,7},{7,6},{8,9},{9,8},{10,11... | collective-permute-start | bytes 786440 | tf_op jit(solution)/shard_map/ppermute | solution.py:776
  364.6 63.0 %collective-permute-start.17 = (bf16[1,128,1024]{2,1,0:T(8,128)(2,1)}, bf16[1,128,1024]{2,1,0:T(8,128)(2,1)}, u32[]{:S(2)}, u32[]{:S(2)}) collective-permute-start(bf16[1,128,1024]{2,1,0:T(8,128)(2,1)} %get-tuple-element.240), channel_id=1, source_target_pairs={{0,30},{2,28},{4,26},{6,24},{8,22},{10,20},{12,18},{14,16},{16,14}... | collective-permute-start | bytes 786440 | tf_op jit(solution)/shard_map/ppermute | solution.py:773
  374.7 56.6 %collective-permute-start.67 = (bf16[16,64,256]{2,1,0:T(8,128)(2,1)}, bf16[16,64,256]{2,1,0:T(8,128)(2,1)}, u32[]{:S(2)}, u32[]{:S(2)}) collective-permute-start(bf16[16,64,256]{2,1,0:T(8,128)(2,1)} %fusion.123), channel_id=1, source_target_pairs={{0,1},{1,0},{2,3},{3,2},{4,5},{5,4},{6,7},{7,6},{8,9},{9,8},{10,11... | collective-permute-start | bytes 1572872 | tf_op jit(solution)/shard_map/ppermute | solution.py:776
  377.1 67.5 %collective-permute-start.21 = (bf16[1,8,256,256]{3,2,1,0:T(8,128)(2,1)}, bf16[1,8,256,256]{3,2,1,0:T(8,128)(2,1)}, u32[]{:S(2)}, u32[]{:S(2)}) collective-permute-start(bf16[1,8,256,256]{3,2,1,0:T(8,128)(2,1)} %slice_bitcast_fusion.6), channel_id=1, source_target_pairs={{0,2},{2,0},{4,6},{6,4},{8,10},{10,8},{12,14},{14,12},{16,18},{18,... | collective-permute-start | bytes 3145736 | tf_op jit(solution)/shard_map/ppermute | solution.py:779
  427.1 368.2 %reduce-scatter.3.cloned.1.call-start = ((), (), s32[]{:S(2)}) async-start(), calls=%async_computation.2 | async-start | bytes 10305536 | tf_op jit(solution)/shard_map/reduce_scatter | solution.py:971
  448.2 38.2 %collective-permute-start.26 = (bf16[1,4,256,256]{3,2,1,0:T(8,128)(2,1)S(1)}, bf16[1,4,256,256]{3,2,1,0:T(8,128)(2,1)S(1)}, u32[]{:S(2)}, u32[]{:S(2)}) collective-permute-start(bf16[1,4,256,256]{3,2,1,0:T(8,128)(2,1)S(1)} %slice_bitcast_fusion.14), channel_id=1, source_target_pairs={{0,4},{2,6},{4,0},{6,2},{8,12},{10,14},{12,8},{14,10},{16,20},{18,... | collective-permute-start | bytes 1572872 | tf_op jit(solution)/shard_map/ppermute | solution.py:779
  450.0 43.4 %collective-permute-start.69 = (bf16[128,1536]{1,0:T(8,128)(2,1)S(1)}, bf16[128,1536]{1,0:T(8,128)(2,1)S(1)}, u32[]{:S(2)}, u32[]{:S(2)}) collective-permute-start(bf16[128,1536]{1,0:T(8,128)(2,1)S(1)} %get-tuple-element.208), channel_id=1, source_target_pairs={{0,4},{2,6},{4,0},{6,2},{8,12},{10,14},{12,8},{14,10},{16,20},{18,... | collective-permute-start | bytes 1179656 | tf_op jit(solution)/shard_map/ppermute | solution.py:779
  464.7 28.9 %collective-permute-start.23 = (bf16[1,2,256,256]{3,2,1,0:T(8,128)(2,1)S(1)}, bf16[1,2,256,256]{3,2,1,0:T(8,128)(2,1)S(1)}, u32[]{:S(2)}, u32[]{:S(2)}) collective-permute-start(bf16[1,2,256,256]{3,2,1,0:T(8,128)(2,1)S(1)} %slice_bitcast_fusion.30), channel_id=1, source_target_pairs={{0,8},{2,10},{4,12},{6,14},{8,0},{10,2},{12,4},{14,6},{16,24},{18,... | collective-permute-start | bytes 786440 | tf_op jit(solution)/shard_map/ppermute | solution.py:779
  533.2 121.4 %collective-permute-start.58 = (bf16[256,640]{1,0:T(8,128)(2,1)}, bf16[256,640]{1,0:T(8,128)(2,1)}, u32[]{:S(2)}, u32[]{:S(2)}) collective-permute-start(bf16[256,640]{1,0:T(8,128)(2,1)} %slice.646), channel_id=1, source_target_pairs={{0,2},{2,0},{4,6},{6,4},{8,10},{10,8},{12,14},{14,12},{16,18},{18,... | collective-permute-start | bytes 983048 | tf_op jit(solution)/shard_map/ppermute | solution.py:779
  582.8 73.4 %collective-permute-start.53 = (bf16[256,512]{1,0:T(8,128)(2,1)S(1)}, bf16[256,512]{1,0:T(8,128)(2,1)S(1)}, u32[]{:S(2)}, u32[]{:S(2)}) collective-permute-start(bf16[256,512]{1,0:T(8,128)(2,1)S(1)} %bitcast.548), channel_id=1, source_target_pairs={{0,1},{1,0},{2,3},{3,2},{4,5},{5,4},{6,7},{7,6},{8,9},{9,8},{10,11... | collective-permute-start | bytes 786440 | tf_op jit(solution)/shard_map/ppermute | solution.py:776
  610.3 57.3 %collective-permute-start.52 = (bf16[256,512]{1,0:T(8,128)(2,1)S(1)}, bf16[256,512]{1,0:T(8,128)(2,1)S(1)}, u32[]{:S(2)}, u32[]{:S(2)}) collective-permute-start(bf16[256,512]{1,0:T(8,128)(2,1)S(1)} %bitcast.551), channel_id=1, source_target_pairs={{0,1},{1,0},{2,3},{3,2},{4,5},{5,4},{6,7},{7,6},{8,9},{9,8},{10,11... | collective-permute-start | bytes 786440 | tf_op jit(solution)/shard_map/ppermute | solution.py:776
  612.6 51.0 %collective-permute-start.62 = (bf16[16,64,256]{2,1,0:T(8,128)(2,1)}, bf16[16,64,256]{2,1,0:T(8,128)(2,1)}, u32[]{:S(2)}, u32[]{:S(2)}) collective-permute-start(bf16[16,64,256]{2,1,0:T(8,128)(2,1)} %fusion.122), channel_id=1, source_target_pairs={{0,1},{1,0},{2,3},{3,2},{4,5},{5,4},{6,7},{7,6},{8,9},{9,8},{10,11... | collective-permute-start | bytes 1572872 | tf_op jit(solution)/shard_map/ppermute | solution.py:776
  615.7 56.6 %collective-permute-start.29 = (bf16[1,8,256,256]{3,2,1,0:T(8,128)(2,1)}, bf16[1,8,256,256]{3,2,1,0:T(8,128)(2,1)}, u32[]{:S(2)}, u32[]{:S(2)}) collective-permute-start(bf16[1,8,256,256]{3,2,1,0:T(8,128)(2,1)} %slice_bitcast_fusion.2), channel_id=1, source_target_pairs={{0,2},{2,0},{4,6},{6,4},{8,10},{10,8},{12,14},{14,12},{16,18},{18,... | collective-permute-start | bytes 3145736 | tf_op jit(solution)/shard_map/ppermute | solution.py:779
  674.9 38.1 %collective-permute-start.34 = (bf16[1,4,256,256]{3,2,1,0:T(8,128)(2,1)S(1)}, bf16[1,4,256,256]{3,2,1,0:T(8,128)(2,1)S(1)}, u32[]{:S(2)}, u32[]{:S(2)}) collective-permute-start(bf16[1,4,256,256]{3,2,1,0:T(8,128)(2,1)S(1)} %slice_bitcast_fusion.10), channel_id=1, source_target_pairs={{0,4},{2,6},{4,0},{6,2},{8,12},{10,14},{12,8},{14,10},{16,20},{18,... | collective-permute-start | bytes 1572872 | tf_op jit(solution)/shard_map/ppermute | solution.py:779
  677.0 40.8 %collective-permute-start.64 = (bf16[128,1536]{1,0:T(8,128)(2,1)S(1)}, bf16[128,1536]{1,0:T(8,128)(2,1)S(1)}, u32[]{:S(2)}, u32[]{:S(2)}) collective-permute-start(bf16[128,1536]{1,0:T(8,128)(2,1)S(1)} %get-tuple-element.206), channel_id=1, source_target_pairs={{0,4},{2,6},{4,0},{6,2},{8,12},{10,14},{12,8},{14,10},{16,20},{18,... | collective-permute-start | bytes 1179656 | tf_op jit(solution)/shard_map/ppermute | solution.py:779
  (199 other events, 2299.8 us)
Sparse Core Ops, SparseCore 0:
  427.2 133.2 reduce-scatter.4
  654.6 136.1 reduce-scatter.2

commit v3 on v2

v3 whole, which is shorter than its diff:
```python
import functools

import jax
import jax.numpy as jnp
from jax import lax
from jax.experimental import pallas as pl
from jax.experimental.pallas import tpu as pltpu
from jax.sharding import PartitionSpec as P

HD = 64
LAYERS = 2
GROUPS = 2
NEG_FILL = -1e30
LOG2E = 1.4426950408889634
ATT_SCALE = HD ** (-0.5)
NT = (((1,), (1,)), ((), ()))
TN = (((0,), (0,)), ((), ()))
F32 = jnp.float32
BF16 = jnp.bfloat16
KEY_BLOCK = 512
QUERY_BLOCK = 1024
FEED_STEP, FEED_AHEAD = 768, 16
BACK_STEP, BACK_AHEAD = 1408, 6


def dot_as(left, right, dims):
    return lax.dot_general(left, right, dims, preferred_element_type=F32)


def dot(left, right):
    return jnp.dot(left, right, preferred_element_type=F32)


def order_keys(scalars, lat_ref, keys, keys_t, seq_count, half):
    for piece in range(2 * seq_count):
        slot = scalars[2 + piece]
        keys[pl.ds(piece * half, half), :] = lat_ref[0, slot, pl.ds((piece % 2) * half, half), :]
    for first in range(0, 2 * seq_count * half, 256):
        keys_t[:, first : first + 256] = keys[first : first + 256, :].T


def block_bounds(scalars, row, part, half, seq_count):
    first = scalars[part]
    cut = scalars[2 + 2 * seq_count + row]
    last = first + half - 1
    low_min = jnp.where(first >= cut, cut, 0)
    low_max = jnp.where(last >= cut, cut, 0)
    return first, cut, low_min // KEY_BLOCK, last // KEY_BLOCK + 1, low_max


def hide(scores, block_at, first, cut, half):
    lanes = lax.broadcasted_iota(jnp.int32, (1, scores.shape[1]), 1)
    query_at = first + lanes % half
    low = jnp.where(query_at >= cut, cut, 0)
    key_at = block_at * KEY_BLOCK + lax.broadcasted_iota(jnp.int32, scores.shape, 0)
    return jnp.where((key_at <= query_at) & (key_at >= low), scores, NEG_FILL)


def over_blocks(bounds, block):
    first, _, start, stop, low_max = bounds

    def body(block_at, carry):
        edge = (block_at * KEY_BLOCK + KEY_BLOCK - 1 > first) | (block_at * KEY_BLOCK < low_max)

        @pl.when(edge)
        def _():
            block(block_at, True)

        @pl.when(jnp.logical_not(edge))
        def _():
            block(block_at, False)

        return carry

    lax.fori_loop(start, stop, body, 0)


def attend_kernel(
    scalars,
    q_ref,
    lat_ref,
    up_k_ref,
    up_v_ref,
    *refs,
    seq_count,
    half,
    heads,
):
    out_ref, out_t_ref, log_ref, query_ref, mixed_ref, keys, keys_t, top, total, acc = refs[-10:]
    row, part = pl.program_id(0), pl.program_id(1)

    @pl.when(part == 0)
    def _():
        order_keys(scalars, lat_ref, keys, keys_t, seq_count, half)

    for head in range(heads):
        feats = slice(head * HD, (head + 1) * HD)
        lifted = dot_as(q_ref[0, 0, feats, :], up_k_ref[feats, :], TN)
        query_ref[0, 0, head * half : (head + 1) * half, :] = (lifted * (LOG2E * ATT_SCALE)).astype(
            BF16
        )
    top[...] = jnp.full_like(top, NEG_FILL)
    total[...] = jnp.zeros_like(total)
    acc[...] = jnp.zeros_like(acc)
    bounds = block_bounds(scalars, row, part, half, seq_count)
    columns = heads * half
    width = min(QUERY_BLOCK, columns)

    def block(block_at, edge):
        at = pl.multiple_of(block_at * KEY_BLOCK, KEY_BLOCK)
        key_rows = keys[pl.ds(at, KEY_BLOCK), :]
        key_cols = keys_t[:, pl.ds(at, KEY_BLOCK)]
        for col in range(0, columns, width):
            cols = slice(col, col + width)
            scores = dot_as(key_rows, query_ref[0, 0, cols, :], NT)
            if edge:
                scores = hide(scores, block_at, bounds[0], bounds[1], half)
            old_top = top[:, cols]
            new_top = jnp.maximum(old_top, jnp.max(scores, axis=0, keepdims=True))
            probs = jnp.exp2(scores - new_top)
            fade = jnp.exp2(old_top - new_top)
            total[:, cols] = total[:, cols] * fade + jnp.sum(probs, axis=0, keepdims=True)
            top[:, cols] = new_top
            acc[:, cols] = acc[:, cols] * fade + dot(key_cols, probs.astype(BF16))

    over_blocks(bounds, block)
    mixed_ref[0, 0, :, :] = (acc[...] * (1.0 / total[...])).astype(BF16)
    log_ref[0, 0, :, :] = top[...] + jnp.log2(total[...])
    for head in range(heads):
        feats = slice(head * HD, (head + 1) * HD)
        out_t = dot(
            up_v_ref[feats, :], mixed_ref[0, 0, :, head * half : (head + 1) * half]
        ).astype(BF16)
        out_t_ref[0, 0, feats, :] = out_t
        out_ref[0, 0, :, feats] = out_t.T


def attend_back_kernel(
    scalars,
    q_ref,
    d_out_ref,
    out_ref,
    lat_ref,
    up_k_ref,
    up_v_ref,
    query_ref,
    mixed_ref,
    log_ref,
    *refs,
    seq_count,
    half,
    heads,
):
    dq_ref, d_lat_ref, d_up_k_ref, d_up_v_ref = refs[-11:-7]
    keys, keys_t, d_keys, query_plain, d_mixed, delta, d_query = refs[-7:]
    row, part = pl.program_id(0), pl.program_id(1)

    @pl.when(part == 0)
    def _():
        order_keys(scalars, lat_ref, keys, keys_t, seq_count, half)
        d_keys[...] = jnp.zeros_like(d_keys)

    @pl.when((part == 0) & (row == 0))
    def _():
        d_up_k_ref[...] = jnp.zeros_like(d_up_k_ref)
        d_up_v_ref[...] = jnp.zeros_like(d_up_v_ref)

    for head in range(heads):
        feats = slice(head * HD, (head + 1) * HD)
        cols = slice(head * half, (head + 1) * half)
        d_out = d_out_ref[0, 0, feats, :]
        query_plain[cols, :] = (
            dot_as(q_ref[0, 0, feats, :], up_k_ref[feats, :], TN) * ATT_SCALE
        ).astype(BF16)
        d_mixed[cols, :] = dot_as(d_out, up_v_ref[feats, :], TN).astype(BF16)
        delta[:, cols] = jnp.sum(
            d_out.astype(F32) * out_ref[0, 0, feats, :].astype(F32), axis=0, keepdims=True
        )
    d_query[...] = jnp.zeros_like(d_query)
    bounds = block_bounds(scalars, row, part, half, seq_count)
    columns = heads * half
    width = min(QUERY_BLOCK, columns)

    def block(block_at, edge):
        at = pl.multiple_of(block_at * KEY_BLOCK, KEY_BLOCK)
        key_rows = keys[pl.ds(at, KEY_BLOCK), :]
        key_cols = keys_t[:, pl.ds(at, KEY_BLOCK)]
        key_total = d_keys[pl.ds(at, KEY_BLOCK), :]
        for col in range(0, columns, width):
            cols = slice(col, col + width)
            scores = dot_as(key_rows, query_ref[0, 0, cols, :], NT)
            if edge:
                scores = hide(scores, block_at, bounds[0], bounds[1], half)
            probs = jnp.exp2(scores - log_ref[0, 0, :, cols])
            d_probs = dot_as(key_rows, d_mixed[cols, :], NT)
            d_scores = (probs * (d_probs - delta[:, cols])).astype(BF16)
            key_total = key_total + (
                dot(d_scores, query_plain[cols, :]) + dot(probs.astype(BF16), d_mixed[cols, :])
            )
            d_query[:, cols] += dot(key_cols, d_scores)
        d_keys[pl.ds(at, KEY_BLOCK), :] = key_total

    over_blocks(bounds, block)
    for head in range(heads):
        feats = slice(head * HD, (head + 1) * HD)
        cols = slice(head * half, (head + 1) * half)
        d_lifted = (d_query[:, cols] * ATT_SCALE).astype(BF16)
        dq_ref[0, 0, :, feats] = dot(up_k_ref[feats, :], d_lifted).astype(BF16).T
        d_up_k_ref[feats, :] += dot_as(q_ref[0, 0, feats, :], d_lifted, NT)
        d_up_v_ref[feats, :] += dot_as(d_out_ref[0, 0, feats, :], mixed_ref[0, 0, :, cols], NT)

    @pl.when(part == 1)
    def _():
        for piece in range(2 * seq_count):
            slot = scalars[2 + piece]
            d_lat_ref[0, slot, pl.ds((piece % 2) * half, half), :] = d_keys[
                pl.ds(piece * half, half), :
            ].astype(BF16)


def attention_sizes(queries_t, lats):
    rows, _, feats, half = queries_t.shape
    group_feats = feats // GROUPS
    heads = group_feats // HD
    seq_count, size = lats.shape[1], lats.shape[3]
    return rows, half, group_feats, heads, heads * half, seq_count, size, seq_count * 2 * half


def head_spec(group_feats, half, group):
    return pl.BlockSpec((1, 1, group_feats, half), lambda row, part, _: (row, part, group, 0))


def token_spec(group_feats, half, group):
    return pl.BlockSpec((1, 1, half, group_feats), lambda row, part, _: (row, part, 0, group))


def lat_spec(lats):
    return pl.BlockSpec((1,) + lats.shape[1:], lambda row, part, _: (row, 0, 0, 0))


ANY = pl.BlockSpec(memory_space=pl.ANY)


def plain_spec(*block):
    return pl.BlockSpec((1, 1) + block, lambda row, part, _: (row, part, 0, 0))


def up_spec(group_feats, size, at):
    return pl.BlockSpec((group_feats, size), lambda row, part, _: (at, 0))


def in_hbm(value):
    return pltpu.with_memory_space_constraint(value, pltpu.HBM)


def attend(scalars, queries_t, lats, up_t, group, filled):
    rows, half, group_feats, heads, columns, seq_count, size, keys = attention_sizes(
        queries_t, lats
    )
    return pl.pallas_call(
        functools.partial(
            attend_kernel, seq_count=seq_count, half=half, heads=heads
        ),
        grid_spec=pltpu.PrefetchScalarGridSpec(
            num_scalar_prefetch=1,
            grid=(rows, 2),
            in_specs=[
                head_spec(group_feats, half, group),
                lat_spec(lats),
                up_spec(group_feats, size, group),
                up_spec(group_feats, size, GROUPS + group),
            ]
            + [ANY] * len(filled),
            out_specs=[
                token_spec(group_feats, half, group),
                plain_spec(group_feats, half),
                plain_spec(1, columns),
                plain_spec(columns, size),
                plain_spec(size, columns),
            ],
            scratch_shapes=[
                pltpu.VMEM((keys, size), BF16),
                pltpu.VMEM((size, keys), BF16),
                pltpu.VMEM((1, columns), F32),
                pltpu.VMEM((1, columns), F32),
                pltpu.VMEM((size, columns), F32),
            ],
        ),
        out_shape=[
            jax.ShapeDtypeStruct((rows, 2, half, GROUPS * group_feats), BF16),
            pltpu.HBM((rows, 2, group_feats, half), BF16),
            pltpu.HBM((rows, 2, 1, columns), F32),
            pltpu.HBM((rows, 2, columns, size), BF16),
            pltpu.HBM((rows, 2, size, columns), BF16),
        ],
        compiler_params=pltpu.CompilerParams(
            dimension_semantics=("arbitrary", "arbitrary"), vmem_limit_bytes=40 << 20
        ),
        cost_estimate=pl.CostEstimate(
            flops=rows * 2 * columns * keys * size * 2,
            bytes_accessed=rows * (2 * keys * size + 8 * columns * size),
            transcendentals=rows * columns * keys,
        ),
        input_output_aliases={5: 0} if filled else {},
        name="attend",
    )(scalars, queries_t, lats, up_t, up_t, *filled)


def attend_back(
    scalars, queries_t, d_heads_t, heads_t, lats, up_t, kept, group, filled
):
    rows, half, group_feats, heads, columns, seq_count, size, keys = attention_sizes(
        queries_t, lats
    )
    logs, lifted, mixed = kept
    return pl.pallas_call(
        functools.partial(
            attend_back_kernel, seq_count=seq_count, half=half, heads=heads
        ),
        grid_spec=pltpu.PrefetchScalarGridSpec(
            num_scalar_prefetch=1,
            grid=(rows, 2),
            in_specs=[
                head_spec(group_feats, half, group),
                head_spec(group_feats, half, group),
                plain_spec(group_feats, half),
                lat_spec(lats),
                up_spec(group_feats, size, group),
                up_spec(group_feats, size, GROUPS + group),
                plain_spec(columns, size),
                plain_spec(size, columns),
                plain_spec(1, columns),
            ]
            + [ANY] * len(filled),
            out_specs=[
                token_spec(group_feats, half, group),
                lat_spec(lats),
                up_spec(group_feats, size, 0),
                up_spec(group_feats, size, 0),
            ],
            scratch_shapes=[
                pltpu.VMEM((keys, size), BF16),
                pltpu.VMEM((size, keys), BF16),
                pltpu.VMEM((keys, size), F32),
                pltpu.VMEM((columns, size), BF16),
                pltpu.VMEM((columns, size), BF16),
                pltpu.VMEM((1, columns), F32),
                pltpu.VMEM((size, columns), F32),
            ],
        ),
        out_shape=[
            jax.ShapeDtypeStruct((rows, 2, half, GROUPS * group_feats), BF16),
            jax.ShapeDtypeStruct(lats.shape, BF16),
            jax.ShapeDtypeStruct((group_feats, size), F32),
            jax.ShapeDtypeStruct((group_feats, size), F32),
        ],
        compiler_params=pltpu.CompilerParams(
            dimension_semantics=("arbitrary", "arbitrary"), vmem_limit_bytes=48 << 20
        ),
        cost_estimate=pl.CostEstimate(
            flops=rows * 5 * columns * keys * size * 2,
            bytes_accessed=rows * (4 * keys * size + 12 * columns * size),
            transcendentals=rows * columns * keys,
        ),
        input_output_aliases={10: 0} if filled else {},
        name="attend_back",
    )(
        scalars,
        *map(
            in_hbm, (queries_t, d_heads_t, heads_t, lats, up_t, up_t, lifted, mixed, logs)
        ),
        *filled,
    )


def rms_scale(value_rows):
    return lax.rsqrt(jnp.mean(value_rows * value_rows, axis=-1, keepdims=True) + 1e-06)


def norm_back(grad_in, value_rows, scale_rows, gain_vec):
    normed = value_rows * scale_rows
    upstream = grad_in * gain_vec
    return (
        scale_rows * (upstream - normed * jnp.mean(upstream * normed, axis=-1, keepdims=True)),
        jnp.sum(grad_in * normed, axis=0),
    )


def hidden_chunks(hidden, step):
    return [(at, min(step, hidden - at)) for at in range(0, hidden, step)]


class Copies:
    def __init__(self, sems, ahead):
        self.sems, self.made, self.begun, self.done, self.ahead = sems, [], 0, 0, ahead

    def add(self, source, target):
        self.made.append(pltpu.make_async_copy(source, target, self.sems.at[len(self.made)]))

    def begin(self, count):
        while self.begun < min(count, len(self.made)):
            self.made[self.begun].start()
            self.begun += 1

    def need(self, count):
        while self.done < count:
            self.made[self.done].wait()
            self.done += 1
            self.begin(self.done + self.ahead)


def feed_kernel(
    heads,
    state,
    bias,
    gain,
    next_gain,
    w_out,
    w_both,
    w_down,
    hidden_in,
    normed_mlp,
    gate,
    up,
    act,
    following,
    normed_next,
    v_heads,
    v_state,
    v_out,
    v_gate_w,
    v_up_w,
    v_down_w,
    v_normed,
    v_gate,
    v_up,
    v_act,
    v_next,
    v_normed_next,
    in_sems,
    out_sems,
    *,
    layer,
    hidden,
):
    chunks = hidden_chunks(hidden, FEED_STEP)
    loads, stores = Copies(in_sems, FEED_AHEAD), Copies(out_sems, 1)
    loads.add(heads, v_heads)
    loads.add(state, v_state)
    loads.add(w_out.at[layer], v_out)
    for at, count in chunks:
        cols = pl.ds(at, count)
        loads.add(w_both.at[layer, :, cols], v_gate_w.at[:, cols])
        loads.add(w_both.at[layer, :, pl.ds(hidden + at, count)], v_up_w.at[:, cols])
        loads.add(w_down.at[layer, cols, :], v_down_w.at[cols, :])
    loads.begin(FEED_AHEAD)
    loads.need(3)

    def store(source, target):
        stores.add(source, target)
        stores.begin(len(stores.made))

    value = v_state[...] + (dot(v_heads[...], v_out[...]) + bias[0])
    v_state[...] = value
    store(v_state, hidden_in)
    normed = (value * rms_scale(value) * gain[0]).astype(BF16)
    v_normed[...] = normed
    store(v_normed, normed_mlp)
    v_next[...] = value
    needed = 3
    for at, count in chunks:
        cols = pl.ds(at, count)
        loads.need(needed + 2)
        gate_part = dot(v_normed[...], v_gate_w[:, cols])
        up_part = dot(v_normed[...], v_up_w[:, cols])
        act_part = (gate_part * jax.nn.sigmoid(gate_part) * up_part).astype(BF16)
        v_gate[:, cols] = gate_part.astype(BF16)
        v_up[:, cols] = up_part.astype(BF16)
        v_act[:, cols] = act_part
        store(v_gate.at[:, cols], gate.at[:, cols])
        store(v_up.at[:, cols], up.at[:, cols])
        store(v_act.at[:, cols], act.at[:, cols])
        needed += 3
        loads.need(needed)
        v_next[...] += dot(act_part, v_down_w[cols, :])
    value = v_next[...]
    store(v_next, following)
    v_normed_next[...] = (value * rms_scale(value) * next_gain[0]).astype(BF16)
    store(v_normed_next, normed_next)
    stores.need(len(stores.made))


def vector_spec(at, width):
    return pl.BlockSpec((1, 1, width), lambda step: (at, 0, 0))


def feed(state, heads, layer, next_layer, weights):
    out_weight, out_bias, mlp_gain, attn_gain, gate_up_matrix, down_matrix = weights
    toks, width = state.shape
    hidden = down_matrix.shape[1]
    count = len(hidden_chunks(hidden, FEED_STEP))
    wide = lambda dtype: jax.ShapeDtypeStruct((toks, width), dtype)
    tiled = jax.ShapeDtypeStruct((toks, hidden), BF16)
    return pl.pallas_call(
        functools.partial(feed_kernel, layer=layer, hidden=hidden),
        grid=(1,),
        in_specs=[ANY] * 2
        + [vector_spec(layer, width), vector_spec(layer, width), vector_spec(next_layer, width)]
        + [ANY] * 3,
        out_specs=[ANY] * 7,
        out_shape=[wide(F32), wide(BF16), tiled, tiled, tiled, wide(F32), wide(BF16)],
        scratch_shapes=[
            pltpu.VMEM(heads.shape, BF16),
            pltpu.VMEM((toks, width), F32),
            pltpu.VMEM(out_weight.shape[1:], BF16),
            pltpu.VMEM((width, hidden), BF16),
            pltpu.VMEM((width, hidden), BF16),
            pltpu.VMEM((hidden, width), BF16),
            pltpu.VMEM((toks, width), BF16),
            pltpu.VMEM((toks, hidden), BF16),
            pltpu.VMEM((toks, hidden), BF16),
            pltpu.VMEM((toks, hidden), BF16),
            pltpu.VMEM((toks, width), F32),
            pltpu.VMEM((toks, width), BF16),
            pltpu.SemaphoreType.DMA((3 + 3 * count,)),
            pltpu.SemaphoreType.DMA((4 + 3 * count,)),
        ],
        compiler_params=pltpu.CompilerParams(
            dimension_semantics=("arbitrary",), vmem_limit_bytes=40 << 20
        ),
        cost_estimate=pl.CostEstimate(
            flops=2 * toks * width * (3 * hidden + width),
            bytes_accessed=2 * width * (3 * hidden + width) + 6 * toks * hidden,
            transcendentals=toks * hidden,
        ),
        name="feed",
    )(
        heads,
        state,
        out_bias[:, None],
        mlp_gain[:, None],
        attn_gain[:, None],
        out_weight,
        gate_up_matrix,
        down_matrix,
    )


def feed_back_kernel(
    grad,
    hidden_in,
    gain,
    gate,
    up,
    w_out,
    w_both,
    w_down,
    d_gate,
    d_up,
    d_mlp,
    d_hidden_in,
    d_attn,
    d_heads_t,
    gain_sum,
    bias_sum,
    v_grad,
    v_hidden_in,
    v_gate,
    v_up,
    v_out,
    v_gate_w,
    v_up_w,
    v_down_w,
    v_d_mlp,
    v_d_attn,
    v_d_heads,
    acc,
    in_sems,
    out_sems,
    *,
    layer,
    hidden,
    half,
):
    chunks = hidden_chunks(hidden, BACK_STEP)
    loads, stores = Copies(in_sems, BACK_AHEAD), Copies(out_sems, 1)
    loads.add(grad, v_grad)
    for at, count in chunks:
        cols = pl.ds(at, count)
        loads.add(gate.at[:, cols], v_gate.at[:, cols])
        loads.add(up.at[:, cols], v_up.at[:, cols])
        loads.add(w_down.at[layer, cols, :], v_down_w.at[cols, :])
        loads.add(w_both.at[layer, :, cols], v_gate_w.at[:, cols])
        loads.add(w_both.at[layer, :, pl.ds(hidden + at, count)], v_up_w.at[:, cols])
    loads.add(hidden_in, v_hidden_in)
    loads.add(w_out.at[layer], v_out)
    loads.begin(BACK_AHEAD)
    loads.need(1)

    def store(source, target):
        stores.add(source, target)
        stores.begin(len(stores.made))

    v_d_mlp[...] = v_grad[...].astype(BF16)
    store(v_d_mlp, d_mlp)
    needed = 1
    for at, count in chunks:
        cols = pl.ds(at, count)
        loads.need(needed + 3)
        d_act = dot_as(v_d_mlp[...], v_down_w[cols, :], NT)
        gate_part = v_gate[:, cols].astype(F32)
        up_part = v_up[:, cols].astype(F32)
        sig_gate = jax.nn.sigmoid(gate_part)
        d_gate_part = (d_act * up_part * sig_gate * (1.0 + gate_part * (1.0 - sig_gate))).astype(
            BF16
        )
        d_up_part = (d_act * gate_part * sig_gate).astype(BF16)
        v_gate[:, cols] = d_gate_part
        v_up[:, cols] = d_up_part
        store(v_gate.at[:, cols], d_gate.at[:, cols])
        store(v_up.at[:, cols], d_up.at[:, cols])
        needed += 5
        loads.need(needed)
        part = dot_as(d_gate_part, v_gate_w[:, cols], NT) + dot_as(d_up_part, v_up_w[:, cols], NT)
        if at == 0:
            acc[...] = part
        else:
            acc[...] += part
    loads.need(needed + 1)
    value = v_hidden_in[...]
    d_norm, gain_terms = norm_back(acc[...], value, rms_scale(value), gain[0])
    gain_sum[...] = gain_terms[None]
    total = v_grad[...] + d_norm
    low = total.astype(BF16)
    v_grad[...] = total
    store(v_grad, d_hidden_in)
    v_d_attn[...] = low
    store(v_d_attn, d_attn)
    bias_sum[...] = jnp.sum(low.astype(F32), axis=0, keepdims=True)
    loads.need(needed + 2)
    for piece in range(d_heads_t.shape[0]):
        v_d_heads[piece] = dot_as(v_out[...], low[piece * half : (piece + 1) * half], NT).astype(
            BF16
        )
    store(v_d_heads, d_heads_t)
    stores.need(len(stores.made))


def feed_back(grad, hidden_in, gate, up, layer, half, weights):
    out_weight, _, mlp_gain, _, gate_up_matrix, down_matrix = weights
    toks, width = grad.shape
    heads_dim = out_weight.shape[1]
    hidden = down_matrix.shape[1]
    vector_out = pl.BlockSpec((1, width), lambda step: (0, 0))
    wide = lambda dtype: jax.ShapeDtypeStruct((toks, width), dtype)
    tiled = jax.ShapeDtypeStruct((toks, hidden), BF16)
    pieces = toks // half
    count = len(hidden_chunks(hidden, BACK_STEP))
    return pl.pallas_call(
        functools.partial(feed_back_kernel, layer=layer, hidden=hidden, half=half),
        grid=(1,),
        in_specs=[ANY, ANY, vector_spec(layer, width)] + [ANY] * 5,
        out_specs=[ANY] * 6 + [vector_out] * 2,
        out_shape=[
            tiled,
            tiled,
            wide(BF16),
            wide(F32),
            wide(BF16),
            jax.ShapeDtypeStruct((pieces, heads_dim, half), BF16),
            jax.ShapeDtypeStruct((1, width), F32),
            jax.ShapeDtypeStruct((1, width), F32),
        ],
        scratch_shapes=[
            pltpu.VMEM((toks, width), F32),
            pltpu.VMEM((toks, width), F32),
            pltpu.VMEM((toks, hidden), BF16),
            pltpu.VMEM((toks, hidden), BF16),
            pltpu.VMEM(out_weight.shape[1:], BF16),
            pltpu.VMEM((width, hidden), BF16),
            pltpu.VMEM((width, hidden), BF16),
            pltpu.VMEM((hidden, width), BF16),
            pltpu.VMEM((toks, width), BF16),
            pltpu.VMEM((toks, width), BF16),
            pltpu.VMEM((pieces, heads_dim, half), BF16),
            pltpu.VMEM((toks, width), F32),
            pltpu.SemaphoreType.DMA((3 + 5 * count,)),
            pltpu.SemaphoreType.DMA((4 + 2 * count,)),
        ],
        compiler_params=pltpu.CompilerParams(
            dimension_semantics=("arbitrary",), vmem_limit_bytes=40 << 20
        ),
        cost_estimate=pl.CostEstimate(
            flops=2 * toks * width * (3 * hidden + heads_dim),
            bytes_accessed=2 * width * (3 * hidden + heads_dim) + 8 * toks * hidden,
            transcendentals=toks * hidden,
        ),
        name="feed_back",
    )(
        grad,
        hidden_in,
        mlp_gain[:, None],
        gate,
        up,
        out_weight,
        gate_up_matrix,
        down_matrix,
    )


def gated_sum_kernel(left_a, left_b, gate_a, gate_b, up_a, up_b, kept, sent):
    half_rows = kept.shape[0]

    def add(right_a, right_b):
        value = (dot(left_a[...], right_a[...]) + dot(left_b[...], right_b[...])).astype(BF16)
        kept[...] = value[:half_rows]
        sent[...] = value[half_rows:]

    first = pl.program_id(0) < pl.num_programs(0) // 2

    @pl.when(first)
    def _():
        add(gate_a, gate_b)

    @pl.when(jnp.logical_not(first))
    def _():
        add(up_a, up_b)


def gated_sum(lefts, gates, ups):
    rows, toks = lefts[0].shape
    hidden = gates[0].shape[1]
    tile = hidden // 2 if hidden % 256 == 0 else hidden
    count = hidden // tile
    whole = pl.BlockSpec((rows, toks), lambda step: (0, 0))
    gate_spec = pl.BlockSpec((toks, tile), lambda step: (0, jnp.minimum(step, count - 1)))
    up_spec_ = pl.BlockSpec((toks, tile), lambda step: (0, jnp.maximum(step - count, 0)))
    return pl.pallas_call(
        gated_sum_kernel,
        grid=(2 * count,),
        in_specs=[whole] * 2 + [gate_spec] * 2 + [up_spec_] * 2,
        out_specs=[pl.BlockSpec((rows // 2, tile), lambda step: (0, step))] * 2,
        out_shape=[jax.ShapeDtypeStruct((rows // 2, 2 * hidden), BF16)] * 2,
        compiler_params=pltpu.CompilerParams(
            dimension_semantics=("arbitrary",), vmem_limit_bytes=36 << 20
        ),
        cost_estimate=pl.CostEstimate(
            flops=8 * rows * toks * hidden,
            bytes_accessed=4 * hidden * (2 * toks + rows),
            transcendentals=0,
        ),
        name="gated_sum",
    )(*lefts, *gates, *ups)


def pair_sum_kernel(*refs, count):
    lefts, rights = refs[: 2 * count], refs[2 * count : 4 * count]
    kept, sent = refs[-2:]
    half_rows = kept.shape[0]
    at = 0
    for one in range(0, 2 * count, 2):
        cols = slice(at, at + rights[one].shape[1])
        value = (
            dot(lefts[one][...], rights[one][...]) + dot(lefts[one + 1][...], rights[one + 1][...])
        ).astype(BF16)
        kept[:, cols] = value[:half_rows]
        sent[:, cols] = value[half_rows:]
        at = cols.stop
    for extra in refs[4 * count : -2]:
        cols = slice(at, at + extra.shape[1])
        kept[:, cols] = extra[:half_rows]
        sent[:, cols] = extra[half_rows:]
        at = cols.stop


def pair_sum(terms, extras=()):
    rows, toks = terms[0][0][0].shape
    cols = sum(rights[0].shape[1] for _, rights in terms)
    total = cols + sum(value.shape[1] for value in extras)
    return pl.pallas_call(
        functools.partial(pair_sum_kernel, count=len(terms)),
        out_shape=[jax.ShapeDtypeStruct((rows // 2, total), BF16)] * 2,
        compiler_params=pltpu.CompilerParams(vmem_limit_bytes=36 << 20),
        cost_estimate=pl.CostEstimate(
            flops=4 * rows * toks * cols,
            bytes_accessed=4 * toks * cols + 2 * rows * total,
            transcendentals=0,
        ),
        name="pair_sum",
    )(*[left for lefts, _ in terms for left in lefts], *[r for _, rights in terms for r in rights], *extras)


class HalvingSum:
    def __init__(self, trade, pair, order, begin=True):
        self.trade, self.order, self.step = trade, order, 1
        self.kept, self.sent = pair
        self.got = self.result = None
        if begin:
            self.got = trade(self.sent, order[0])

    def advance_first(self, gate):
        (self.kept, self.sent), _ = lax.optimization_barrier(((self.kept, self.sent), gate))
        self.got = self.trade(self.sent, self.order[0])

    def advance(self, gate=None):
        if self.result is not None:
            return
        kept, got = self.kept, self.got
        if gate is not None:
            (kept, got), _ = lax.optimization_barrier(((kept, got), gate))
        if self.step == len(self.order):
            self.result = kept.astype(F32) + got.astype(F32)
            return
        left = kept.shape[0] // 2
        self.sent = (kept[left:].astype(F32) + got[left:].astype(F32)).astype(BF16)
        self.kept = (kept[:left].astype(F32) + got[:left].astype(F32)).astype(BF16)
        self.got = self.trade(self.sent, self.order[self.step])
        self.step += 1

    def finish(self):
        while self.result is None:
            self.advance()
        return self.result


class SlotSum:
    def __init__(self, trade, value, order):
        self.trade, self.value, self.order, self.step = trade, value, order, 0
        self.send()

    def send(self):
        left = self.value.shape[1] // 2
        self.kept, self.sent = self.value[:, :left], self.value[:, left:]
        self.got = self.trade(self.sent, self.order[self.step])
        self.step += 1

    def advance(self, gate):
        if self.got is None:
            return
        kept, got = self.kept, self.got
        if gate is not None:
            (kept, got), _ = lax.optimization_barrier(((kept, got), gate))
        self.value = (kept.astype(F32) + got.astype(F32)).astype(BF16)
        self.got = None
        if self.step < len(self.order):
            self.send()
        else:
            self.sent = self.value


def shards(
    tokens,
    cotangent,
    domain_ids,
    domain_counts,
    domain_weights,
    seq_cuts,
    attn_gain,
    query_weight,
    latent_weight,
    latent_up,
    out_weight,
    out_bias,
    mlp_gain,
    gate_up_matrix,
    down_matrix,
):
    seq_count = lax.axis_size("seq")
    rep_count = lax.axis_size("rep")
    place = lax.axis_index("seq").astype(jnp.int32)
    side = lax.axis_index("rep").astype(jnp.int32)
    seq_rows, loc_len, width = tokens.shape
    rows = seq_rows // rep_count
    half = loc_len // 2
    toks = rows * loc_len
    heads_dim = query_weight.shape[2]
    size = latent_up.shape[1]
    hidden = down_matrix.shape[1]
    group_cols = heads_dim // GROUPS
    bits = [1 << at for at in range(seq_count.bit_length() - 1)]
    far_late = bits[:1] + bits[2:3] + bits[1:2] + bits[3:]
    weights = (out_weight, out_bias, mlp_gain, attn_gain, gate_up_matrix, down_matrix)

    def after(value, gate):
        return lax.optimization_barrier((value, gate))[0]

    def swap_ends(value):
        moves = [(at, seq_count - 1 - at) for at in range(seq_count)]
        return lax.ppermute(value, "seq", moves)

    def across(value):
        return lax.ppermute(value, "rep", [(at, rep_count - 1 - at) for at in range(rep_count)])

    def trade(value, bit):
        return lax.ppermute(value, "seq", [(at, at ^ bit) for at in range(seq_count)])

    def rows_of(value, owner):
        return lax.dynamic_slice_in_dim(value, owner * rows, rows, 0)

    def turned(value):
        split = value.reshape((rows, 2, half) + value.shape[1:])
        return jnp.stack([split[:, 0], swap_ends(split[:, 1])], axis=1).reshape(value.shape)

    def tokens_of(value, owner):
        return rows_of(value, owner).reshape((toks,) + value.shape[2:])

    def spread(values, fill_at, fill):
        values = [value.reshape(rows, 1, loc_len, size) for value in values]
        filled = None
        for at, bit in enumerate(reversed(bits)):
            got = [trade(value, bit) for value in values]
            if at == fill_at:
                filled = fill(values)
                values, got = after((values, got), filled)
            values = [jnp.concatenate(pair, axis=1) for pair in zip(values, got)]
        return values, filled

    block = width // (seq_count * rep_count)
    kept_rows = seq_count * block
    row_at = jnp.arange(kept_rows, dtype=jnp.int32)
    col_at = jnp.arange(width, dtype=jnp.int32)

    def halving_step(order):
        distance = jnp.zeros_like(row_at)
        for level, bit in enumerate(order):
            distance = distance + (row_at // block // (seq_count // 2 >> level)) % 2 * bit
        return place ^ distance

    def picker(order, owner):
        source = (halving_step(order) * rep_count + owner) * block + row_at % block
        return (source[:, None] == col_at[None, :]).astype(BF16)

    pick, pick_late = picker(bits, side), picker(far_late, side)
    pick_other = picker(bits, rep_count - 1 - side)
    vector_at = jnp.arange(128, dtype=jnp.int32)[:, None]
    to_halving = (
        (halving_step(bits) * block + row_at % block)[:, None] == row_at[None, :]
    ).astype(BF16)

    def picked(picks, value):
        return dot_as(picks, value, NT).astype(BF16)

    domain_total = domain_counts.shape[0]
    all_tokens = seq_rows * loc_len * seq_count
    per_domain = domain_weights * (all_tokens / domain_total) / domain_counts.astype(F32)
    one_hot = (domain_ids[..., None] == jnp.arange(domain_total, dtype=jnp.int32)).astype(F32)
    row_scale = jnp.sum(one_hot * per_domain, axis=-1)
    pieces = jnp.arange(2 * seq_count, dtype=jnp.int32)

    def scalars_of(zigzag):
        source = pieces // 2
        if zigzag:
            source = jnp.where(pieces % 2 == 0, source, (2 * seq_count - 1 - pieces) // 2)
        distance = source ^ place
        slots = jnp.zeros_like(pieces)
        for level, bit in enumerate(bits):
            slots = slots + distance // bit % 2 * (seq_count // 2 >> level)
        starts = jnp.stack([place * loc_len, (2 * seq_count - 1 - 2 * place) * half])
        return jnp.concatenate([starts, slots, rows_of(seq_cuts, side)])

    def project_back(d_hidden_in, dq, d_lat, state, layer):
        d_normed = dot_as(dq, query_weight[layer], NT) + dot_as(d_lat, latent_weight[layer], NT)
        d_norm, g_gain = norm_back(d_normed, state, rms_scale(state), attn_gain[layer])
        return d_hidden_in + d_norm, g_gain

    def grad_of(owner, gate):
        value = tokens_of(cotangent, owner).astype(F32) * tokens_of(row_scale, owner)[:, None]
        split = value.reshape(rows, 2, half, width)
        swapped = swap_ends(after(split[:, 1].astype(BF16), gate))
        return jnp.stack([split[:, 0], swapped.astype(F32)], axis=1).reshape(toks, width)

    def first_normed(state):
        return (state * rms_scale(state) * attn_gain[0]).astype(BF16)

    natural_own = tokens_of(tokens, side)
    natural_normed = [first_normed(natural_own.astype(F32))]
    hidden_other = None
    saved = []
    for layer in range(LAYERS):
        last = layer == LAYERS - 1
        next_layer = min(layer + 1, LAYERS - 1)
        scalars = scalars_of(layer > 0)
        lat_input = normed_own if layer else natural_normed[0]
        lats = [
            dot(lat_input, latent_weight[layer, :, group * size : (group + 1) * size]).astype(BF16)
            for group in range(GROUPS)
        ]
        if layer == 0:
            lats, own = spread(
                lats, 2, lambda values: turned(after(natural_own, values)).astype(F32)
            )
            normed_own = first_normed(own)
        else:
            lats, hidden_other = spread(
                lats,
                0,
                lambda values: feed(
                    after(other, values), other_heads, layer - 1, next_layer, weights
                ),
            )
            saved[-1].append(hidden_other)
            other, normed_other = hidden_other[5:]
        queries_t = jnp.einsum(
            "rpid,df->rpfi",
            normed_own.reshape(rows, 2, half, width),
            query_weight[layer],
            preferred_element_type=F32,
        ).astype(BF16)
        up_t = latent_up[layer].T
        heads, attended = [], []
        for group in range(GROUPS):
            out, *rest = attend(scalars, queries_t, lats[group], up_t, group, heads)
            heads = [out]
            attended.append(rest)
            if group == 0:
                if last:
                    grad_own = grad_of(side, out)
                else:
                    natural_other = tokens_of(after(tokens, out), rep_count - 1 - side)
                    natural_normed.append(first_normed(natural_other.astype(F32)))
                    other = turned(natural_other)
        heads = heads[0].reshape(toks, heads_dim)
        other_heads = across(heads)
        if last:
            own, grad_own = after((own, grad_own), heads)
        else:
            own, other = after((own, other), heads)
            other = other.astype(F32)
        hidden_own = feed(own, heads, layer, next_layer, weights)
        saved.append([own, normed_own, heads, hidden_own, lats, queries_t, up_t, attended, scalars])
        saved[-1] += [other, normed_other if layer else None, other_heads]
        own, normed_own = hidden_own[5:]

    def placed(value, moved):
        both = jnp.stack([value, moved]).reshape(2, rows, loc_len, width)
        return jnp.where(side == 0, both, both[::-1]).reshape(seq_rows, loc_len, width)

    output = turned(own.astype(BF16))
    grad_other = None
    pending = []
    other_input = None
    layer_sums = []
    for layer in reversed(range(LAYERS)):
        last = layer == LAYERS - 1
        own, normed_own, heads, hidden_own, lats, queries_t, up_t, attended, scalars = saved[layer][:9]
        other, normed_other, other_heads = saved[layer][9:12]
        back_own = feed_back(
            grad_own, hidden_own[0], hidden_own[2], hidden_own[3], layer, half, weights
        )
        d_heads_t = back_own[5].reshape(rows, 2, heads_dim, half)
        d_in_own = back_own[3]
        d_lat, up_k, up_v, filled = [], [], [], []

        def stepped(gate):
            for late in d_lat:
                late.advance(gate)
            return [late.sent for late in d_lat]

        def sents_of(sums):
            return [one.sent for one in sums]

        def wide_sums(back_other, gate):
            backs = (back_own, back_other)
            hiddens = (hidden_own, hidden_other)
            gates, acts = after(([back[0] for back in backs], [hid[4] for hid in hiddens]), gate)
            gated = gated_sum(
                [picked(pick, hid[1]) for hid in hiddens], gates, [back[1] for back in backs]
            )
            plain = pair_sum(
                [
                    ([picked(pick_late, back[2]) for back in backs], acts),
                    ([picked(pick_late, back[4]) for back in backs], [heads, other_heads]),
                ]
            )
            return [HalvingSum(trade, gated, bits), HalvingSum(trade, plain, far_late)]

        def other_back(gate):
            return feed_back(
                after(grad_other, gate),
                hidden_other[0],
                hidden_other[2],
                hidden_other[3],
                layer,
                half,
                weights,
            )

        if last:
            d_heads_t = after(d_heads_t, output)
            output_moved = across(output)
        else:
            d_in_own = turned(d_in_own.astype(BF16)).astype(F32)
            hidden_other = saved[layer][12]
            grad_other, _ = project_back(*after(other_input, back_own[3]), layer + 1)
            back_other = other_back(back_own[3])
            for late in pending[:2]:
                late.advance(back_other[3])
            sums = wide_sums(back_other, (sents_of(pending[:2]), d_in_own))
            pending[2].advance_first([sums[0].kept, sums[1].kept])
            for late in pending[:2]:
                late.advance(pending[2].sent)
            for one in sums:
                one.advance(sents_of(pending[:2]))
            d_heads_t = after(d_heads_t, sents_of(sums + pending))
        for group in range(GROUPS):
            dq, d_lat_one, up_k_one, up_v_one = attend_back(
                scalars,
                queries_t,
                d_heads_t,
                attended[group][0],
                lats[group],
                up_t,
                attended[group][1:],
                group,
                filled,
            )
            up_k.append(up_k_one)
            up_v.append(up_v_one)
            for late in pending + d_lat:
                late.advance(up_k_one)
            d_lat.append(SlotSum(trade, d_lat_one, bits))
            sents = sents_of(pending + d_lat)
            filled = [dq]
            if group == 0:
                d_heads_t = after(d_heads_t, (sents, output_moved) if last else sents)
                if last:
                    grad_other = grad_of(rep_count - 1 - side, sents)
        dq = dq.reshape(toks, heads_dim)
        up_block = latent_up.shape[2] // (seq_count * rep_count)
        folds = up_block // block
        split = [value.reshape(-1, rep_count, up_block, size) for value in up_k + up_v]

        def up_of(owner):
            chosen = [lax.dynamic_index_in_dim(value, owner, 1, False) for value in split]
            return jnp.concatenate([value.astype(BF16) for value in chosen], axis=0)

        up_sent = up_of(rep_count - 1 - side)
        if last:
            grad_other = after(grad_other, dq)
            state, _ = after((other, grad_other), sents)
            dq_other = across(dq)
            hidden_other = feed(state, other_heads, layer, layer, weights)
            sents = stepped(hidden_other[0])
            dq_other = after(dq_other, hidden_other[0])
            up_got = across(up_sent)
            back_other = other_back(sents + [dq_other, up_sent])
            sents = stepped(back_other[3])
            up_got = after(up_got, back_other[3])
            sums = wide_sums(back_other, sents + [up_got])
            sents = stepped([sums[0].kept, sums[1].kept])
            for one in sums:
                one.advance(sents)
            stepped(sents_of(sums))
        else:
            dq = turned(dq)
            up_got = across(up_sent)
            sents = stepped(up_sent)
            for one in sums:
                one.advance(sents)
            sents = stepped(sents_of(sums))
            dq = after(dq, sents)
            dq_other = across(dq)
            pending[2].advance(sents)
            sents = stepped(pending[2].sent)
            up_got = after(up_got, sents)
            pending[2].advance(sents)
        while any(late.got is not None for late in d_lat):
            stepped(None)
        d_lat = jnp.concatenate([late.value.reshape(toks, size) for late in d_lat], axis=1)
        d_lat_other = across(d_lat)
        state = own if layer else natural_own.astype(F32)
        grad_own, attn_gain_own = project_back(d_in_own, dq, d_lat, state, layer)
        if last:
            other_input = (back_other[3], dq_other, d_lat_other, other)
        normed = [
            picked(pick, value)
            for value in ((normed_own, normed_other) if layer else natural_normed)
        ]

        up_rows = (up_of(side).astype(F32) + up_got.astype(F32)).astype(BF16)
        up_rows = jnp.concatenate(
            [up_rows[:, at * block : (at + 1) * block] for at in range(folds)], axis=2
        ).reshape(kept_rows, folds * size)
        up_rows = dot(to_halving, up_rows).astype(BF16)
        vectors = jnp.where(
            vector_at == 0,
            back_own[6] + back_other[6],
            jnp.where(
                vector_at == 1,
                back_own[7] + back_other[7],
                jnp.where(vector_at == 2, attn_gain_own[None], 0.0),
            ),
        )
        vectors_other = jnp.where(vector_at == 3, attn_gain_own[None], 0.0)
        vectors = (
            dot_as(pick, vectors.astype(BF16), NT) + dot_as(pick_other, vectors_other.astype(BF16), NT)
        ).astype(BF16)
        terms = [(normed, [dq, dq_other]), (normed, [d_lat, d_lat_other])]
        rest = HalvingSum(trade, pair_sum(terms, [up_rows, vectors]), bits, begin=not last)
        if not last:
            sums[1].advance(rest.sent)
            sums[0].advance(sums[1].sent)
            rest.advance(sums[0].sent)
        sums.append(rest)
        pending = sums
        layer_sums.insert(0, sums)
    layer_grads = []
    for sums in layer_sums:
        g_gate_up, g_plain, g_rest = [one.finish() for one in sums]
        lat_at, up_at = heads_dim, heads_dim + GROUPS * size
        vectors_at = up_at + folds * size
        g_up = jnp.concatenate(
            [g_rest[:, up_at + at * size : up_at + (at + 1) * size] for at in range(folds)]
        )
        layer_grads.append(
            (
                g_rest[:, vectors_at + 2] + across(g_rest[:, vectors_at + 3]),
                g_rest[:, :lat_at],
                g_rest[:, lat_at:up_at],
                g_up.T,
                g_plain[:, hidden:].T,
                g_rest[:, vectors_at + 1],
                g_rest[:, vectors_at],
                g_gate_up,
                g_plain[:, :hidden].T,
            )
        )
    stacked = [jnp.stack([grads[member] for grads in layer_grads]) for member in range(9)]
    input_grad = grad_own.astype(BF16)
    return (
        placed(output, output_moved),
        placed(input_grad, across(input_grad)),
        *stacked,
    )


def solution(mesh):
    rows = P(None, "seq", None)
    scattered = P(None, ("seq", "rep"))
    first = P(None, ("seq", "rep"), None)
    second = P(None, None, ("seq", "rep"))
    return jax.shard_map(
        shards,
        mesh=mesh,
        in_specs=(rows, rows, P(None, "seq")) + (P(),) * 12,
        out_specs=(
            rows,
            rows,
            scattered,
            first,
            first,
            second,
            second,
            scattered,
            scattered,
            first,
            second,
        ),
        check_vma=False,
    )
```

time: 818 us -> 646 us (0.79)
  Pallas kernels: 301 us -> 246 us
  waiting for transfers between devices: 252 us -> 207 us
  local copies, waits for them, and re-layouts: 75.6 us -> 32.3 us
  matrix products: 42.9 us -> 29.1 us
  other arithmetic: 33.8 us -> 47.5 us
  between operations: 16.9 us -> 3.32 us
    ppermute x48 -> x56, waiting for transfers between devices: 231 us -> 176 us  [trade(): lax.ppermute(value, 'seq', [(at, at ^ bit) for at in range(seq_count)])]
    pallas_call x16 -> x14, Pallas kernels: 156 us -> 102 us  [the longest x4 47.3 us: feed_back(): pl.pallas_call(functools.partial(feed_back_kernel, layer=layer, hidden=hi...]
    unnamed x300 -> x206, local copies, waits for them, and re-layouts: 56.1 us -> 18.8 us
    dot_general x34 -> x26, matrix products: 36.6 us -> 21.7 us  [dot_as(): return lax.dot_general(left, right, dims, preferred_element_type=F32)]
    ppermute x8 -> x7, waiting for transfers between devices: 7.57 us -> 21.6 us  [swap_ends(): return lax.ppermute(value, 'seq', moves)]
    convert_element_type x29 -> x39, other arithmetic: 12.3 us -> 25.5 us  [the longest x14 17.7 us: advance(): self.kept = (kept[:left].astype(F32) + got[:left].astype(F32)).astype(BF16)]
    ppermute x8 -> x7, starting transfers between devices: 17.4 us -> 13.1 us  [swap_ends(): return lax.ppermute(value, 'seq', moves)]
    ppermute x48 -> x56, starting transfers between devices: 57.3 us -> 55.6 us  [trade(): lax.ppermute(value, 'seq', [(at, at ^ bit) for at in range(seq_count)])]
  transfers between devices with their start and end apart: 74 -> 75, of which waited for: 38 -> 29; matrix products, arithmetic and copies ran while one was open for 11% -> 14% of each run, Pallas kernels for 34% -> 38%
where the time goes in v3:
time: 646 us; the launch traced here: 642 us
  Pallas kernels  246 us (38%)
  waiting for transfers between devices  207 us (32%)
  starting transfers between devices  77 us (12%)
  other arithmetic  47.5 us (7%)
  local copies, waits for them, and re-layouts  32.3 us (5%)
  matrix products  29.1 us (5%)
    ppermute x56, waiting for transfers between devices, trade(): lax.ppermute(value, 'seq', [(at, at ^ bit) for at in range(seq_count)])  176 us
    pallas_call x4, Pallas kernels, attend_back(): pl.pallas_call(functools.partial(attend_back_kernel, seq_count=seq_count,...  83.8 us
    pallas_call x4, Pallas kernels, attend(): pl.pallas_call(functools.partial(attend_kernel, seq_count=seq_count, half...  60.7 us
    ppermute x56, starting transfers between devices, trade(): lax.ppermute(value, 'seq', [(at, at ^ bit) for at in range(seq_count)])  55.6 us
    pallas_call x4, Pallas kernels, feed_back(): pl.pallas_call(functools.partial(feed_back_kernel, layer=layer, hidden=hi...  47.3 us
    pallas_call x4, Pallas kernels, feed(): pl.pallas_call(functools.partial(feed_kernel, layer=layer, hidden=hidden)...  36.5 us
    dot_general x26, matrix products, dot_as(): return lax.dot_general(left, right, dims, preferred_element_type=F32)  21.7 us
    ppermute x7, waiting for transfers between devices, swap_ends(): return lax.ppermute(value, 'seq', moves)  21.6 us
  transfers between devices with their start and end apart: 75, of which 29 were waited for; matrix products, arithmetic and copies ran while one was open for 14% of the time, Pallas kernels for 38%

profile of v3, /device:TPU:0, one launch (start us, length us, event | category | flops | bytes accessed | tf_op | source)
XLA Modules:
  0.0 642.3 jit_solution(13911404977564977693)
XLA Ops:
  62.1 15.2 %attend.4 = (bf16[1,2,128,1024]{3,2,1,0:T(8,128)(2,1)S(1)}, bf16[1,2,512,128]{3,2,1,0:T(8,128)(2,1)}, f32[1,2,1,1024]{3,2,1,0:T(1,128)}, bf16[1,2,1024,256]{3,2,1,0:T(8,128)(2,1)}, bf16[1,2,256,1024]{3,2,1,0:T(8,128)(2,1)}) custom-call(s32[35]{0:T(128)S(1)} %add_add_fusion.1.scalars, bf16[1,2,1024,128]{3,2,1,0:T(8,128)(2,1)S(1)} %fusion.57.q_ref, ...), custom_call_target="tpu_custom_call" | custom-call | flops 4294967296 | bytes 4194304 | tf_op jit(solution)/shard_map/attend/pallas_call | solution.py:260
  81.7 15.2 %attend.5 = (bf16[1,2,128,1024]{3,2,1,0:T(8,128)(2,1)S(1)}, bf16[1,2,512,128]{3,2,1,0:T(8,128)(2,1)}, f32[1,2,1,1024]{3,2,1,0:T(1,128)}, bf16[1,2,1024,256]{3,2,1,0:T(8,128)(2,1)}, bf16[1,2,256,1024]{3,2,1,0:T(8,128)(2,1)}) custom-call(s32[35]{0:T(128)S(1)} %add_add_fusion.1.scalars, ...), custom_call_target="tpu_custom_call", output_to_operand_aliasing={{0}: (5, {})} | custom-call | flops 4294967296 | bytes 4194304 | tf_op jit(solution)/shard_map/attend/pallas_call | solution.py:260
  113.1 8.8 %feed.5 = (f32[256,1024]{1,0:T(8,128)S(1)}, bf16[256,1024]{1,0:T(8,128)(2,1)S(1)}, bf16[256,2816]{1,0:T(8,128)(2,1)S(1)}, bf16[256,2816]{1,0:T(8,128)(2,1)S(1)},...) custom-call(bf16[256,1024]{1,0:T(8,128)(2,1)S(1)} %collective-permute-done.12.heads.refs_7_, ...), custom_call_target="tpu_custom_call" | custom-call | flops 4966055936 | bytes 23724032 | tf_op jit(solution)/shard_map/feed/pallas_call | solution.py:504
  137.6 8.8 %collective-permute-done.17 = bf16[1,4,256,256]{3,2,1,0:T(8,128)(2,1)S(1)} collective-permute-done((bf16[1,4,256,256]{3,2,1,0:T(8,128)(2,1)S(1)}, bf16[1,4,256,256]{3,2,1,0:T(8,128)(2,1)S(1)}, u32[]{:S(2)}, u32[]{:S(2)}) %collective-permute-start.17) | collective-permute-done | bytes 524320 | tf_op jit(solution)/shard_map/ppermute | solution.py:895
  156.7 15.1 %attend.6 = (bf16[1,2,128,1024]{3,2,1,0:T(8,128)(2,1)}, bf16[1,2,512,128]{3,2,1,0:T(8,128)(2,1)}, f32[1,2,1,1024]{3,2,1,0:T(1,128)}, bf16[1,2,1024,256]{3,2,1,0:T(8,128)(2,1)}, bf16[1,2,256,1024]{3,2,1,0:T(8,128)(2,1)}) custom-call(s32[35]{0:T(128)S(1)} %add_add_fusion.scalars, bf16[1,2,1024,128]{3,2,1,0:T(8,128)(2,1)S(1)} %fusion.54.q_ref, ...), custom_call_target="tpu_custom_call" | custom-call | flops 4294967296 | bytes 4194304 | tf_op jit(solution)/shard_map/attend/pallas_call | solution.py:260
  172.4 15.1 %attend.7 = (bf16[1,2,128,1024]{3,2,1,0:T(8,128)(2,1)}, bf16[1,2,512,128]{3,2,1,0:T(8,128)(2,1)}, f32[1,2,1,1024]{3,2,1,0:T(1,128)}, bf16[1,2,1024,256]{3,2,1,0:T(8,128)(2,1)}, bf16[1,2,256,1024]{3,2,1,0:T(8,128)(2,1)}) custom-call(s32[35]{0:T(128)S(1)} %add_add_fusion.scalars, ...), custom_call_target="tpu_custom_call", output_to_operand_aliasing={{0}: (5, {})} | custom-call | flops 4294967296 | bytes 4194304 | tf_op jit(solution)/shard_map/attend/pallas_call | solution.py:260
  187.7 9.5 %feed.6 = (f32[256,1024]{1,0:T(8,128)S(1)}, bf16[256,1024]{1,0:T(8,128)(2,1)S(1)}, bf16[256,2816]{1,0:T(8,128)(2,1)S(1)}, bf16[256,2816]{1,0:T(8,128)(2,1)S(1)},...) custom-call(bf16[256,1024]{1,0:T(8,128)(2,1)} %bitcast.44.heads.refs_6_, ...), custom_call_target="tpu_custom_call" | custom-call | flops 4966055936 | bytes 23724032 | tf_op jit(solution)/shard_map/feed/pallas_call | solution.py:504
  201.5 11.6 %feed_back.4 = (bf16[256,2816]{1,0:T(8,128)(2,1)S(1)}, bf16[256,2816]{1,0:T(8,128)(2,1)S(1)}, bf16[256,1024]{1,0:T(8,128)(2,1)S(1)}, f32[256,1024]{1,0:T(8,128)S...) custom-call(f32[256,1024]{1,0:T(8,128)S(1)} %bitcast.333, ...), custom_call_target="tpu_custom_call" | custom-call | flops 4966055936 | bytes 25165824 | tf_op jit(solution)/shard_map/feed_back/pallas_call | solution.py:659
  217.3 20.9 %attend_back.4 = (bf16[1,2,128,1024]{3,2,1,0:T(8,128)(2,1)S(1)}, bf16[1,16,256,256]{3,2,1,0:T(8,128)(2,1)S(1)}, f32[512,256]{1,0:T(8,128)S(1)}, f32[512,256]{1,0:T(8,128)S(1)}) custom-call(s32[35]{0:T(128)S(1)} %add_add_fusion.scalars, bf16[1,2,1024,128]{3,2,1,0:T(8,128)(2,1)} %copy-done.51, bf16[1,2,1024,128]{3,2,1,0:T(8,128)(2,1)} %bitcast.369, ...), custom_call_target="tpu_custom_call" | custom-call | flops 10737418240 | bytes 7340032 | tf_op jit(solution)/shard_map/attend_back/pallas_call | solution.py:316
  241.1 9.1 %collective-permute-done.25 = bf16[1,128,1024]{2,1,0:T(8,128)(2,1)S(1)} collective-permute-done((bf16[1,128,1024]{2,1,0:T(8,128)(2,1)S(1)}, bf16[1,128,1024]{2,1,0:T(8,128)(2,1)S(1)}, u32[]{:S(2)}, u32[]{:S(2)}) %collective-permute-start.25) | collective-permute-done | bytes 262176 | tf_op jit(solution)/shard_map/ppermute | solution.py:889
  254.8 21.0 %attend_back.5 = (bf16[1,2,128,1024]{3,2,1,0:T(8,128)(2,1)S(1)}, bf16[1,16,256,256]{3,2,1,0:T(8,128)(2,1)S(1)}, f32[512,256]{1,0:T(8,128)S(1)}, f32[512,256]{1,0:T(8,128)S(1)}) custom-call(s32[35]{0:T(128)S(1)} %add_add_fusion.scalars, bf16[1,2,1024,128]{3,2,1,0:T(8,128)(2,1)} %copy-done.51, ...), custom_call_target="tpu_custom_call", output_to_operand_aliasing={{0}: (10, {})} | custom-call | flops 10737418240 | bytes 7340032 | tf_op jit(solution)/shard_map/attend_back/pallas_call | solution.py:316
  285.5 9.6 %feed.7 = (f32[256,1024]{1,0:T(8,128)S(1)}, bf16[256,1024]{1,0:T(8,128)(2,1)S(1)}, bf16[256,2816]{1,0:T(8,128)(2,1)S(1)}, bf16[256,2816]{1,0:T(8,128)(2,1)S(1)},...) custom-call(bf16[256,1024]{1,0:T(8,128)(2,1)S(1)} %copy-done.19, ...), custom_call_target="tpu_custom_call" | custom-call | flops 4966055936 | bytes 23724032 | tf_op jit(solution)/shard_map/feed/pallas_call | solution.py:504
  299.8 12.3 %feed_back.5 = (bf16[256,2816]{1,0:T(8,128)(2,1)S(1)}, bf16[256,2816]{1,0:T(8,128)(2,1)S(1)}, bf16[256,1024]{1,0:T(8,128)(2,1)S(1)}, f32[256,1024]{1,0:T(8,128)S...) custom-call(f32[256,1024]{1,0:T(8,128)S(1)} %bitcast.331, ...), custom_call_target="tpu_custom_call" | custom-call | flops 4966055936 | bytes 25165824 | tf_op jit(solution)/shard_map/feed_back/pallas_call | solution.py:659
  356.1 11.2 %feed_back.6 = (bf16[256,2816]{1,0:T(8,128)(2,1)S(1)}, bf16[256,2816]{1,0:T(8,128)(2,1)S(1)}, bf16[256,1024]{1,0:T(8,128)(2,1)S(1)}, f32[256,1024]{1,0:T(8,128)S...) custom-call(f32[256,1024]{1,0:T(8,128)S(1)} %multiply_add_fusion.1.g, ...), custom_call_target="tpu_custom_call" | custom-call | flops 4966055936 | bytes 25165824 | tf_op jit(solution)/shard_map/feed_back/pallas_call | solution.py:659
  373.1 12.2 %feed_back.7 = (bf16[256,2816]{1,0:T(8,128)(2,1)S(1)}, bf16[256,2816]{1,0:T(8,128)(2,1)S(1)}, bf16[256,1024]{1,0:T(8,128)(2,1)S(1)}, f32[256,1024]{1,0:T(8,128)}...) custom-call(f32[256,1024]{1,0:T(8,128)S(1)} %multiply_add_fusion.gra, ...), custom_call_target="tpu_custom_call" | custom-call | flops 4966055936 | bytes 25165824 | tf_op jit(solution)/shard_map/feed_back/pallas_call | solution.py:659
  406.3 12.1 %collective-permute-done.41 = bf16[64,5632]{1,0:T(8,128)(2,1)S(1)} collective-permute-done((bf16[64,5632]{1,0:T(8,128)(2,1)}, bf16[64,5632]{1,0:T(8,128)(2,1)S(1)}, u32[]{:S(2)}, u32[]{:S(2)}) %collective-permute-start.41) | collective-permute-done | bytes 720928 | tf_op jit(solution)/shard_map/ppermute | solution.py:895
  425.3 20.9 %attend_back.6 = (bf16[1,2,128,1024]{3,2,1,0:T(8,128)(2,1)S(1)}, bf16[1,16,256,256]{3,2,1,0:T(8,128)(2,1)S(1)}, f32[512,256]{1,0:T(8,128)S(1)}, f32[512,256]{1,0:T(8,128)S(1)}) custom-call(s32[35]{0:T(128)S(1)} %copy-done.30, bf16[1,2,1024,128]{3,2,1,0:T(8,128)(2,1)} %copy-done.57, bf16[1,2,1024,128]{3,2,1,0:T(8,128)(2,1)} %bitcast.367, ...), custom_call_target="tpu_custom_call" | custom-call | flops 10737418240 | bytes 7340032 | tf_op jit(solution)/shard_map/attend_back/pallas_call | solution.py:316
  448.6 21.0 %attend_back.7 = (bf16[1,2,128,1024]{3,2,1,0:T(8,128)(2,1)S(1)}, bf16[1,16,256,256]{3,2,1,0:T(8,128)(2,1)S(1)}, f32[512,256]{1,0:T(8,128)S(1)}, f32[512,256]{1,0:T(8,128)S(1)}) custom-call(s32[35]{0:T(128)S(1)} %copy-done.30, bf16[1,2,1024,128]{3,2,1,0:T(8,128)(2,1)} %copy-done.57, ...), custom_call_target="tpu_custom_call", output_to_operand_aliasing={{0}: (10, {})} | custom-call | flops 10737418240 | bytes 7340032 | tf_op jit(solution)/shard_map/attend_back/pallas_call | solution.py:316
  476.2 9.0 %collective-permute-done.45 = bf16[1,128,1024]{2,1,0:T(8,128)(2,1)S(1)} collective-permute-done((bf16[1,128,1024]{2,1,0:T(8,128)(2,1)S(1)}, bf16[1,128,1024]{2,1,0:T(8,128)(2,1)S(1)}, u32[]{:S(2)}, u32[]{:S(2)}) %collective-permute-start.45) | collective-permute-done | bytes 262176 | tf_op jit(solution)/shard_map/ppermute | solution.py:889
  491.7 30.3 %collective-permute-done.47 = bf16[1,4,256,256]{3,2,1,0:T(8,128)(2,1)S(1)} collective-permute-done((bf16[1,4,256,256]{3,2,1,0:T(8,128)(2,1)S(1)}, bf16[1,4,256,256]{3,2,1,0:T(8,128)(2,1)S(1)}, u32[]{:S(2)}, u32[]{:S(2)}) %collective-permute-start.47) | collective-permute-done | bytes 524320 | tf_op jit(solution)/shard_map/ppermute | solution.py:895
  526.1 10.7 %collective-permute-done.52 = bf16[1,4,256,256]{3,2,1,0:T(8,128)(2,1)S(1)} collective-permute-done((bf16[1,4,256,256]{3,2,1,0:T(8,128)(2,1)S(1)}, bf16[1,4,256,256]{3,2,1,0:T(8,128)(2,1)S(1)}, u32[]{:S(2)}, u32[]{:S(2)}) %collective-permute-start.52) | collective-permute-done | bytes 524320 | tf_op jit(solution)/shard_map/ppermute | solution.py:895
  540.9 19.9 %collective-permute-done.56 = bf16[1,2,256,256]{3,2,1,0:T(8,128)(2,1)S(1)} collective-permute-done((bf16[1,2,256,256]{3,2,1,0:T(8,128)(2,1)S(1)}, bf16[1,2,256,256]{3,2,1,0:T(8,128)(2,1)S(1)}, u32[]{:S(2)}, u32[]{:S(2)}) %collective-permute-start.56) | collective-permute-done | bytes 262176 | tf_op jit(solution)/shard_map/ppermute | solution.py:895
  592.3 15.5 %collective-permute-done.71 = bf16[32,3840]{1,0:T(8,128)(2,1)S(1)} collective-permute-done((bf16[32,3840]{1,0:T(8,128)(2,1)S(1)}, bf16[32,3840]{1,0:T(8,128)(2,1)S(1)}, u32[]{:S(2)}, u32[]{:S(2)}) %collective-permute-start.71) | collective-permute-done | bytes 245792 | tf_op jit(solution)/shard_map/ppermute | solution.py:895
  611.1 11.4 %collective-permute-done.65 = bf16[128,2176]{1,0:T(8,128)(2,1)S(1)} collective-permute-done((bf16[128,2176]{1,0:T(8,128)(2,1)S(1)}, bf16[128,2176]{1,0:T(8,128)(2,1)S(1)}, u32[]{:S(2)}, u32[]{:S(2)}) %collective-permute-start.65) | collective-permute-done | bytes 557088 | tf_op jit(solution)/shard_map/ppermute | solution.py:895
  (571 shorter events, 292.5 us)
Async XLA Ops:
  32.9 23.9 %collective-permute-start.6 = (bf16[1,4,256,256]{3,2,1,0:T(8,128)(2,1)S(1)}, bf16[1,4,256,256]{3,2,1,0:T(8,128)(2,1)}, u32[]{:S(2)}, u32[]{:S(2)}) collective-permute-start(bf16[1,4,256,256]{3,2,1,0:T(8,128)(2,1)S(1)} %pad_maximum_fusion.11), channel_id=1, source_target_pairs={{0,4},{2,6},{4,0},{6,2},{8,12},{10,14},{12,8},{14,10},{16,20},{18,... | collective-permute-start | bytes 1572872 | tf_op jit(solution)/shard_map/ppermute | solution.py:895
  187.5 96.2 %collective-permute-start.24 = (bf16[256,1024]{1,0:T(8,128)(2,1)}, bf16[256,1024]{1,0:T(8,128)(2,1)S(1)}, u32[]{:S(2)}, u32[]{:S(2)}) collective-permute-start(bf16[256,1024]{1,0:T(8,128)(2,1)} %bitcast.44.heads.refs_6_), channel_id=1, source_target_pairs={{0,1},{1,0},{2,3},{3,2},{4,5},{5,4},{6,7},{7,6},{8,9},{9,8},{10,11... | collective-permute-start | bytes 1572872 | tf_op jit(solution)/shard_map/ppermute | solution.py:892
  240.6 39.5 %collective-permute-start.22 = (bf16[1,8,256,256]{3,2,1,0:T(8,128)(2,1)}, bf16[1,8,256,256]{3,2,1,0:T(8,128)(2,1)}, u32[]{:S(2)}, u32[]{:S(2)}) collective-permute-start(bf16[1,8,256,256]{3,2,1,0:T(8,128)(2,1)} %get-tuple-element.476), channel_id=1, source_target_pairs={{0,2},{2,0},{4,6},{6,4},{8,10},{10,8},{12,14},{14,12},{16,18},{18,... | collective-permute-start | bytes 3145736 | tf_op jit(solution)/shard_map/ppermute | solution.py:895
  278.0 35.3 %collective-permute-start.31 = (bf16[16,64,256]{2,1,0:T(8,128)(2,1)}, bf16[16,64,256]{2,1,0:T(8,128)(2,1)S(1)}, u32[]{:S(2)}, u32[]{:S(2)}) collective-permute-start(bf16[16,64,256]{2,1,0:T(8,128)(2,1)} %pad_maximum_fusion.16), channel_id=1, source_target_pairs={{0,1},{1,0},{2,3},{3,2},{4,5},{5,4},{6,7},{7,6},{8,9},{9,8},{10,11... | collective-permute-start | bytes 1572872 | tf_op jit(solution)/shard_map/ppermute | solution.py:892
  318.8 24.1 %collective-permute-start.35 = (bf16[256,3840]{1,0:T(8,128)(2,1)S(1)}, bf16[256,3840]{1,0:T(8,128)(2,1)}, u32[]{:S(2)}, u32[]{:S(2)}) collective-permute-start(bf16[256,3840]{1,0:T(8,128)(2,1)S(1)} %get-tuple-element.323), channel_id=1, source_target_pairs={{0,2},{2,0},{4,6},{6,4},{8,10},{10,8},{12,14},{14,12},{16,18},{18,... | collective-permute-start | bytes 5898248 | tf_op jit(solution)/shard_map/ppermute | solution.py:895
  345.8 39.5 %collective-permute-start.39 = (bf16[128,3840]{1,0:T(8,128)(2,1)}, bf16[128,3840]{1,0:T(8,128)(2,1)}, u32[]{:S(2)}, u32[]{:S(2)}) collective-permute-start(bf16[128,3840]{1,0:T(8,128)(2,1)} %get-tuple-element.462), channel_id=1, source_target_pairs={{0,8},{2,10},{4,12},{6,14},{8,0},{10,2},{12,4},{14,6},{16,24},{18,... | collective-permute-start | bytes 2949128 | tf_op jit(solution)/shard_map/ppermute | solution.py:895
  351.0 40.3 %collective-permute-start.38 = (bf16[128,5632]{1,0:T(8,128)(2,1)}, bf16[128,5632]{1,0:T(8,128)(2,1)}, u32[]{:S(2)}, u32[]{:S(2)}) collective-permute-start(bf16[128,5632]{1,0:T(8,128)(2,1)} %get-tuple-element.458), channel_id=1, source_target_pairs={{0,4},{2,6},{4,0},{6,2},{8,12},{10,14},{12,8},{14,10},{16,20},{18,... | collective-permute-start | bytes 4325384 | tf_op jit(solution)/shard_map/ppermute | solution.py:895
  394.0 24.4 %collective-permute-start.41 = (bf16[64,5632]{1,0:T(8,128)(2,1)}, bf16[64,5632]{1,0:T(8,128)(2,1)S(1)}, u32[]{:S(2)}, u32[]{:S(2)}) collective-permute-start(bf16[64,5632]{1,0:T(8,128)(2,1)} %get-tuple-element.466), channel_id=1, source_target_pairs={{0,8},{2,10},{4,12},{6,14},{8,0},{10,2},{12,4},{14,6},{16,24},{18,... | collective-permute-start | bytes 2162696 | tf_op jit(solution)/shard_map/ppermute | solution.py:895
  396.3 23.4 %collective-permute-start.43 = (bf16[256,3840]{1,0:T(8,128)(2,1)S(1)}, bf16[256,3840]{1,0:T(8,128)(2,1)S(1)}, u32[]{:S(2)}, u32[]{:S(2)}) collective-permute-start(bf16[256,3840]{1,0:T(8,128)(2,1)S(1)} %get-tuple-element.373), channel_id=1, source_target_pairs={{0,2},{2,0},{4,6},{6,4},{8,10},{10,8},{12,14},{14,12},{16,18},{18,... | collective-permute-start | bytes 5898248 | tf_op jit(solution)/shard_map/ppermute | solution.py:895
  402.7 44.7 %collective-permute-start.44 = (bf16[256,2176]{1,0:T(8,128)(2,1)S(1)}, bf16[256,2176]{1,0:T(8,128)(2,1)S(1)}, u32[]{:S(2)}, u32[]{:S(2)}) collective-permute-start(bf16[256,2176]{1,0:T(8,128)(2,1)S(1)} %get-tuple-element.366), channel_id=1, source_target_pairs={{0,2},{2,0},{4,6},{6,4},{8,10},{10,8},{12,14},{14,12},{16,18},{18,... | collective-permute-start | bytes 3342344 | tf_op jit(solution)/shard_map/ppermute | solution.py:895
  403.4 66.4 %collective-permute-start.72 = (bf16[32,3840]{1,0:T(8,128)(2,1)S(1)}, bf16[32,3840]{1,0:T(8,128)(2,1)}, u32[]{:S(2)}, u32[]{:S(2)}) collective-permute-start(bf16[32,3840]{1,0:T(8,128)(2,1)S(1)} %get-tuple-element.502), channel_id=1, source_target_pairs={{0,16},{2,18},{4,20},{6,22},{8,24},{10,26},{12,28},{14,30},{16,0},... | collective-permute-start | bytes 737288 | tf_op jit(solution)/shard_map/ppermute | solution.py:895
  419.3 54.8 %collective-permute-start.74 = (bf16[32,5632]{1,0:T(8,128)(2,1)}, bf16[32,5632]{1,0:T(8,128)(2,1)S(1)}, u32[]{:S(2)}, u32[]{:S(2)}) collective-permute-start(bf16[32,5632]{1,0:T(8,128)(2,1)} %get-tuple-element.486), channel_id=1, source_target_pairs={{0,16},{2,18},{4,20},{6,22},{8,24},{10,26},{12,28},{14,30},{16,0},... | collective-permute-start | bytes 1081352 | tf_op jit(solution)/shard_map/ppermute | solution.py:895
  421.2 102.7 %collective-permute-start.51 = (bf16[128,3840]{1,0:T(8,128)(2,1)}, bf16[128,3840]{1,0:T(8,128)(2,1)}, u32[]{:S(2)}, u32[]{:S(2)}) collective-permute-start(bf16[128,3840]{1,0:T(8,128)(2,1)} %get-tuple-element.460), channel_id=1, source_target_pairs={{0,8},{2,10},{4,12},{6,14},{8,0},{10,2},{12,4},{14,6},{16,24},{18,... | collective-permute-start | bytes 2949128 | tf_op jit(solution)/shard_map/ppermute | solution.py:895
  448.4 37.1 %collective-permute-start.54 = (bf16[128,2176]{1,0:T(8,128)(2,1)}, bf16[128,2176]{1,0:T(8,128)(2,1)}, u32[]{:S(2)}, u32[]{:S(2)}) collective-permute-start(bf16[128,2176]{1,0:T(8,128)(2,1)} %get-tuple-element.470), channel_id=1, source_target_pairs={{0,4},{2,6},{4,0},{6,2},{8,12},{10,14},{12,8},{14,10},{16,20},{18,... | collective-permute-start | bytes 1671176 | tf_op jit(solution)/shard_map/ppermute | solution.py:895
  448.6 38.2 %collective-permute-start.46 = (bf16[1,8,256,256]{3,2,1,0:T(8,128)(2,1)}, bf16[1,8,256,256]{3,2,1,0:T(8,128)(2,1)S(1)}, u32[]{:S(2)}, u32[]{:S(2)}) collective-permute-start(bf16[1,8,256,256]{3,2,1,0:T(8,128)(2,1)} %get-tuple-element.474), channel_id=1, source_target_pairs={{0,2},{2,0},{4,6},{6,4},{8,10},{10,8},{12,14},{14,12},{16,18},{18,... | collective-permute-start | bytes 3145736 | tf_op jit(solution)/shard_map/ppermute | solution.py:895
  470.9 53.0 %collective-permute-start.49 = (bf16[128,5632]{1,0:T(8,128)(2,1)S(1)}, bf16[128,5632]{1,0:T(8,128)(2,1)S(1)}, u32[]{:S(2)}, u32[]{:S(2)}) collective-permute-start(bf16[128,5632]{1,0:T(8,128)(2,1)S(1)} %copy-done.67), channel_id=1, source_target_pairs={{0,4},{2,6},{4,0},{6,2},{8,12},{10,14},{12,8},{14,10},{16,20},{18,... | collective-permute-start | bytes 4325384 | tf_op jit(solution)/shard_map/ppermute | solution.py:895
  485.5 86.5 %collective-permute-start.61 = (bf16[16,64,256]{2,1,0:T(8,128)(2,1)S(1)}, bf16[16,64,256]{2,1,0:T(8,128)(2,1)S(1)}, u32[]{:S(2)}, u32[]{:S(2)}) collective-permute-start(bf16[16,64,256]{2,1,0:T(8,128)(2,1)S(1)} %pad_maximum_fusion.20), channel_id=1, source_target_pairs={{0,1},{1,0},{2,3},{3,2},{4,5},{5,4},{6,7},{7,6},{8,9},{9,8},{10,11... | collective-permute-start | bytes 1572872 | tf_op jit(solution)/shard_map/ppermute | solution.py:892
  486.8 52.4 %collective-permute-start.55 = (bf16[64,2176]{1,0:T(8,128)(2,1)S(1)}, bf16[64,2176]{1,0:T(8,128)(2,1)S(1)}, u32[]{:S(2)}, u32[]{:S(2)}) collective-permute-start(bf16[64,2176]{1,0:T(8,128)(2,1)S(1)} %get-tuple-element.489), channel_id=1, source_target_pairs={{0,8},{2,10},{4,12},{6,14},{8,0},{10,2},{12,4},{14,6},{16,24},{18,... | collective-permute-start | bytes 835592 | tf_op jit(solution)/shard_map/ppermute | solution.py:895
  491.1 30.9 %collective-permute-start.47 = (bf16[1,4,256,256]{3,2,1,0:T(8,128)(2,1)S(1)}, bf16[1,4,256,256]{3,2,1,0:T(8,128)(2,1)S(1)}, u32[]{:S(2)}, u32[]{:S(2)}) collective-permute-start(bf16[1,4,256,256]{3,2,1,0:T(8,128)(2,1)S(1)} %get-tuple-element.493), channel_id=1, source_target_pairs={{0,4},{2,6},{4,0},{6,2},{8,12},{10,14},{12,8},{14,10},{16,20},{18,... | collective-permute-start | bytes 1572872 | tf_op jit(solution)/shard_map/ppermute | solution.py:895
  525.4 59.5 %collective-permute-start.64 = (bf16[64,3840]{1,0:T(8,128)(2,1)S(1)}, bf16[64,3840]{1,0:T(8,128)(2,1)S(1)}, u32[]{:S(2)}, u32[]{:S(2)}) collective-permute-start(bf16[64,3840]{1,0:T(8,128)(2,1)S(1)} %get-tuple-element.482), channel_id=1, source_target_pairs={{0,4},{2,6},{4,0},{6,2},{8,12},{10,14},{12,8},{14,10},{16,20},{18,... | collective-permute-start | bytes 1474568 | tf_op jit(solution)/shard_map/ppermute | solution.py:895
  536.7 51.3 %collective-permute-start.63 = (bf16[64,5632]{1,0:T(8,128)(2,1)S(1)}, bf16[64,5632]{1,0:T(8,128)(2,1)S(1)}, u32[]{:S(2)}, u32[]{:S(2)}) collective-permute-start(bf16[64,5632]{1,0:T(8,128)(2,1)S(1)} %get-tuple-element.464), channel_id=1, source_target_pairs={{0,8},{2,10},{4,12},{6,14},{8,0},{10,2},{12,4},{14,6},{16,24},{18,... | collective-permute-start | bytes 2162696 | tf_op jit(solution)/shard_map/ppermute | solution.py:895
  536.9 24.0 %collective-permute-start.56 = (bf16[1,2,256,256]{3,2,1,0:T(8,128)(2,1)S(1)}, bf16[1,2,256,256]{3,2,1,0:T(8,128)(2,1)S(1)}, u32[]{:S(2)}, u32[]{:S(2)}) collective-permute-start(bf16[1,2,256,256]{3,2,1,0:T(8,128)(2,1)S(1)} %get-tuple-element.518), channel_id=1, source_target_pairs={{0,8},{2,10},{4,12},{6,14},{8,0},{10,2},{12,4},{14,6},{16,24},{18,... | collective-permute-start | bytes 786440 | tf_op jit(solution)/shard_map/ppermute | solution.py:895
  584.8 23.1 %collective-permute-start.62 = (bf16[256,2176]{1,0:T(8,128)(2,1)S(1)}, bf16[256,2176]{1,0:T(8,128)(2,1)S(1)}, u32[]{:S(2)}, u32[]{:S(2)}) collective-permute-start(bf16[256,2176]{1,0:T(8,128)(2,1)S(1)} %get-tuple-element.426), channel_id=1, source_target_pairs={{0,2},{2,0},{4,6},{6,4},{8,10},{10,8},{12,14},{14,12},{16,18},{18,... | collective-permute-start | bytes 3342344 | tf_op jit(solution)/shard_map/ppermute | solution.py:895
  588.1 34.6 %collective-permute-start.73 = (bf16[32,5632]{1,0:T(8,128)(2,1)S(1)}, bf16[32,5632]{1,0:T(8,128)(2,1)S(1)}, u32[]{:S(2)}, u32[]{:S(2)}) collective-permute-start(bf16[32,5632]{1,0:T(8,128)(2,1)S(1)} %add_convert_fusion.32), channel_id=1, source_target_pairs={{0,16},{2,18},{4,20},{6,22},{8,24},{10,26},{12,28},{14,30},{16,0},... | collective-permute-start | bytes 1081352 | tf_op jit(solution)/shard_map/ppermute | solution.py:895
  (149 other events, 1652.4 us)

commit v4 on v3

--- a/solution.py
+++ b/solution.py
@@ -791,16 +791,11 @@
 
 
 class HalvingSum:
-    def __init__(self, trade, pair, order, begin=True):
+    def __init__(self, trade, pair, order):
         self.trade, self.order, self.step = trade, order, 1
         self.kept, self.sent = pair
-        self.got = self.result = None
-        if begin:
-            self.got = trade(self.sent, order[0])
-
-    def advance_first(self, gate):
-        (self.kept, self.sent), _ = lax.optimization_barrier(((self.kept, self.sent), gate))
-        self.got = self.trade(self.sent, self.order[0])
+        self.got = trade(self.sent, order[0])
+        self.result = None
 
     def advance(self, gate=None):
         if self.result is not None:
@@ -824,6 +819,8 @@
 
 
 class SlotSum:
+    result = None
+
     def __init__(self, trade, value, order):
         self.trade, self.value, self.order, self.step = trade, value, order, 0
         self.send()
@@ -1057,7 +1054,7 @@
             return [late.sent for late in d_lat]
 
         def sents_of(sums):
-            return [one.sent for one in sums]
+            return [one.sent if one.result is None else one.result for one in sums]
 
         def wide_sums(back_other, gate):
             backs = (back_own, back_other)
@@ -1092,13 +1089,13 @@
             d_in_own = turned(d_in_own.astype(BF16)).astype(F32)
             hidden_other = saved[layer][12]
             grad_other, _ = project_back(*after(other_input, back_own[3]), layer + 1)
-            back_other = other_back(back_own[3])
+            back_other = other_back((back_own[3], pending[2].sent))
             for late in pending[:2]:
                 late.advance(back_other[3])
-            sums = wide_sums(back_other, (sents_of(pending[:2]), d_in_own))
-            pending[2].advance_first([sums[0].kept, sums[1].kept])
+            pending[2].advance(back_other[3])
+            sums = wide_sums(back_other, (sents_of(pending), d_in_own))
             for late in pending[:2]:
-                late.advance(pending[2].sent)
+                late.advance([sums[0].kept, sums[1].kept])
             for one in sums:
                 one.advance(sents_of(pending[:2]))
             d_heads_t = after(d_heads_t, sents_of(sums + pending))
@@ -1116,7 +1113,7 @@
             )
             up_k.append(up_k_one)
             up_v.append(up_v_one)
-            for late in pending + d_lat:
+            for late in (pending if group == 0 else []) + d_lat:
                 late.advance(up_k_one)
             d_lat.append(SlotSum(trade, d_lat_one, bits))
             sents = sents_of(pending + d_lat)
@@ -1152,18 +1149,19 @@
                 one.advance(sents)
             stepped(sents_of(sums))
         else:
+            pending[2].advance(up_k[-1])
+            sents = stepped(up_k[-1])
+            for one in sums:
+                one.advance(sents)
+            dq, up_sent = after((dq, up_sent), sents_of(sums))
             dq = turned(dq)
             up_got = across(up_sent)
-            sents = stepped(up_sent)
-            for one in sums:
-                one.advance(sents)
             sents = stepped(sents_of(sums))
             dq = after(dq, sents)
             dq_other = across(dq)
             pending[2].advance(sents)
-            sents = stepped(pending[2].sent)
+            sents = stepped(None)
             up_got = after(up_got, sents)
-            pending[2].advance(sents)
         while any(late.got is not None for late in d_lat):
             stepped(None)
         d_lat = jnp.concatenate([late.value.reshape(toks, size) for late in d_lat], axis=1)
@@ -1196,11 +1194,15 @@
             dot_as(pick, vectors.astype(BF16), NT) + dot_as(pick_other, vectors_other.astype(BF16), NT)
         ).astype(BF16)
         terms = [(normed, [dq, dq_other]), (normed, [d_lat, d_lat_other])]
-        rest = HalvingSum(trade, pair_sum(terms, [up_rows, vectors]), bits, begin=not last)
+        rest = HalvingSum(trade, pair_sum(terms, [up_rows, vectors]), bits)
         if not last:
             sums[1].advance(rest.sent)
             sums[0].advance(sums[1].sent)
-            rest.advance(sums[0].sent)
+            for _ in bits[1:]:
+                rest.advance(sums[0].sent)
+            for one in (sums[1], sums[0]):
+                while one.result is None:
+                    one.advance(rest.sent)
         sums.append(rest)
         pending = sums
         layer_sums.insert(0, sums)

time: 646 us -> 607 us (0.940)
  waiting for transfers between devices: 207 us -> 181 us
  starting transfers between devices: 77 us -> 65.2 us
    ppermute x56, waiting for transfers between devices: 176 us -> 140 us  [trade(): lax.ppermute(value, 'seq', [(at, at ^ bit) for at in range(seq_count)])]
    ppermute x56, starting transfers between devices: 55.6 us -> 48 us  [trade(): lax.ppermute(value, 'seq', [(at, at ^ bit) for at in range(seq_count)])]
    ppermute x7, waiting for transfers between devices: 21.6 us -> 28.3 us  [swap_ends(): return lax.ppermute(value, 'seq', moves)]
    unnamed x206 -> x200, local copies, waits for them, and re-layouts: 18.8 us -> 18.3 us
  transfers between devices with their start and end apart: 75 -> 75, of which waited for: 29 -> 31; matrix products, arithmetic and copies ran while one was open for 14% -> 15% of each run, Pallas kernels for 38% -> 40%
where the time goes in v4:
time: 607 us; the launch traced here: 603 us
  Pallas kernels  246 us (41%)
  waiting for transfers between devices  181 us (30%)
  starting transfers between devices  65.2 us (11%)
  other arithmetic  45 us (7%)
  local copies, waits for them, and re-layouts  31.7 us (5%)
  matrix products  30.7 us (5%)
    ppermute x56, waiting for transfers between devices, trade(): lax.ppermute(value, 'seq', [(at, at ^ bit) for at in range(seq_count)])  140 us
    pallas_call x4, Pallas kernels, attend_back(): pl.pallas_call(functools.partial(attend_back_kernel, seq_count=seq_count,...  83.8 us
    pallas_call x4, Pallas kernels, attend(): pl.pallas_call(functools.partial(attend_kernel, seq_count=seq_count, half...  60.7 us
    ppermute x56, starting transfers between devices, trade(): lax.ppermute(value, 'seq', [(at, at ^ bit) for at in range(seq_count)])  48 us
    pallas_call x4, Pallas kernels, feed_back(): pl.pallas_call(functools.partial(feed_back_kernel, layer=layer, hidden=hi...  46.9 us
    pallas_call x4, Pallas kernels, feed(): pl.pallas_call(functools.partial(feed_kernel, layer=layer, hidden=hidden)...  36.6 us
    ppermute x7, waiting for transfers between devices, swap_ends(): return lax.ppermute(value, 'seq', moves)  28.3 us
    dot_general x26, matrix products, dot_as(): return lax.dot_general(left, right, dims, preferred_element_type=F32)  23.3 us
  transfers between devices with their start and end apart: 75, of which 31 were waited for; matrix products, arithmetic and copies ran while one was open for 15% of the time, Pallas kernels for 40%

profile of v4, /device:TPU:0, one launch (start us, length us, event | category | flops | bytes accessed | tf_op | source)
XLA Modules:
  0.0 603.0 jit_solution(12999276465393721375)
XLA Ops:
  62.3 15.2 %attend.4 = (bf16[1,2,128,1024]{3,2,1,0:T(8,128)(2,1)S(1)}, bf16[1,2,512,128]{3,2,1,0:T(8,128)(2,1)}, f32[1,2,1,1024]{3,2,1,0:T(1,128)}, bf16[1,2,1024,256]{3,2,1,0:T(8,128)(2,1)}, bf16[1,2,256,1024]{3,2,1,0:T(8,128)(2,1)}) custom-call(s32[35]{0:T(128)S(1)} %add_add_fusion.1.scalars, bf16[1,2,1024,128]{3,2,1,0:T(8,128)(2,1)S(1)} %fusion.57.q_ref, ...), custom_call_target="tpu_custom_call" | custom-call | flops 4294967296 | bytes 4194304 | tf_op jit(solution)/shard_map/attend/pallas_call | solution.py:260
  81.8 15.2 %attend.5 = (bf16[1,2,128,1024]{3,2,1,0:T(8,128)(2,1)S(1)}, bf16[1,2,512,128]{3,2,1,0:T(8,128)(2,1)}, f32[1,2,1,1024]{3,2,1,0:T(1,128)}, bf16[1,2,1024,256]{3,2,1,0:T(8,128)(2,1)}, bf16[1,2,256,1024]{3,2,1,0:T(8,128)(2,1)}) custom-call(s32[35]{0:T(128)S(1)} %add_add_fusion.1.scalars, ...), custom_call_target="tpu_custom_call", output_to_operand_aliasing={{0}: (5, {})} | custom-call | flops 4294967296 | bytes 4194304 | tf_op jit(solution)/shard_map/attend/pallas_call | solution.py:260
  98.5 8.7 %feed.4 = (f32[256,1024]{1,0:T(8,128)S(1)}, bf16[256,1024]{1,0:T(8,128)(2,1)S(1)}, bf16[256,2816]{1,0:T(8,128)(2,1)S(1)}, bf16[256,2816]{1,0:T(8,128)(2,1)S(1)},...) custom-call(bf16[256,1024]{1,0:T(8,128)(2,1)S(1)} %bitcast.356, ...), custom_call_target="tpu_custom_call" | custom-call | flops 4966055936 | bytes 23724032 | tf_op jit(solution)/shard_map/feed/pallas_call | solution.py:504
  113.2 8.8 %feed.5 = (f32[256,1024]{1,0:T(8,128)S(1)}, bf16[256,1024]{1,0:T(8,128)(2,1)S(1)}, bf16[256,2816]{1,0:T(8,128)(2,1)S(1)}, bf16[256,2816]{1,0:T(8,128)(2,1)S(1)},...) custom-call(bf16[256,1024]{1,0:T(8,128)(2,1)S(1)} %collective-permute-done.12.heads.refs_7_, ...), custom_call_target="tpu_custom_call" | custom-call | flops 4966055936 | bytes 23724032 | tf_op jit(solution)/shard_map/feed/pallas_call | solution.py:504
  137.0 9.6 %collective-permute-done.17 = bf16[1,4,256,256]{3,2,1,0:T(8,128)(2,1)S(1)} collective-permute-done((bf16[1,4,256,256]{3,2,1,0:T(8,128)(2,1)S(1)}, bf16[1,4,256,256]{3,2,1,0:T(8,128)(2,1)S(1)}, u32[]{:S(2)}, u32[]{:S(2)}) %collective-permute-start.17) | collective-permute-done | bytes 524320 | tf_op jit(solution)/shard_map/ppermute | solution.py:892
  156.8 15.1 %attend.6 = (bf16[1,2,128,1024]{3,2,1,0:T(8,128)(2,1)}, bf16[1,2,512,128]{3,2,1,0:T(8,128)(2,1)}, f32[1,2,1,1024]{3,2,1,0:T(1,128)}, bf16[1,2,1024,256]{3,2,1,0:T(8,128)(2,1)}, bf16[1,2,256,1024]{3,2,1,0:T(8,128)(2,1)}) custom-call(s32[35]{0:T(128)S(1)} %add_add_fusion.scalars, bf16[1,2,1024,128]{3,2,1,0:T(8,128)(2,1)S(1)} %fusion.54.q_ref, ...), custom_call_target="tpu_custom_call" | custom-call | flops 4294967296 | bytes 4194304 | tf_op jit(solution)/shard_map/attend/pallas_call | solution.py:260
  172.9 15.1 %attend.7 = (bf16[1,2,128,1024]{3,2,1,0:T(8,128)(2,1)}, bf16[1,2,512,128]{3,2,1,0:T(8,128)(2,1)}, f32[1,2,1,1024]{3,2,1,0:T(1,128)}, bf16[1,2,1024,256]{3,2,1,0:T(8,128)(2,1)}, bf16[1,2,256,1024]{3,2,1,0:T(8,128)(2,1)}) custom-call(s32[35]{0:T(128)S(1)} %add_add_fusion.scalars, ...), custom_call_target="tpu_custom_call", output_to_operand_aliasing={{0}: (5, {})} | custom-call | flops 4294967296 | bytes 4194304 | tf_op jit(solution)/shard_map/attend/pallas_call | solution.py:260
  188.3 9.5 %feed.6 = (f32[256,1024]{1,0:T(8,128)S(1)}, bf16[256,1024]{1,0:T(8,128)(2,1)S(1)}, bf16[256,2816]{1,0:T(8,128)(2,1)S(1)}, bf16[256,2816]{1,0:T(8,128)(2,1)S(1)},...) custom-call(bf16[256,1024]{1,0:T(8,128)(2,1)} %bitcast.44.heads.refs_6_, ...), custom_call_target="tpu_custom_call" | custom-call | flops 4966055936 | bytes 23724032 | tf_op jit(solution)/shard_map/feed/pallas_call | solution.py:504
  201.7 11.6 %feed_back.4 = (bf16[256,2816]{1,0:T(8,128)(2,1)S(1)}, bf16[256,2816]{1,0:T(8,128)(2,1)S(1)}, bf16[256,1024]{1,0:T(8,128)(2,1)S(1)}, f32[256,1024]{1,0:T(8,128)S...) custom-call(f32[256,1024]{1,0:T(8,128)S(1)} %bitcast.335, ...), custom_call_target="tpu_custom_call" | custom-call | flops 4966055936 | bytes 25165824 | tf_op jit(solution)/shard_map/feed_back/pallas_call | solution.py:659
  217.4 20.9 %attend_back.4 = (bf16[1,2,128,1024]{3,2,1,0:T(8,128)(2,1)S(1)}, bf16[1,16,256,256]{3,2,1,0:T(8,128)(2,1)S(1)}, f32[512,256]{1,0:T(8,128)S(1)}, f32[512,256]{1,0:T(8,128)S(1)}) custom-call(s32[35]{0:T(128)S(1)} %add_add_fusion.scalars, bf16[1,2,1024,128]{3,2,1,0:T(8,128)(2,1)} %copy-done.49, bf16[1,2,1024,128]{3,2,1,0:T(8,128)(2,1)} %bitcast.371, ...), custom_call_target="tpu_custom_call" | custom-call | flops 10737418240 | bytes 7340032 | tf_op jit(solution)/shard_map/attend_back/pallas_call | solution.py:316
  241.2 9.2 %collective-permute-done.25 = bf16[1,128,1024]{2,1,0:T(8,128)(2,1)S(1)} collective-permute-done((bf16[1,128,1024]{2,1,0:T(8,128)(2,1)S(1)}, bf16[1,128,1024]{2,1,0:T(8,128)(2,1)S(1)}, u32[]{:S(2)}, u32[]{:S(2)}) %collective-permute-start.25) | collective-permute-done | bytes 262176 | tf_op jit(solution)/shard_map/ppermute | solution.py:886
  254.9 21.0 %attend_back.5 = (bf16[1,2,128,1024]{3,2,1,0:T(8,128)(2,1)S(1)}, bf16[1,16,256,256]{3,2,1,0:T(8,128)(2,1)S(1)}, f32[512,256]{1,0:T(8,128)S(1)}, f32[512,256]{1,0:T(8,128)S(1)}) custom-call(s32[35]{0:T(128)S(1)} %add_add_fusion.scalars, bf16[1,2,1024,128]{3,2,1,0:T(8,128)(2,1)} %copy-done.49, ...), custom_call_target="tpu_custom_call", output_to_operand_aliasing={{0}: (10, {})} | custom-call | flops 10737418240 | bytes 7340032 | tf_op jit(solution)/shard_map/attend_back/pallas_call | solution.py:316
  285.1 9.6 %feed.7 = (f32[256,1024]{1,0:T(8,128)S(1)}, bf16[256,1024]{1,0:T(8,128)(2,1)S(1)}, bf16[256,2816]{1,0:T(8,128)(2,1)S(1)}, bf16[256,2816]{1,0:T(8,128)(2,1)S(1)},...) custom-call(bf16[256,1024]{1,0:T(8,128)(2,1)S(1)} %copy-done.19, ...), custom_call_target="tpu_custom_call" | custom-call | flops 4966055936 | bytes 23724032 | tf_op jit(solution)/shard_map/feed/pallas_call | solution.py:504
  299.4 12.3 %feed_back.5 = (bf16[256,2816]{1,0:T(8,128)(2,1)S(1)}, bf16[256,2816]{1,0:T(8,128)(2,1)S(1)}, bf16[256,1024]{1,0:T(8,128)(2,1)S(1)}, f32[256,1024]{1,0:T(8,128)S...) custom-call(f32[256,1024]{1,0:T(8,128)S(1)} %bitcast.333, ...), custom_call_target="tpu_custom_call" | custom-call | flops 4966055936 | bytes 25165824 | tf_op jit(solution)/shard_map/feed_back/pallas_call | solution.py:659
  355.7 11.2 %feed_back.6 = (bf16[256,2816]{1,0:T(8,128)(2,1)S(1)}, bf16[256,2816]{1,0:T(8,128)(2,1)S(1)}, bf16[256,1024]{1,0:T(8,128)(2,1)S(1)}, f32[256,1024]{1,0:T(8,128)S...) custom-call(f32[256,1024]{1,0:T(8,128)S(1)} %multiply_add_fusion.1.g, ...), custom_call_target="tpu_custom_call" | custom-call | flops 4966055936 | bytes 25165824 | tf_op jit(solution)/shard_map/feed_back/pallas_call | solution.py:659
  376.9 11.8 %feed_back.7 = (bf16[256,2816]{1,0:T(8,128)(2,1)S(1)}, bf16[256,2816]{1,0:T(8,128)(2,1)S(1)}, bf16[256,1024]{1,0:T(8,128)(2,1)S(1)}, f32[256,1024]{1,0:T(8,128)}...) custom-call(f32[256,1024]{1,0:T(8,128)S(1)} %multiply_add_fusion.gra, ...), custom_call_target="tpu_custom_call" | custom-call | flops 4966055936 | bytes 25165824 | tf_op jit(solution)/shard_map/feed_back/pallas_call | solution.py:659
  407.1 11.2 %collective-permute-done.42 = bf16[64,5632]{1,0:T(8,128)(2,1)S(1)} collective-permute-done((bf16[64,5632]{1,0:T(8,128)(2,1)S(1)}, bf16[64,5632]{1,0:T(8,128)(2,1)S(1)}, u32[]{:S(2)}, u32[]{:S(2)}) %collective-permute-start.42) | collective-permute-done | bytes 720928 | tf_op jit(solution)/shard_map/ppermute | solution.py:892
  423.8 20.9 %attend_back.6 = (bf16[1,2,128,1024]{3,2,1,0:T(8,128)(2,1)S(1)}, bf16[1,16,256,256]{3,2,1,0:T(8,128)(2,1)S(1)}, f32[512,256]{1,0:T(8,128)S(1)}, f32[512,256]{1,0:T(8,128)S(1)}) custom-call(s32[35]{0:T(128)S(1)} %copy-done.30, bf16[1,2,1024,128]{3,2,1,0:T(8,128)(2,1)} %copy-done.55, bf16[1,2,1024,128]{3,2,1,0:T(8,128)(2,1)} %bitcast.369, ...), custom_call_target="tpu_custom_call" | custom-call | flops 10737418240 | bytes 7340032 | tf_op jit(solution)/shard_map/attend_back/pallas_call | solution.py:316
  447.2 21.0 %attend_back.7 = (bf16[1,2,128,1024]{3,2,1,0:T(8,128)(2,1)S(1)}, bf16[1,16,256,256]{3,2,1,0:T(8,128)(2,1)S(1)}, f32[512,256]{1,0:T(8,128)S(1)}, f32[512,256]{1,0:T(8,128)S(1)}) custom-call(s32[35]{0:T(128)S(1)} %copy-done.30, bf16[1,2,1024,128]{3,2,1,0:T(8,128)(2,1)} %copy-done.55, ...), custom_call_target="tpu_custom_call", output_to_operand_aliasing={{0}: (10, {})} | custom-call | flops 10737418240 | bytes 7340032 | tf_op jit(solution)/shard_map/attend_back/pallas_call | solution.py:316
  478.5 12.3 %collective-permute-done.50 = bf16[1,4,256,256]{3,2,1,0:T(8,128)(2,1)S(1)} collective-permute-done((bf16[1,4,256,256]{3,2,1,0:T(8,128)(2,1)S(1)}, bf16[1,4,256,256]{3,2,1,0:T(8,128)(2,1)S(1)}, u32[]{:S(2)}, u32[]{:S(2)}) %collective-permute-start.50) | collective-permute-done | bytes 524320 | tf_op jit(solution)/shard_map/ppermute | solution.py:892
  502.9 15.7 %collective-permute-done.53 = bf16[1,128,1024]{2,1,0:T(8,128)(2,1)S(1)} collective-permute-done((bf16[1,128,1024]{2,1,0:T(8,128)(2,1)S(1)}, bf16[1,128,1024]{2,1,0:T(8,128)(2,1)S(1)}, u32[]{:S(2)}, u32[]{:S(2)}) %collective-permute-start.53) | collective-permute-done | bytes 262176 | tf_op jit(solution)/shard_map/ppermute | solution.py:886
  542.0 8.2 %collective-permute-done.61.refs_7_ = bf16[256,512]{1,0:T(8,128)(2,1)S(1)} collective-permute-done((bf16[256,512]{1,0:T(8,128)(2,1)S(1)}, bf16[256,512]{1,0:T(8,128)(2,1)S(1)}, u32[]{:S(2)}, u32[]{:S(2)}) %collective-permute-start.61) | collective-permute-done | bytes 262176 | tf_op jit(solution)/shard_map/ppermute | solution.py:889
  558.8 10.1 %collective-permute-done.66 = bf16[128,2176]{1,0:T(8,128)(2,1)S(1)} collective-permute-done((bf16[128,2176]{1,0:T(8,128)(2,1)S(1)}, bf16[128,2176]{1,0:T(8,128)(2,1)S(1)}, u32[]{:S(2)}, u32[]{:S(2)}) %collective-permute-start.66) | collective-permute-done | bytes 557088 | tf_op jit(solution)/shard_map/ppermute | solution.py:892
  570.8 19.0 %collective-permute-done.67 = bf16[64,2176]{1,0:T(8,128)(2,1)S(1)} collective-permute-done((bf16[64,2176]{1,0:T(8,128)(2,1)S(1)}, bf16[64,2176]{1,0:T(8,128)(2,1)S(1)}, u32[]{:S(2)}, u32[]{:S(2)}) %collective-permute-start.67) | collective-permute-done | bytes 278560 | tf_op jit(solution)/shard_map/ppermute | solution.py:892
  (565 shorter events, 276.5 us)
Async XLA Ops:
  33.0 23.9 %collective-permute-start.6 = (bf16[1,4,256,256]{3,2,1,0:T(8,128)(2,1)S(1)}, bf16[1,4,256,256]{3,2,1,0:T(8,128)(2,1)}, u32[]{:S(2)}, u32[]{:S(2)}) collective-permute-start(bf16[1,4,256,256]{3,2,1,0:T(8,128)(2,1)S(1)} %pad_maximum_fusion.11), channel_id=1, source_target_pairs={{0,4},{2,6},{4,0},{6,2},{8,12},{10,14},{12,8},{14,10},{16,20},{18,... | collective-permute-start | bytes 1572872 | tf_op jit(solution)/shard_map/ppermute | solution.py:892
  188.1 95.2 %collective-permute-start.24 = (bf16[256,1024]{1,0:T(8,128)(2,1)}, bf16[256,1024]{1,0:T(8,128)(2,1)S(1)}, u32[]{:S(2)}, u32[]{:S(2)}) collective-permute-start(bf16[256,1024]{1,0:T(8,128)(2,1)} %bitcast.44.heads.refs_6_), channel_id=1, source_target_pairs={{0,1},{1,0},{2,3},{3,2},{4,5},{5,4},{6,7},{7,6},{8,9},{9,8},{10,11... | collective-permute-start | bytes 1572872 | tf_op jit(solution)/shard_map/ppermute | solution.py:889
  240.7 39.5 %collective-permute-start.22 = (bf16[1,8,256,256]{3,2,1,0:T(8,128)(2,1)}, bf16[1,8,256,256]{3,2,1,0:T(8,128)(2,1)}, u32[]{:S(2)}, u32[]{:S(2)}) collective-permute-start(bf16[1,8,256,256]{3,2,1,0:T(8,128)(2,1)} %get-tuple-element.484), channel_id=1, source_target_pairs={{0,2},{2,0},{4,6},{6,4},{8,10},{10,8},{12,14},{14,12},{16,18},{18,... | collective-permute-start | bytes 3145736 | tf_op jit(solution)/shard_map/ppermute | solution.py:892
  278.1 34.8 %collective-permute-start.31 = (bf16[16,64,256]{2,1,0:T(8,128)(2,1)}, bf16[16,64,256]{2,1,0:T(8,128)(2,1)S(1)}, u32[]{:S(2)}, u32[]{:S(2)}) collective-permute-start(bf16[16,64,256]{2,1,0:T(8,128)(2,1)} %pad_maximum_fusion.16), channel_id=1, source_target_pairs={{0,1},{1,0},{2,3},{3,2},{4,5},{5,4},{6,7},{7,6},{8,9},{9,8},{10,11... | collective-permute-start | bytes 1572872 | tf_op jit(solution)/shard_map/ppermute | solution.py:889
  318.4 24.7 %collective-permute-start.35 = (bf16[256,3840]{1,0:T(8,128)(2,1)S(1)}, bf16[256,3840]{1,0:T(8,128)(2,1)}, u32[]{:S(2)}, u32[]{:S(2)}) collective-permute-start(bf16[256,3840]{1,0:T(8,128)(2,1)S(1)} %get-tuple-element.327), channel_id=1, source_target_pairs={{0,2},{2,0},{4,6},{6,4},{8,10},{10,8},{12,14},{14,12},{16,18},{18,... | collective-permute-start | bytes 5898248 | tf_op jit(solution)/shard_map/ppermute | solution.py:892
  346.1 42.6 %collective-permute-start.39 = (bf16[128,3840]{1,0:T(8,128)(2,1)}, bf16[128,3840]{1,0:T(8,128)(2,1)}, u32[]{:S(2)}, u32[]{:S(2)}) collective-permute-start(bf16[128,3840]{1,0:T(8,128)(2,1)} %get-tuple-element.470), channel_id=1, source_target_pairs={{0,8},{2,10},{4,12},{6,14},{8,0},{10,2},{12,4},{14,6},{16,24},{18,... | collective-permute-start | bytes 2949128 | tf_op jit(solution)/shard_map/ppermute | solution.py:892
  352.0 41.7 %collective-permute-start.38 = (bf16[128,5632]{1,0:T(8,128)(2,1)}, bf16[128,5632]{1,0:T(8,128)(2,1)}, u32[]{:S(2)}, u32[]{:S(2)}) collective-permute-start(bf16[128,5632]{1,0:T(8,128)(2,1)} %get-tuple-element.466), channel_id=1, source_target_pairs={{0,4},{2,6},{4,0},{6,2},{8,12},{10,14},{12,8},{14,10},{16,20},{18,... | collective-permute-start | bytes 4325384 | tf_op jit(solution)/shard_map/ppermute | solution.py:892
  367.6 23.2 %collective-permute-start.36 = (bf16[1,128,1024]{2,1,0:T(8,128)(2,1)S(1)}, bf16[1,128,1024]{2,1,0:T(8,128)(2,1)S(1)}, u32[]{:S(2)}, u32[]{:S(2)}) collective-permute-start(bf16[1,128,1024]{2,1,0:T(8,128)(2,1)S(1)} %get-tuple-element.528), channel_id=1, source_target_pairs={{0,30},{2,28},{4,26},{6,24},{8,22},{10,20},{12,18},{14,16},{16,14}... | collective-permute-start | bytes 786440 | tf_op jit(solution)/shard_map/ppermute | solution.py:886
  392.3 52.4 %collective-permute-start.47 = (bf16[128,2176]{1,0:T(8,128)(2,1)S(1)}, bf16[128,2176]{1,0:T(8,128)(2,1)}, u32[]{:S(2)}, u32[]{:S(2)}) collective-permute-start(bf16[128,2176]{1,0:T(8,128)(2,1)S(1)} %get-tuple-element.478), channel_id=1, source_target_pairs={{0,4},{2,6},{4,0},{6,2},{8,12},{10,14},{12,8},{14,10},{16,20},{18,... | collective-permute-start | bytes 1671176 | tf_op jit(solution)/shard_map/ppermute | solution.py:892
  395.5 22.8 %collective-permute-start.42 = (bf16[64,5632]{1,0:T(8,128)(2,1)S(1)}, bf16[64,5632]{1,0:T(8,128)(2,1)S(1)}, u32[]{:S(2)}, u32[]{:S(2)}) collective-permute-start(bf16[64,5632]{1,0:T(8,128)(2,1)S(1)} %get-tuple-element.474), channel_id=1, source_target_pairs={{0,8},{2,10},{4,12},{6,14},{8,0},{10,2},{12,4},{14,6},{16,24},{18,... | collective-permute-start | bytes 2162696 | tf_op jit(solution)/shard_map/ppermute | solution.py:892
  404.4 41.4 %collective-permute-start.46 = (bf16[32,3840]{1,0:T(8,128)(2,1)S(1)}, bf16[32,3840]{1,0:T(8,128)(2,1)S(1)}, u32[]{:S(2)}, u32[]{:S(2)}) collective-permute-start(bf16[32,3840]{1,0:T(8,128)(2,1)S(1)} %get-tuple-element.514), channel_id=1, source_target_pairs={{0,16},{2,18},{4,20},{6,22},{8,24},{10,26},{12,28},{14,30},{16,0},... | collective-permute-start | bytes 737288 | tf_op jit(solution)/shard_map/ppermute | solution.py:892
  418.5 50.0 %collective-permute-start.45 = (bf16[32,5632]{1,0:T(8,128)(2,1)S(1)}, bf16[32,5632]{1,0:T(8,128)(2,1)S(1)}, u32[]{:S(2)}, u32[]{:S(2)}) collective-permute-start(bf16[32,5632]{1,0:T(8,128)(2,1)S(1)} %get-tuple-element.496), channel_id=1, source_target_pairs={{0,16},{2,18},{4,20},{6,22},{8,24},{10,26},{12,28},{14,30},{16,0},... | collective-permute-start | bytes 1081352 | tf_op jit(solution)/shard_map/ppermute | solution.py:892
  420.0 71.4 %collective-permute-start.52 = (bf16[128,3840]{1,0:T(8,128)(2,1)}, bf16[128,3840]{1,0:T(8,128)(2,1)}, u32[]{:S(2)}, u32[]{:S(2)}) collective-permute-start(bf16[128,3840]{1,0:T(8,128)(2,1)} %get-tuple-element.468), channel_id=1, source_target_pairs={{0,8},{2,10},{4,12},{6,14},{8,0},{10,2},{12,4},{14,6},{16,24},{18,... | collective-permute-start | bytes 2949128 | tf_op jit(solution)/shard_map/ppermute | solution.py:892
  422.8 68.7 %collective-permute-start.48 = (bf16[128,5632]{1,0:T(8,128)(2,1)S(1)}, bf16[128,5632]{1,0:T(8,128)(2,1)S(1)}, u32[]{:S(2)}, u32[]{:S(2)}) collective-permute-start(bf16[128,5632]{1,0:T(8,128)(2,1)S(1)} %get-tuple-element.464), channel_id=1, source_target_pairs={{0,4},{2,6},{4,0},{6,2},{8,12},{10,14},{12,8},{14,10},{16,20},{18,... | collective-permute-start | bytes 4325384 | tf_op jit(solution)/shard_map/ppermute | solution.py:892
  445.8 28.6 %collective-permute-start.49 = (bf16[1,8,256,256]{3,2,1,0:T(8,128)(2,1)}, bf16[1,8,256,256]{3,2,1,0:T(8,128)(2,1)}, u32[]{:S(2)}, u32[]{:S(2)}) collective-permute-start(bf16[1,8,256,256]{3,2,1,0:T(8,128)(2,1)} %get-tuple-element.482), channel_id=1, source_target_pairs={{0,2},{2,0},{4,6},{6,4},{8,10},{10,8},{12,14},{14,12},{16,18},{18,... | collective-permute-start | bytes 3145736 | tf_op jit(solution)/shard_map/ppermute | solution.py:892
  447.1 23.9 %collective-permute-start.70 = (bf16[64,2176]{1,0:T(8,128)(2,1)S(1)}, bf16[64,2176]{1,0:T(8,128)(2,1)}, u32[]{:S(2)}, u32[]{:S(2)}) collective-permute-start(bf16[64,2176]{1,0:T(8,128)(2,1)S(1)} %get-tuple-element.500), channel_id=1, source_target_pairs={{0,8},{2,10},{4,12},{6,14},{8,0},{10,2},{12,4},{14,6},{16,24},{18,... | collective-permute-start | bytes 835592 | tf_op jit(solution)/shard_map/ppermute | solution.py:892
  472.0 47.3 %collective-permute-start.71 = (bf16[32,2176]{1,0:T(8,128)(2,1)S(1)}, bf16[32,2176]{1,0:T(8,128)(2,1)S(1)}, u32[]{:S(2)}, u32[]{:S(2)}) collective-permute-start(bf16[32,2176]{1,0:T(8,128)(2,1)S(1)} %get-tuple-element.515), channel_id=1, source_target_pairs={{0,16},{2,18},{4,20},{6,22},{8,24},{10,26},{12,28},{14,30},{16,0},... | collective-permute-start | bytes 417800 | tf_op jit(solution)/shard_map/ppermute | solution.py:892
  477.8 24.3 %collective-permute-start.55 = (bf16[1,4,256,256]{3,2,1,0:T(8,128)(2,1)S(1)}, bf16[1,4,256,256]{3,2,1,0:T(8,128)(2,1)S(1)}, u32[]{:S(2)}, u32[]{:S(2)}) collective-permute-start(bf16[1,4,256,256]{3,2,1,0:T(8,128)(2,1)S(1)} %get-tuple-element.502), channel_id=1, source_target_pairs={{0,4},{2,6},{4,0},{6,2},{8,12},{10,14},{12,8},{14,10},{16,20},{18,... | collective-permute-start | bytes 1572872 | tf_op jit(solution)/shard_map/ppermute | solution.py:892
  492.8 58.5 %collective-permute-start.65 = (bf16[64,3840]{1,0:T(8,128)(2,1)S(1)}, bf16[64,3840]{1,0:T(8,128)(2,1)S(1)}, u32[]{:S(2)}, u32[]{:S(2)}) collective-permute-start(bf16[64,3840]{1,0:T(8,128)(2,1)S(1)} %get-tuple-element.490), channel_id=1, source_target_pairs={{0,4},{2,6},{4,0},{6,2},{8,12},{10,14},{12,8},{14,10},{16,20},{18,... | collective-permute-start | bytes 1474568 | tf_op jit(solution)/shard_map/ppermute | solution.py:892
  494.6 56.9 %collective-permute-start.64 = (bf16[64,5632]{1,0:T(8,128)(2,1)S(1)}, bf16[64,5632]{1,0:T(8,128)(2,1)S(1)}, u32[]{:S(2)}, u32[]{:S(2)}) collective-permute-start(bf16[64,5632]{1,0:T(8,128)(2,1)S(1)} %get-tuple-element.472), channel_id=1, source_target_pairs={{0,8},{2,10},{4,12},{6,14},{8,0},{10,2},{12,4},{14,6},{16,24},{18,... | collective-permute-start | bytes 2162696 | tf_op jit(solution)/shard_map/ppermute | solution.py:892
  518.5 22.3 %collective-permute-start.62 = (bf16[16,64,256]{2,1,0:T(8,128)(2,1)S(1)}, bf16[16,64,256]{2,1,0:T(8,128)(2,1)S(1)}, u32[]{:S(2)}, u32[]{:S(2)}) collective-permute-start(bf16[16,64,256]{2,1,0:T(8,128)(2,1)S(1)} %pad_maximum_fusion.19), channel_id=1, source_target_pairs={{0,1},{1,0},{2,3},{3,2},{4,5},{5,4},{6,7},{7,6},{8,9},{9,8},{10,11... | collective-permute-start | bytes 1572872 | tf_op jit(solution)/shard_map/ppermute | solution.py:889
  524.6 25.5 %collective-permute-start.60 = (bf16[256,1024]{1,0:T(8,128)(2,1)S(1)}, bf16[256,1024]{1,0:T(8,128)(2,1)S(1)}, u32[]{:S(2)}, u32[]{:S(2)}) collective-permute-start(bf16[256,1024]{1,0:T(8,128)(2,1)S(1)} %bitcast.337), channel_id=1, source_target_pairs={{0,1},{1,0},{2,3},{3,2},{4,5},{5,4},{6,7},{7,6},{8,9},{9,8},{10,11... | collective-permute-start | bytes 1572872 | tf_op jit(solution)/shard_map/ppermute | solution.py:889
  555.8 34.1 %collective-permute-start.73 = (bf16[32,3840]{1,0:T(8,128)(2,1)S(1)}, bf16[32,3840]{1,0:T(8,128)(2,1)S(1)}, u32[]{:S(2)}, u32[]{:S(2)}) collective-permute-start(bf16[32,3840]{1,0:T(8,128)(2,1)S(1)} %get-tuple-element.512), channel_id=1, source_target_pairs={{0,16},{2,18},{4,20},{6,22},{8,24},{10,26},{12,28},{14,30},{16,0},... | collective-permute-start | bytes 737288 | tf_op jit(solution)/shard_map/ppermute | solution.py:892
  555.9 34.1 %collective-permute-start.74 = (bf16[32,5632]{1,0:T(8,128)(2,1)S(1)}, bf16[32,5632]{1,0:T(8,128)(2,1)S(1)}, u32[]{:S(2)}, u32[]{:S(2)}) collective-permute-start(bf16[32,5632]{1,0:T(8,128)(2,1)S(1)} %get-tuple-element.494), channel_id=1, source_target_pairs={{0,16},{2,18},{4,20},{6,22},{8,24},{10,26},{12,28},{14,30},{16,0},... | collective-permute-start | bytes 1081352 | tf_op jit(solution)/shard_map/ppermute | solution.py:892
  (146 other events, 1630.0 us)

commit v5 on v4

--- a/solution.py
+++ b/solution.py
@@ -19,6 +19,7 @@
 BF16 = jnp.bfloat16
 KEY_BLOCK = 512
 QUERY_BLOCK = 1024
+FORWARD_QUERIES = 256
 FEED_STEP, FEED_AHEAD = 768, 16
 BACK_STEP, BACK_AHEAD = 1408, 6
 
@@ -104,22 +105,25 @@
     acc[...] = jnp.zeros_like(acc)
     bounds = block_bounds(scalars, row, part, half, seq_count)
     columns = heads * half
-    width = min(QUERY_BLOCK, columns)
+    width = min(FORWARD_QUERIES, columns)
 
     def block(block_at, edge):
         at = pl.multiple_of(block_at * KEY_BLOCK, KEY_BLOCK)
         key_rows = keys[pl.ds(at, KEY_BLOCK), :]
         key_cols = keys_t[:, pl.ds(at, KEY_BLOCK)]
-        for col in range(0, columns, width):
-            cols = slice(col, col + width)
+        parts = [slice(col, col + width) for col in range(0, columns, width)]
+        olds = [(top[:, cols], total[:, cols]) for cols in parts]
+
+        def scores_of(cols):
             scores = dot_as(key_rows, query_ref[0, 0, cols, :], NT)
-            if edge:
-                scores = hide(scores, block_at, bounds[0], bounds[1], half)
-            old_top = top[:, cols]
+            return hide(scores, block_at, bounds[0], bounds[1], half) if edge else scores
+
+        all_scores = [scores_of(cols) for cols in parts]
+        for cols, scores, (old_top, old_total) in zip(parts, all_scores, olds):
             new_top = jnp.maximum(old_top, jnp.max(scores, axis=0, keepdims=True))
             probs = jnp.exp2(scores - new_top)
             fade = jnp.exp2(old_top - new_top)
-            total[:, cols] = total[:, cols] * fade + jnp.sum(probs, axis=0, keepdims=True)
+            total[:, cols] = old_total * fade + jnp.sum(probs, axis=0, keepdims=True)
             top[:, cols] = new_top
             acc[:, cols] = acc[:, cols] * fade + dot(key_cols, probs.astype(BF16))
 
@@ -1156,8 +1160,7 @@
             dq, up_sent = after((dq, up_sent), sents_of(sums))
             dq = turned(dq)
             up_got = across(up_sent)
-            sents = stepped(sents_of(sums))
-            dq = after(dq, sents)
+            sents = stepped((sents_of(sums), dq))
             dq_other = across(dq)
             pending[2].advance(sents)
             sents = stepped(None)
@@ -1166,6 +1169,9 @@
             stepped(None)
         d_lat = jnp.concatenate([late.value.reshape(toks, size) for late in d_lat], axis=1)
         d_lat_other = across(d_lat)
+        if not last:
+            for one in (sums[1], sums[0]):
+                one.advance(d_lat)
         state = own if layer else natural_own.astype(F32)
         grad_own, attn_gain_own = project_back(d_in_own, dq, d_lat, state, layer)
         if last:
@@ -1196,10 +1202,8 @@
         terms = [(normed, [dq, dq_other]), (normed, [d_lat, d_lat_other])]
         rest = HalvingSum(trade, pair_sum(terms, [up_rows, vectors]), bits)
         if not last:
-            sums[1].advance(rest.sent)
-            sums[0].advance(sums[1].sent)
             for _ in bits[1:]:
-                rest.advance(sums[0].sent)
+                rest.advance(None)
             for one in (sums[1], sums[0]):
                 while one.result is None:
                     one.advance(rest.sent)

time: 607 us -> 596 us (0.982)
  waiting for transfers between devices: 181 us -> 170 us
  starting transfers between devices: 65.2 us -> 73.5 us
    ppermute x56, waiting for transfers between devices: 140 us -> 129 us  [trade(): lax.ppermute(value, 'seq', [(at, at ^ bit) for at in range(seq_count)])]
    ppermute x7, waiting for transfers between devices: 28.3 us -> 20.3 us  [swap_ends(): return lax.ppermute(value, 'seq', moves)]
    ppermute x56, starting transfers between devices: 48 us -> 55.4 us  [trade(): lax.ppermute(value, 'seq', [(at, at ^ bit) for at in range(seq_count)])]
    ppermute x12, waiting for transfers between devices: 13.3 us -> 20.7 us  [across(): lax.ppermute(value, 'rep', [(at, rep_count - 1 - at) for at in range(rep_...]
    pallas_call x4, Pallas kernels: 60.7 us -> 53.6 us  [attend(): pl.pallas_call(functools.partial(attend_kernel, seq_count=seq_count, half...]
    unnamed x200 -> x208, local copies, waits for them, and re-layouts: 18.3 us -> 20.4 us
  transfers between devices with their start and end apart: 75 -> 75, of which waited for: 31 -> 31; matrix products, arithmetic and copies ran while one was open for 15% -> 14% of each run, Pallas kernels for 40% -> 40%
where the time goes in v5:
time: 596 us; the launch traced here: 591 us
  Pallas kernels  240 us (40%)
  waiting for transfers between devices  170 us (29%)
  starting transfers between devices  73.5 us (12%)
  other arithmetic  40.7 us (7%)
  local copies, waits for them, and re-layouts  32.9 us (6%)
  matrix products  30.8 us (5%)
    ppermute x56, waiting for transfers between devices, trade(): lax.ppermute(value, 'seq', [(at, at ^ bit) for at in range(seq_count)])  129 us
    pallas_call x4, Pallas kernels, attend_back(): pl.pallas_call(functools.partial(attend_back_kernel, seq_count=seq_count,...  84.4 us
    ppermute x56, starting transfers between devices, trade(): lax.ppermute(value, 'seq', [(at, at ^ bit) for at in range(seq_count)])  55.4 us
    pallas_call x4, Pallas kernels, attend(): pl.pallas_call(functools.partial(attend_kernel, seq_count=seq_count, half...  53.6 us
    pallas_call x4, Pallas kernels, feed_back(): pl.pallas_call(functools.partial(feed_back_kernel, layer=layer, hidden=hi...  46.7 us
    pallas_call x4, Pallas kernels, feed(): pl.pallas_call(functools.partial(feed_kernel, layer=layer, hidden=hidden)...  37 us
    dot_general x26, matrix products, dot_as(): return lax.dot_general(left, right, dims, preferred_element_type=F32)  23.4 us
    ppermute x12, waiting for transfers between devices, across(): lax.ppermute(value, 'rep', [(at, rep_count - 1 - at) for at in range(rep_...  20.7 us
  transfers between devices with their start and end apart: 75, of which 31 were waited for; matrix products, arithmetic and copies ran while one was open for 14% of the time, Pallas kernels for 40%

profile of v5, /device:TPU:0, one launch (start us, length us, event | category | flops | bytes accessed | tf_op | source)
XLA Modules:
  0.0 591.3 jit_solution(10367004147559713520)
XLA Ops:
  62.2 13.5 %attend.4 = (bf16[1,2,128,1024]{3,2,1,0:T(8,128)(2,1)S(1)}, bf16[1,2,512,128]{3,2,1,0:T(8,128)(2,1)}, f32[1,2,1,1024]{3,2,1,0:T(1,128)}, bf16[1,2,1024,256]{3,2,1,0:T(8,128)(2,1)}, bf16[1,2,256,1024]{3,2,1,0:T(8,128)(2,1)}) custom-call(s32[35]{0:T(128)S(1)} %add_add_fusion.1.scalars, bf16[1,2,1024,128]{3,2,1,0:T(8,128)(2,1)S(1)} %fusion.60.q_ref, ...), custom_call_target="tpu_custom_call" | custom-call | flops 4294967296 | bytes 4194304 | tf_op jit(solution)/shard_map/attend/pallas_call | solution.py:264
  79.9 13.4 %attend.5 = (bf16[1,2,128,1024]{3,2,1,0:T(8,128)(2,1)S(1)}, bf16[1,2,512,128]{3,2,1,0:T(8,128)(2,1)}, f32[1,2,1,1024]{3,2,1,0:T(1,128)}, bf16[1,2,1024,256]{3,2,1,0:T(8,128)(2,1)}, bf16[1,2,256,1024]{3,2,1,0:T(8,128)(2,1)}) custom-call(s32[35]{0:T(128)S(1)} %add_add_fusion.1.scalars, ...), custom_call_target="tpu_custom_call", output_to_operand_aliasing={{0}: (5, {})} | custom-call | flops 4294967296 | bytes 4194304 | tf_op jit(solution)/shard_map/attend/pallas_call | solution.py:264
  94.9 9.2 %feed.4 = (f32[256,1024]{1,0:T(8,128)S(1)}, bf16[256,1024]{1,0:T(8,128)(2,1)S(1)}, bf16[256,2816]{1,0:T(8,128)(2,1)S(1)}, bf16[256,2816]{1,0:T(8,128)(2,1)S(1)},...) custom-call(bf16[256,1024]{1,0:T(8,128)(2,1)S(1)} %bitcast.358, ...), custom_call_target="tpu_custom_call" | custom-call | flops 4966055936 | bytes 23724032 | tf_op jit(solution)/shard_map/feed/pallas_call | solution.py:508
  110.1 8.8 %feed.5 = (f32[256,1024]{1,0:T(8,128)S(1)}, bf16[256,1024]{1,0:T(8,128)(2,1)S(1)}, bf16[256,2816]{1,0:T(8,128)(2,1)S(1)}, bf16[256,2816]{1,0:T(8,128)(2,1)S(1)},...) custom-call(bf16[256,1024]{1,0:T(8,128)(2,1)S(1)} %collective-permute-done.12.heads.refs_7_, ...), custom_call_target="tpu_custom_call" | custom-call | flops 4966055936 | bytes 23724032 | tf_op jit(solution)/shard_map/feed/pallas_call | solution.py:508
  134.6 8.8 %collective-permute-done.17 = bf16[1,4,256,256]{3,2,1,0:T(8,128)(2,1)S(1)} collective-permute-done((bf16[1,4,256,256]{3,2,1,0:T(8,128)(2,1)S(1)}, bf16[1,4,256,256]{3,2,1,0:T(8,128)(2,1)S(1)}, u32[]{:S(2)}, u32[]{:S(2)}) %collective-permute-start.17) | collective-permute-done | bytes 524320 | tf_op jit(solution)/shard_map/ppermute | solution.py:896
  153.7 13.4 %attend.6 = (bf16[1,2,128,1024]{3,2,1,0:T(8,128)(2,1)}, bf16[1,2,512,128]{3,2,1,0:T(8,128)(2,1)}, f32[1,2,1,1024]{3,2,1,0:T(1,128)}, bf16[1,2,1024,256]{3,2,1,0:T(8,128)(2,1)}, bf16[1,2,256,1024]{3,2,1,0:T(8,128)(2,1)}) custom-call(s32[35]{0:T(128)S(1)} %add_add_fusion.scalars, bf16[1,2,1024,128]{3,2,1,0:T(8,128)(2,1)S(1)} %fusion.57.q_ref, ...), custom_call_target="tpu_custom_call" | custom-call | flops 4294967296 | bytes 4194304 | tf_op jit(solution)/shard_map/attend/pallas_call | solution.py:264
  167.4 13.3 %attend.7 = (bf16[1,2,128,1024]{3,2,1,0:T(8,128)(2,1)}, bf16[1,2,512,128]{3,2,1,0:T(8,128)(2,1)}, f32[1,2,1,1024]{3,2,1,0:T(1,128)}, bf16[1,2,1024,256]{3,2,1,0:T(8,128)(2,1)}, bf16[1,2,256,1024]{3,2,1,0:T(8,128)(2,1)}) custom-call(s32[35]{0:T(128)S(1)} %add_add_fusion.scalars, ...), custom_call_target="tpu_custom_call", output_to_operand_aliasing={{0}: (5, {})} | custom-call | flops 4294967296 | bytes 4194304 | tf_op jit(solution)/shard_map/attend/pallas_call | solution.py:264
  181.0 9.5 %feed.6 = (f32[256,1024]{1,0:T(8,128)S(1)}, bf16[256,1024]{1,0:T(8,128)(2,1)S(1)}, bf16[256,2816]{1,0:T(8,128)(2,1)S(1)}, bf16[256,2816]{1,0:T(8,128)(2,1)S(1)},...) custom-call(bf16[256,1024]{1,0:T(8,128)(2,1)} %bitcast.44.heads.refs_6_, ...), custom_call_target="tpu_custom_call" | custom-call | flops 4966055936 | bytes 23724032 | tf_op jit(solution)/shard_map/feed/pallas_call | solution.py:508
  194.9 11.2 %feed_back.4 = (bf16[256,2816]{1,0:T(8,128)(2,1)S(1)}, bf16[256,2816]{1,0:T(8,128)(2,1)S(1)}, bf16[256,1024]{1,0:T(8,128)(2,1)S(1)}, f32[256,1024]{1,0:T(8,128)S...) custom-call(f32[256,1024]{1,0:T(8,128)S(1)} %bitcast.337, ...), custom_call_target="tpu_custom_call" | custom-call | flops 4966055936 | bytes 25165824 | tf_op jit(solution)/shard_map/feed_back/pallas_call | solution.py:663
  210.3 21.3 %attend_back.4 = (bf16[1,2,128,1024]{3,2,1,0:T(8,128)(2,1)S(1)}, bf16[1,16,256,256]{3,2,1,0:T(8,128)(2,1)S(1)}, f32[512,256]{1,0:T(8,128)S(1)}, f32[512,256]{1,0:T(8,128)S(1)}) custom-call(s32[35]{0:T(128)S(1)} %add_add_fusion.scalars, bf16[1,2,1024,128]{3,2,1,0:T(8,128)(2,1)} %copy-done.49, bf16[1,2,1024,128]{3,2,1,0:T(8,128)(2,1)} %bitcast.373, ...), custom_call_target="tpu_custom_call" | custom-call | flops 10737418240 | bytes 7340032 | tf_op jit(solution)/shard_map/attend_back/pallas_call | solution.py:320
  234.5 9.1 %collective-permute-done.25 = bf16[1,128,1024]{2,1,0:T(8,128)(2,1)S(1)} collective-permute-done((bf16[1,128,1024]{2,1,0:T(8,128)(2,1)S(1)}, bf16[1,128,1024]{2,1,0:T(8,128)(2,1)S(1)}, u32[]{:S(2)}, u32[]{:S(2)}) %collective-permute-start.25) | collective-permute-done | bytes 262176 | tf_op jit(solution)/shard_map/ppermute | solution.py:890
  248.3 20.8 %attend_back.5 = (bf16[1,2,128,1024]{3,2,1,0:T(8,128)(2,1)S(1)}, bf16[1,16,256,256]{3,2,1,0:T(8,128)(2,1)S(1)}, f32[512,256]{1,0:T(8,128)S(1)}, f32[512,256]{1,0:T(8,128)S(1)}) custom-call(s32[35]{0:T(128)S(1)} %add_add_fusion.scalars, bf16[1,2,1024,128]{3,2,1,0:T(8,128)(2,1)} %copy-done.49, ...), custom_call_target="tpu_custom_call", output_to_operand_aliasing={{0}: (10, {})} | custom-call | flops 10737418240 | bytes 7340032 | tf_op jit(solution)/shard_map/attend_back/pallas_call | solution.py:320
  278.8 9.5 %feed.7 = (f32[256,1024]{1,0:T(8,128)S(1)}, bf16[256,1024]{1,0:T(8,128)(2,1)S(1)}, bf16[256,2816]{1,0:T(8,128)(2,1)S(1)}, bf16[256,2816]{1,0:T(8,128)(2,1)S(1)},...) custom-call(bf16[256,1024]{1,0:T(8,128)(2,1)S(1)} %copy-done.19, ...), custom_call_target="tpu_custom_call" | custom-call | flops 4966055936 | bytes 23724032 | tf_op jit(solution)/shard_map/feed/pallas_call | solution.py:508
  293.1 12.1 %feed_back.5 = (bf16[256,2816]{1,0:T(8,128)(2,1)S(1)}, bf16[256,2816]{1,0:T(8,128)(2,1)S(1)}, bf16[256,1024]{1,0:T(8,128)(2,1)S(1)}, f32[256,1024]{1,0:T(8,128)S...) custom-call(f32[256,1024]{1,0:T(8,128)S(1)} %bitcast.335, ...), custom_call_target="tpu_custom_call" | custom-call | flops 4966055936 | bytes 25165824 | tf_op jit(solution)/shard_map/feed_back/pallas_call | solution.py:663
  349.4 11.4 %feed_back.6 = (bf16[256,2816]{1,0:T(8,128)(2,1)S(1)}, bf16[256,2816]{1,0:T(8,128)(2,1)S(1)}, bf16[256,1024]{1,0:T(8,128)(2,1)S(1)}, f32[256,1024]{1,0:T(8,128)S...) custom-call(f32[256,1024]{1,0:T(8,128)S(1)} %multiply_add_fusion.1.g, ...), custom_call_target="tpu_custom_call" | custom-call | flops 4966055936 | bytes 25165824 | tf_op jit(solution)/shard_map/feed_back/pallas_call | solution.py:663
  370.2 12.0 %feed_back.7 = (bf16[256,2816]{1,0:T(8,128)(2,1)S(1)}, bf16[256,2816]{1,0:T(8,128)(2,1)S(1)}, bf16[256,1024]{1,0:T(8,128)(2,1)S(1)}, f32[256,1024]{1,0:T(8,128)}...) custom-call(f32[256,1024]{1,0:T(8,128)S(1)} %multiply_add_fusion.gra, ...), custom_call_target="tpu_custom_call" | custom-call | flops 4966055936 | bytes 25165824 | tf_op jit(solution)/shard_map/feed_back/pallas_call | solution.py:663
  397.4 10.2 %collective-permute-done.42 = bf16[64,5632]{1,0:T(8,128)(2,1)S(1)} collective-permute-done((bf16[64,5632]{1,0:T(8,128)(2,1)S(1)}, bf16[64,5632]{1,0:T(8,128)(2,1)S(1)}, u32[]{:S(2)}, u32[]{:S(2)}) %collective-permute-start.42) | collective-permute-done | bytes 720928 | tf_op jit(solution)/shard_map/ppermute | solution.py:896
  413.2 21.3 %attend_back.6 = (bf16[1,2,128,1024]{3,2,1,0:T(8,128)(2,1)S(1)}, bf16[1,16,256,256]{3,2,1,0:T(8,128)(2,1)S(1)}, f32[512,256]{1,0:T(8,128)S(1)}, f32[512,256]{1,0:T(8,128)S(1)}) custom-call(s32[35]{0:T(128)S(1)} %copy-done.30, bf16[1,2,1024,128]{3,2,1,0:T(8,128)(2,1)} %copy-done.55, bf16[1,2,1024,128]{3,2,1,0:T(8,128)(2,1)} %bitcast.371, ...), custom_call_target="tpu_custom_call" | custom-call | flops 10737418240 | bytes 7340032 | tf_op jit(solution)/shard_map/attend_back/pallas_call | solution.py:320
  438.3 21.0 %attend_back.7 = (bf16[1,2,128,1024]{3,2,1,0:T(8,128)(2,1)S(1)}, bf16[1,16,256,256]{3,2,1,0:T(8,128)(2,1)S(1)}, f32[512,256]{1,0:T(8,128)S(1)}, f32[512,256]{1,0:T(8,128)S(1)}) custom-call(s32[35]{0:T(128)S(1)} %copy-done.30, bf16[1,2,1024,128]{3,2,1,0:T(8,128)(2,1)} %copy-done.55, ...), custom_call_target="tpu_custom_call", output_to_operand_aliasing={{0}: (10, {})} | custom-call | flops 10737418240 | bytes 7340032 | tf_op jit(solution)/shard_map/attend_back/pallas_call | solution.py:320
  463.7 11.5 %collective-permute-done.50 = bf16[1,4,256,256]{3,2,1,0:T(8,128)(2,1)S(1)} collective-permute-done((bf16[1,4,256,256]{3,2,1,0:T(8,128)(2,1)S(1)}, bf16[1,4,256,256]{3,2,1,0:T(8,128)(2,1)S(1)}, u32[]{:S(2)}, u32[]{:S(2)}) %collective-permute-start.50) | collective-permute-done | bytes 524320 | tf_op jit(solution)/shard_map/ppermute | solution.py:896
  482.9 7.8 %collective-permute-done.53 = bf16[1,128,1024]{2,1,0:T(8,128)(2,1)S(1)} collective-permute-done((bf16[1,128,1024]{2,1,0:T(8,128)(2,1)S(1)}, bf16[1,128,1024]{2,1,0:T(8,128)(2,1)S(1)}, u32[]{:S(2)}, u32[]{:S(2)}) %collective-permute-start.53) | collective-permute-done | bytes 262176 | tf_op jit(solution)/shard_map/ppermute | solution.py:890
  501.2 9.1 %collective-permute-done.70 = f32[32]{0:T(128)S(1)} collective-permute-done((f32[32]{0:T(128)S(1)}, f32[32]{0:T(128)S(1)}, u32[]{:S(2)}, u32[]{:S(2)}) %collective-permute-start.70) | collective-permute-done | bytes 160 | tf_op jit(solution)/shard_map/ppermute | solution.py:893
  548.2 11.9 %collective-permute-done.64 = bf16[128,2176]{1,0:T(8,128)(2,1)S(1)} collective-permute-done((bf16[128,2176]{1,0:T(8,128)(2,1)S(1)}, bf16[128,2176]{1,0:T(8,128)(2,1)S(1)}, u32[]{:S(2)}, u32[]{:S(2)}) %collective-permute-start.64) | collective-permute-done | bytes 557088 | tf_op jit(solution)/shard_map/ppermute | solution.py:896
  561.8 15.7 %collective-permute-done.65 = bf16[64,2176]{1,0:T(8,128)(2,1)S(1)} collective-permute-done((bf16[64,2176]{1,0:T(8,128)(2,1)S(1)}, bf16[64,2176]{1,0:T(8,128)(2,1)S(1)}, u32[]{:S(2)}, u32[]{:S(2)}) %collective-permute-start.65) | collective-permute-done | bytes 278560 | tf_op jit(solution)/shard_map/ppermute | solution.py:896
  (573 shorter events, 282.4 us)
Async XLA Ops:
  32.9 23.9 %collective-permute-start.6 = (bf16[1,4,256,256]{3,2,1,0:T(8,128)(2,1)S(1)}, bf16[1,4,256,256]{3,2,1,0:T(8,128)(2,1)}, u32[]{:S(2)}, u32[]{:S(2)}) collective-permute-start(bf16[1,4,256,256]{3,2,1,0:T(8,128)(2,1)S(1)} %pad_maximum_fusion.11), channel_id=1, source_target_pairs={{0,4},{2,6},{4,0},{6,2},{8,12},{10,14},{12,8},{14,10},{16,20},{18,... | collective-permute-start | bytes 1572872 | tf_op jit(solution)/shard_map/ppermute | solution.py:896
  180.8 96.1 %collective-permute-start.24 = (bf16[256,1024]{1,0:T(8,128)(2,1)}, bf16[256,1024]{1,0:T(8,128)(2,1)S(1)}, u32[]{:S(2)}, u32[]{:S(2)}) collective-permute-start(bf16[256,1024]{1,0:T(8,128)(2,1)} %bitcast.44.heads.refs_6_), channel_id=1, source_target_pairs={{0,1},{1,0},{2,3},{3,2},{4,5},{5,4},{6,7},{7,6},{8,9},{9,8},{10,11... | collective-permute-start | bytes 1572872 | tf_op jit(solution)/shard_map/ppermute | solution.py:893
  234.0 39.3 %collective-permute-start.22 = (bf16[1,8,256,256]{3,2,1,0:T(8,128)(2,1)}, bf16[1,8,256,256]{3,2,1,0:T(8,128)(2,1)}, u32[]{:S(2)}, u32[]{:S(2)}) collective-permute-start(bf16[1,8,256,256]{3,2,1,0:T(8,128)(2,1)} %get-tuple-element.470), channel_id=1, source_target_pairs={{0,2},{2,0},{4,6},{6,4},{8,10},{10,8},{12,14},{14,12},{16,18},{18,... | collective-permute-start | bytes 3145736 | tf_op jit(solution)/shard_map/ppermute | solution.py:896
  270.3 21.2 %collective-permute-start.27 = (bf16[1,8,256,256]{3,2,1,0:T(8,128)(2,1)}, bf16[1,8,256,256]{3,2,1,0:T(8,128)(2,1)S(1)}, u32[]{:S(2)}, u32[]{:S(2)}) collective-permute-start(bf16[1,8,256,256]{3,2,1,0:T(8,128)(2,1)} %get-tuple-element.471), channel_id=1, source_target_pairs={{0,2},{2,0},{4,6},{6,4},{8,10},{10,8},{12,14},{14,12},{16,18},{18,... | collective-permute-start | bytes 3145736 | tf_op jit(solution)/shard_map/ppermute | solution.py:896
  271.3 35.0 %collective-permute-start.31 = (bf16[16,64,256]{2,1,0:T(8,128)(2,1)}, bf16[16,64,256]{2,1,0:T(8,128)(2,1)S(1)}, u32[]{:S(2)}, u32[]{:S(2)}) collective-permute-start(bf16[16,64,256]{2,1,0:T(8,128)(2,1)} %pad_maximum_fusion.16), channel_id=1, source_target_pairs={{0,1},{1,0},{2,3},{3,2},{4,5},{5,4},{6,7},{7,6},{8,9},{9,8},{10,11... | collective-permute-start | bytes 1572872 | tf_op jit(solution)/shard_map/ppermute | solution.py:893
  311.8 24.5 %collective-permute-start.35 = (bf16[256,3840]{1,0:T(8,128)(2,1)S(1)}, bf16[256,3840]{1,0:T(8,128)(2,1)}, u32[]{:S(2)}, u32[]{:S(2)}) collective-permute-start(bf16[256,3840]{1,0:T(8,128)(2,1)S(1)} %get-tuple-element.320), channel_id=1, source_target_pairs={{0,2},{2,0},{4,6},{6,4},{8,10},{10,8},{12,14},{14,12},{16,18},{18,... | collective-permute-start | bytes 5898248 | tf_op jit(solution)/shard_map/ppermute | solution.py:896
  339.3 43.0 %collective-permute-start.39 = (bf16[128,3840]{1,0:T(8,128)(2,1)}, bf16[128,3840]{1,0:T(8,128)(2,1)S(1)}, u32[]{:S(2)}, u32[]{:S(2)}) collective-permute-start(bf16[128,3840]{1,0:T(8,128)(2,1)} %get-tuple-element.456), channel_id=1, source_target_pairs={{0,8},{2,10},{4,12},{6,14},{8,0},{10,2},{12,4},{14,6},{16,24},{18,... | collective-permute-start | bytes 2949128 | tf_op jit(solution)/shard_map/ppermute | solution.py:896
  344.5 41.6 %collective-permute-start.38 = (bf16[128,5632]{1,0:T(8,128)(2,1)}, bf16[128,5632]{1,0:T(8,128)(2,1)S(1)}, u32[]{:S(2)}, u32[]{:S(2)}) collective-permute-start(bf16[128,5632]{1,0:T(8,128)(2,1)} %get-tuple-element.452), channel_id=1, source_target_pairs={{0,4},{2,6},{4,0},{6,2},{8,12},{10,14},{12,8},{14,10},{16,20},{18,... | collective-permute-start | bytes 4325384 | tf_op jit(solution)/shard_map/ppermute | solution.py:896
  361.6 22.0 %collective-permute-start.36 = (bf16[1,128,1024]{2,1,0:T(8,128)(2,1)S(1)}, bf16[1,128,1024]{2,1,0:T(8,128)(2,1)S(1)}, u32[]{:S(2)}, u32[]{:S(2)}) collective-permute-start(bf16[1,128,1024]{2,1,0:T(8,128)(2,1)S(1)} %get-tuple-element.514), channel_id=1, source_target_pairs={{0,30},{2,28},{4,26},{6,24},{8,22},{10,20},{12,18},{14,16},{16,14}... | collective-permute-start | bytes 786440 | tf_op jit(solution)/shard_map/ppermute | solution.py:890
  384.9 49.6 %collective-permute-start.47 = (bf16[128,2176]{1,0:T(8,128)(2,1)S(1)}, bf16[128,2176]{1,0:T(8,128)(2,1)S(1)}, u32[]{:S(2)}, u32[]{:S(2)}) collective-permute-start(bf16[128,2176]{1,0:T(8,128)(2,1)S(1)} %get-tuple-element.464), channel_id=1, source_target_pairs={{0,4},{2,6},{4,0},{6,2},{8,12},{10,14},{12,8},{14,10},{16,20},{18,... | collective-permute-start | bytes 1671176 | tf_op jit(solution)/shard_map/ppermute | solution.py:896
  386.4 21.2 %collective-permute-start.42 = (bf16[64,5632]{1,0:T(8,128)(2,1)S(1)}, bf16[64,5632]{1,0:T(8,128)(2,1)S(1)}, u32[]{:S(2)}, u32[]{:S(2)}) collective-permute-start(bf16[64,5632]{1,0:T(8,128)(2,1)S(1)} %get-tuple-element.460), channel_id=1, source_target_pairs={{0,8},{2,10},{4,12},{6,14},{8,0},{10,2},{12,4},{14,6},{16,24},{18,... | collective-permute-start | bytes 2162696 | tf_op jit(solution)/shard_map/ppermute | solution.py:896
  396.8 38.7 %collective-permute-start.46 = (bf16[32,3840]{1,0:T(8,128)(2,1)S(1)}, bf16[32,3840]{1,0:T(8,128)(2,1)S(1)}, u32[]{:S(2)}, u32[]{:S(2)}) collective-permute-start(bf16[32,3840]{1,0:T(8,128)(2,1)S(1)} %get-tuple-element.500), channel_id=1, source_target_pairs={{0,16},{2,18},{4,20},{6,22},{8,24},{10,26},{12,28},{14,30},{16,0},... | collective-permute-start | bytes 737288 | tf_op jit(solution)/shard_map/ppermute | solution.py:896
  407.8 51.8 %collective-permute-start.45 = (bf16[32,5632]{1,0:T(8,128)(2,1)S(1)}, bf16[32,5632]{1,0:T(8,128)(2,1)S(1)}, u32[]{:S(2)}, u32[]{:S(2)}) collective-permute-start(bf16[32,5632]{1,0:T(8,128)(2,1)S(1)} %get-tuple-element.482), channel_id=1, source_target_pairs={{0,16},{2,18},{4,20},{6,22},{8,24},{10,26},{12,28},{14,30},{16,0},... | collective-permute-start | bytes 1081352 | tf_op jit(solution)/shard_map/ppermute | solution.py:896
  409.2 68.1 %collective-permute-start.52 = (bf16[128,3840]{1,0:T(8,128)(2,1)}, bf16[128,3840]{1,0:T(8,128)(2,1)}, u32[]{:S(2)}, u32[]{:S(2)}) collective-permute-start(bf16[128,3840]{1,0:T(8,128)(2,1)} %get-tuple-element.454), channel_id=1, source_target_pairs={{0,8},{2,10},{4,12},{6,14},{8,0},{10,2},{12,4},{14,6},{16,24},{18,... | collective-permute-start | bytes 2949128 | tf_op jit(solution)/shard_map/ppermute | solution.py:896
  412.2 65.2 %collective-permute-start.48 = (bf16[128,5632]{1,0:T(8,128)(2,1)S(1)}, bf16[128,5632]{1,0:T(8,128)(2,1)S(1)}, u32[]{:S(2)}, u32[]{:S(2)}) collective-permute-start(bf16[128,5632]{1,0:T(8,128)(2,1)S(1)} %get-tuple-element.450), channel_id=1, source_target_pairs={{0,4},{2,6},{4,0},{6,2},{8,12},{10,14},{12,8},{14,10},{16,20},{18,... | collective-permute-start | bytes 4325384 | tf_op jit(solution)/shard_map/ppermute | solution.py:896
  435.5 24.5 %collective-permute-start.49 = (bf16[1,8,256,256]{3,2,1,0:T(8,128)(2,1)S(1)}, bf16[1,8,256,256]{3,2,1,0:T(8,128)(2,1)S(1)}, u32[]{:S(2)}, u32[]{:S(2)}) collective-permute-start(bf16[1,8,256,256]{3,2,1,0:T(8,128)(2,1)S(1)} %get-tuple-element.466), channel_id=1, source_target_pairs={{0,2},{2,0},{4,6},{6,4},{8,10},{10,8},{12,14},{14,12},{16,18},{18,... | collective-permute-start | bytes 3145736 | tf_op jit(solution)/shard_map/ppermute | solution.py:896
  437.2 22.8 %collective-permute-start.68 = (bf16[64,2176]{1,0:T(8,128)(2,1)}, bf16[64,2176]{1,0:T(8,128)(2,1)}, u32[]{:S(2)}, u32[]{:S(2)}) collective-permute-start(bf16[64,2176]{1,0:T(8,128)(2,1)} %get-tuple-element.486), channel_id=1, source_target_pairs={{0,8},{2,10},{4,12},{6,14},{8,0},{10,2},{12,4},{14,6},{16,24},{18,... | collective-permute-start | bytes 835592 | tf_op jit(solution)/shard_map/ppermute | solution.py:896
  462.7 35.0 %collective-permute-start.56 = (bf16[1,4,256,256]{3,2,1,0:T(8,128)(2,1)S(1)}, bf16[1,4,256,256]{3,2,1,0:T(8,128)(2,1)S(1)}, u32[]{:S(2)}, u32[]{:S(2)}) collective-permute-start(bf16[1,4,256,256]{3,2,1,0:T(8,128)(2,1)S(1)} %get-tuple-element.489), channel_id=1, source_target_pairs={{0,4},{2,6},{4,0},{6,2},{8,12},{10,14},{12,8},{14,10},{16,20},{18,... | collective-permute-start | bytes 1572872 | tf_op jit(solution)/shard_map/ppermute | solution.py:896
  475.4 22.1 %collective-permute-start.54 = (bf16[1,2,256,256]{3,2,1,0:T(8,128)(2,1)S(1)}, bf16[1,2,256,256]{3,2,1,0:T(8,128)(2,1)S(1)}, u32[]{:S(2)}, u32[]{:S(2)}) collective-permute-start(bf16[1,2,256,256]{3,2,1,0:T(8,128)(2,1)S(1)} %get-tuple-element.516), channel_id=1, source_target_pairs={{0,8},{2,10},{4,12},{6,14},{8,0},{10,2},{12,4},{14,6},{16,24},{18,... | collective-permute-start | bytes 786440 | tf_op jit(solution)/shard_map/ppermute | solution.py:896
  481.6 52.0 %collective-permute-start.71 = (bf16[64,3840]{1,0:T(8,128)(2,1)S(1)}, bf16[64,3840]{1,0:T(8,128)(2,1)S(1)}, u32[]{:S(2)}, u32[]{:S(2)}) collective-permute-start(bf16[64,3840]{1,0:T(8,128)(2,1)S(1)} %get-tuple-element.476), channel_id=1, source_target_pairs={{0,4},{2,6},{4,0},{6,2},{8,12},{10,14},{12,8},{14,10},{16,20},{18,... | collective-permute-start | bytes 1474568 | tf_op jit(solution)/shard_map/ppermute | solution.py:896
  490.7 52.6 %collective-permute-start.73 = (bf16[64,5632]{1,0:T(8,128)(2,1)S(1)}, bf16[64,5632]{1,0:T(8,128)(2,1)S(1)}, u32[]{:S(2)}, u32[]{:S(2)}) collective-permute-start(bf16[64,5632]{1,0:T(8,128)(2,1)S(1)} %get-tuple-element.458), channel_id=1, source_target_pairs={{0,8},{2,10},{4,12},{6,14},{8,0},{10,2},{12,4},{14,6},{16,24},{18,... | collective-permute-start | bytes 2162696 | tf_op jit(solution)/shard_map/ppermute | solution.py:896
  497.5 26.7 %collective-permute-start.62 = (bf16[16,64,256]{2,1,0:T(8,128)(2,1)S(1)}, bf16[16,64,256]{2,1,0:T(8,128)(2,1)S(1)}, u32[]{:S(2)}, u32[]{:S(2)}) collective-permute-start(bf16[16,64,256]{2,1,0:T(8,128)(2,1)S(1)} %pad_maximum_fusion.19), channel_id=1, source_target_pairs={{0,1},{1,0},{2,3},{3,2},{4,5},{5,4},{6,7},{7,6},{8,9},{9,8},{10,11... | collective-permute-start | bytes 1572872 | tf_op jit(solution)/shard_map/ppermute | solution.py:893
  542.5 35.4 %collective-permute-start.72 = (bf16[32,3840]{1,0:T(8,128)(2,1)S(1)}, bf16[32,3840]{1,0:T(8,128)(2,1)S(1)}, u32[]{:S(2)}, u32[]{:S(2)}) collective-permute-start(bf16[32,3840]{1,0:T(8,128)(2,1)S(1)} %get-tuple-element.497), channel_id=1, source_target_pairs={{0,16},{2,18},{4,20},{6,22},{8,24},{10,26},{12,28},{14,30},{16,0},... | collective-permute-start | bytes 737288 | tf_op jit(solution)/shard_map/ppermute | solution.py:896
  547.1 30.9 %collective-permute-start.74 = (bf16[32,5632]{1,0:T(8,128)(2,1)S(1)}, bf16[32,5632]{1,0:T(8,128)(2,1)S(1)}, u32[]{:S(2)}, u32[]{:S(2)}) collective-permute-start(bf16[32,5632]{1,0:T(8,128)(2,1)S(1)} %get-tuple-element.479), channel_id=1, source_target_pairs={{0,16},{2,18},{4,20},{6,22},{8,24},{10,26},{12,28},{14,30},{16,0},... | collective-permute-start | bytes 1081352 | tf_op jit(solution)/shard_map/ppermute | solution.py:896
  (150 other events, 1537.4 us)

commit v6 on v5

--- a/solution.py
+++ b/solution.py
@@ -1155,15 +1155,15 @@
         else:
             pending[2].advance(up_k[-1])
             sents = stepped(up_k[-1])
-            for one in sums:
-                one.advance(sents)
-            dq, up_sent = after((dq, up_sent), sents_of(sums))
+            sums[1].advance(sents)
+            dq, up_sent = after((dq, up_sent), sums[1].sent)
             dq = turned(dq)
             up_got = across(up_sent)
-            sents = stepped((sents_of(sums), dq))
+            sents = stepped((sums[1].sent, dq))
+            sums[0].advance(sents)
             dq_other = across(dq)
             pending[2].advance(sents)
-            sents = stepped(None)
+            sents = stepped(sums[0].sent)
             up_got = after(up_got, sents)
         while any(late.got is not None for late in d_lat):
             stepped(None)
@@ -1210,7 +1210,7 @@
         sums.append(rest)
         pending = sums
         layer_sums.insert(0, sums)
-    layer_grads = []
+    layer_grads, other_gains = [], []
     for sums in layer_sums:
         g_gate_up, g_plain, g_rest = [one.finish() for one in sums]
         lat_at, up_at = heads_dim, heads_dim + GROUPS * size
@@ -1218,9 +1218,10 @@
         g_up = jnp.concatenate(
             [g_rest[:, up_at + at * size : up_at + (at + 1) * size] for at in range(folds)]
         )
+        other_gains.append(g_rest[:, vectors_at + 3])
         layer_grads.append(
             (
-                g_rest[:, vectors_at + 2] + across(g_rest[:, vectors_at + 3]),
+                g_rest[:, vectors_at + 2],
                 g_rest[:, :lat_at],
                 g_rest[:, lat_at:up_at],
                 g_up.T,
@@ -1232,6 +1233,7 @@
             )
         )
     stacked = [jnp.stack([grads[member] for grads in layer_grads]) for member in range(9)]
+    stacked[0] = stacked[0] + across(jnp.stack(other_gains))
     input_grad = grad_own.astype(BF16)
     return (
         placed(output, output_moved),

time: 596 us -> 590 us (0.990)
  starting transfers between devices: 73.5 us -> 130 us
  Pallas kernels: 240 us -> 188 us
  waiting for transfers between devices: 170 us -> 161 us
    ppermute x12 -> x11, starting transfers between devices: 5.46 us -> 45.6 us  [across(): lax.ppermute(value, 'rep', [(at, rep_count - 1 - at) for at in range(rep_...]
    pallas_call x4, Pallas kernels: 84.4 us -> 53.1 us  [attend_back(): pl.pallas_call(functools.partial(attend_back_kernel, seq_count=seq_count,...]
    pallas_call x4, Pallas kernels: 53.6 us -> 33.2 us  [attend(): pl.pallas_call(functools.partial(attend_kernel, seq_count=seq_count, half...]
    ppermute x56, starting transfers between devices: 55.4 us -> 71.3 us  [trade(): lax.ppermute(value, 'seq', [(at, at ^ bit) for at in range(seq_count)])]
    ppermute x7, waiting for transfers between devices: 20.3 us -> 13.4 us  [swap_ends(): return lax.ppermute(value, 'seq', moves)]
    ppermute x12 -> x11, waiting for transfers between devices: 20.7 us -> 16.2 us  [across(): lax.ppermute(value, 'rep', [(at, rep_count - 1 - at) for at in range(rep_...]
  transfers between devices with their start and end apart: 75 -> 74, of which waited for: 31 -> 28; matrix products, arithmetic and copies ran while one was open for 14% -> 14% of each run, Pallas kernels for 40% -> 31%
where the time goes in v6:
time: 590 us; the launch traced here: 587 us
  Pallas kernels  188 us (32%)
  waiting for transfers between devices  161 us (27%)
  starting transfers between devices  130 us (22%)
  other arithmetic  40.8 us (7%)
  local copies, waits for them, and re-layouts  32.9 us (6%)
  matrix products  30.8 us (5%)
    ppermute x56, waiting for transfers between devices, trade(): lax.ppermute(value, 'seq', [(at, at ^ bit) for at in range(seq_count)])  131 us
    ppermute x56, starting transfers between devices, trade(): lax.ppermute(value, 'seq', [(at, at ^ bit) for at in range(seq_count)])  71.3 us
    pallas_call x4, Pallas kernels, attend_back(): pl.pallas_call(functools.partial(attend_back_kernel, seq_count=seq_count,...  53.1 us
    pallas_call x4, Pallas kernels, feed_back(): pl.pallas_call(functools.partial(feed_back_kernel, layer=layer, hidden=hi...  46.7 us
    ppermute x11, starting transfers between devices, across(): lax.ppermute(value, 'rep', [(at, rep_count - 1 - at) for at in range(rep_...  45.6 us
    pallas_call x4, Pallas kernels, feed(): pl.pallas_call(functools.partial(feed_kernel, layer=layer, hidden=hidden)...  37 us
    pallas_call x4, Pallas kernels, attend(): pl.pallas_call(functools.partial(attend_kernel, seq_count=seq_count, half...  33.2 us
    dot_general x26, matrix products, dot_as(): return lax.dot_general(left, right, dims, preferred_element_type=F32)  23.4 us
  transfers between devices with their start and end apart: 74, of which 28 were waited for; matrix products, arithmetic and copies ran while one was open for 14% of the time, Pallas kernels for 31%

profile of v6, /device:TPU:0, one launch (start us, length us, event | category | flops | bytes accessed | tf_op | source)
XLA Modules:
  0.0 586.5 jit_solution(18184090655982891100)
XLA Ops:
  62.2 8.3 %attend.4 = (bf16[1,2,128,1024]{3,2,1,0:T(8,128)(2,1)S(1)}, bf16[1,2,512,128]{3,2,1,0:T(8,128)(2,1)}, f32[1,2,1,1024]{3,2,1,0:T(1,128)}, bf16[1,2,1024,256]{3,2,1,0:T(8,128)(2,1)}, bf16[1,2,256,1024]{3,2,1,0:T(8,128)(2,1)}) custom-call(s32[35]{0:T(128)S(1)} %add_add_fusion.1.scalars, bf16[1,2,1024,128]{3,2,1,0:T(8,128)(2,1)S(1)} %fusion.60.q_ref, ...), custom_call_target="tpu_custom_call" | custom-call | flops 4294967296 | bytes 4194304 | tf_op jit(solution)/shard_map/attend/pallas_call | solution.py:264
  83.3 11.8 %collective-permute-start.12 = (bf16[256,1024]{1,0:T(8,128)(2,1)S(1)}, bf16[256,1024]{1,0:T(8,128)(2,1)S(1)}, u32[]{:S(2)}, u32[]{:S(2)}) collective-permute-start(bf16[256,1024]{1,0:T(8,128)(2,1)S(1)} %bitcast.357), channel_id=1, source_target_pairs={{0,1},{1,0},{2,3},{3,2},{4,5},{5,4},{6,7},{7,6},{8,9},{9,8},{10,11... | collective-permute-start | bytes 1572872 | tf_op jit(solution)/shard_map/ppermute | solution.py:893
  96.5 9.2 %feed.4 = (f32[256,1024]{1,0:T(8,128)S(1)}, bf16[256,1024]{1,0:T(8,128)(2,1)S(1)}, bf16[256,2816]{1,0:T(8,128)(2,1)S(1)}, bf16[256,2816]{1,0:T(8,128)(2,1)S(1)},...) custom-call(bf16[256,1024]{1,0:T(8,128)(2,1)S(1)} %bitcast.358, ...), custom_call_target="tpu_custom_call" | custom-call | flops 4966055936 | bytes 23724032 | tf_op jit(solution)/shard_map/feed/pallas_call | solution.py:508
  111.7 8.8 %feed.5 = (f32[256,1024]{1,0:T(8,128)S(1)}, bf16[256,1024]{1,0:T(8,128)(2,1)S(1)}, bf16[256,2816]{1,0:T(8,128)(2,1)S(1)}, bf16[256,2816]{1,0:T(8,128)(2,1)S(1)},...) custom-call(bf16[256,1024]{1,0:T(8,128)(2,1)S(1)} %collective-permute-done.12.heads.refs_7_, ...), custom_call_target="tpu_custom_call" | custom-call | flops 4966055936 | bytes 23724032 | tf_op jit(solution)/shard_map/feed/pallas_call | solution.py:508
  135.1 9.8 %collective-permute-done.17 = bf16[1,4,256,256]{3,2,1,0:T(8,128)(2,1)S(1)} collective-permute-done((bf16[1,4,256,256]{3,2,1,0:T(8,128)(2,1)S(1)}, bf16[1,4,256,256]{3,2,1,0:T(8,128)(2,1)S(1)}, u32[]{:S(2)}, u32[]{:S(2)}) %collective-permute-start.17) | collective-permute-done | bytes 524320 | tf_op jit(solution)/shard_map/ppermute | solution.py:896
  171.4 11.0 %collective-permute-start.24 = (bf16[256,1024]{1,0:T(8,128)(2,1)}, bf16[256,1024]{1,0:T(8,128)(2,1)S(1)}, u32[]{:S(2)}, u32[]{:S(2)}) collective-permute-start(bf16[256,1024]{1,0:T(8,128)(2,1)} %bitcast.44.heads.refs_6_), channel_id=1, source_target_pairs={{0,1},{1,0},{2,3},{3,2},{4,5},{5,4},{6,7},{7,6},{8,9},{9,8},{10,11... | collective-permute-start | bytes 1572872 | tf_op jit(solution)/shard_map/ppermute | solution.py:893
  182.6 9.5 %feed.6 = (f32[256,1024]{1,0:T(8,128)S(1)}, bf16[256,1024]{1,0:T(8,128)(2,1)S(1)}, bf16[256,2816]{1,0:T(8,128)(2,1)S(1)}, bf16[256,2816]{1,0:T(8,128)(2,1)S(1)},...) custom-call(bf16[256,1024]{1,0:T(8,128)(2,1)} %bitcast.44.heads.refs_6_, ...), custom_call_target="tpu_custom_call" | custom-call | flops 4966055936 | bytes 23724032 | tf_op jit(solution)/shard_map/feed/pallas_call | solution.py:508
  196.4 11.2 %feed_back.4 = (bf16[256,2816]{1,0:T(8,128)(2,1)S(1)}, bf16[256,2816]{1,0:T(8,128)(2,1)S(1)}, bf16[256,1024]{1,0:T(8,128)(2,1)S(1)}, f32[256,1024]{1,0:T(8,128)S...) custom-call(f32[256,1024]{1,0:T(8,128)S(1)} %bitcast.337, ...), custom_call_target="tpu_custom_call" | custom-call | flops 4966055936 | bytes 25165824 | tf_op jit(solution)/shard_map/feed_back/pallas_call | solution.py:663
  211.8 13.5 %attend_back.4 = (bf16[1,2,128,1024]{3,2,1,0:T(8,128)(2,1)S(1)}, bf16[1,16,256,256]{3,2,1,0:T(8,128)(2,1)S(1)}, f32[512,256]{1,0:T(8,128)S(1)}, f32[512,256]{1,0:T(8,128)S(1)}) custom-call(s32[35]{0:T(128)S(1)} %add_add_fusion.scalars, bf16[1,2,1024,128]{3,2,1,0:T(8,128)(2,1)} %copy-done.49, bf16[1,2,1024,128]{3,2,1,0:T(8,128)(2,1)} %bitcast.373, ...), custom_call_target="tpu_custom_call" | custom-call | flops 10737418240 | bytes 7340032 | tf_op jit(solution)/shard_map/attend_back/pallas_call | solution.py:320
  237.0 11.3 %collective-permute-done.21 = bf16[256,1024]{1,0:T(8,128)(2,1)S(1)} collective-permute-done((bf16[256,1024]{1,0:T(8,128)(2,1)S(1)}, bf16[256,1024]{1,0:T(8,128)(2,1)S(1)}, u32[]{:S(2)}, u32[]{:S(2)}) %collective-permute-start.21) | collective-permute-done | bytes 524320 | tf_op jit(solution)/shard_map/ppermute | solution.py:893
  248.3 13.0 %attend_back.5 = (bf16[1,2,128,1024]{3,2,1,0:T(8,128)(2,1)S(1)}, bf16[1,16,256,256]{3,2,1,0:T(8,128)(2,1)S(1)}, f32[512,256]{1,0:T(8,128)S(1)}, f32[512,256]{1,0:T(8,128)S(1)}) custom-call(s32[35]{0:T(128)S(1)} %add_add_fusion.scalars, bf16[1,2,1024,128]{3,2,1,0:T(8,128)(2,1)} %copy-done.49, ...), custom_call_target="tpu_custom_call", output_to_operand_aliasing={{0}: (10, {})} | custom-call | flops 10737418240 | bytes 7340032 | tf_op jit(solution)/shard_map/attend_back/pallas_call | solution.py:320
  261.3 9.6 %collective-permute-start.28 = (bf16[256,1024]{1,0:T(8,128)(2,1)S(1)}, bf16[256,1024]{1,0:T(8,128)(2,1)S(1)}, u32[]{:S(2)}, u32[]{:S(2)}) collective-permute-start(bf16[256,1024]{1,0:T(8,128)(2,1)S(1)} %bitcast.360), channel_id=1, source_target_pairs={{0,1},{1,0},{2,3},{3,2},{4,5},{5,4},{6,7},{7,6},{8,9},{9,8},{10,11... | collective-permute-start | bytes 1572872 | tf_op jit(solution)/shard_map/ppermute | solution.py:893
  277.9 9.5 %feed.7 = (f32[256,1024]{1,0:T(8,128)S(1)}, bf16[256,1024]{1,0:T(8,128)(2,1)S(1)}, bf16[256,2816]{1,0:T(8,128)(2,1)S(1)}, bf16[256,2816]{1,0:T(8,128)(2,1)S(1)},...) custom-call(bf16[256,1024]{1,0:T(8,128)(2,1)S(1)} %copy-done.19, ...), custom_call_target="tpu_custom_call" | custom-call | flops 4966055936 | bytes 23724032 | tf_op jit(solution)/shard_map/feed/pallas_call | solution.py:508
  293.0 12.1 %feed_back.5 = (bf16[256,2816]{1,0:T(8,128)(2,1)S(1)}, bf16[256,2816]{1,0:T(8,128)(2,1)S(1)}, bf16[256,1024]{1,0:T(8,128)(2,1)S(1)}, f32[256,1024]{1,0:T(8,128)S...) custom-call(f32[256,1024]{1,0:T(8,128)S(1)} %bitcast.335, ...), custom_call_target="tpu_custom_call" | custom-call | flops 4966055936 | bytes 25165824 | tf_op jit(solution)/shard_map/feed_back/pallas_call | solution.py:663
  350.5 11.3 %feed_back.6 = (bf16[256,2816]{1,0:T(8,128)(2,1)S(1)}, bf16[256,2816]{1,0:T(8,128)(2,1)S(1)}, bf16[256,1024]{1,0:T(8,128)(2,1)S(1)}, f32[256,1024]{1,0:T(8,128)S...) custom-call(f32[256,1024]{1,0:T(8,128)S(1)} %multiply_add_fusion.1.g, ...), custom_call_target="tpu_custom_call" | custom-call | flops 4966055936 | bytes 25165824 | tf_op jit(solution)/shard_map/feed_back/pallas_call | solution.py:663
  371.8 12.0 %feed_back.7 = (bf16[256,2816]{1,0:T(8,128)(2,1)S(1)}, bf16[256,2816]{1,0:T(8,128)(2,1)S(1)}, bf16[256,1024]{1,0:T(8,128)(2,1)S(1)}, f32[256,1024]{1,0:T(8,128)}...) custom-call(f32[256,1024]{1,0:T(8,128)S(1)} %multiply_add_fusion.gra, ...), custom_call_target="tpu_custom_call" | custom-call | flops 4966055936 | bytes 25165824 | tf_op jit(solution)/shard_map/feed_back/pallas_call | solution.py:663
  399.6 10.3 %collective-permute-done.42 = bf16[64,5632]{1,0:T(8,128)(2,1)S(1)} collective-permute-done((bf16[64,5632]{1,0:T(8,128)(2,1)S(1)}, bf16[64,5632]{1,0:T(8,128)(2,1)S(1)}, u32[]{:S(2)}, u32[]{:S(2)}) %collective-permute-start.42) | collective-permute-done | bytes 720928 | tf_op jit(solution)/shard_map/ppermute | solution.py:896
  414.9 13.5 %attend_back.6 = (bf16[1,2,128,1024]{3,2,1,0:T(8,128)(2,1)S(1)}, bf16[1,16,256,256]{3,2,1,0:T(8,128)(2,1)S(1)}, f32[512,256]{1,0:T(8,128)S(1)}, f32[512,256]{1,0:T(8,128)S(1)}) custom-call(s32[35]{0:T(128)S(1)} %copy-done.30, bf16[1,2,1024,128]{3,2,1,0:T(8,128)(2,1)} %copy-done.55, bf16[1,2,1024,128]{3,2,1,0:T(8,128)(2,1)} %bitcast.371, ...), custom_call_target="tpu_custom_call" | custom-call | flops 10737418240 | bytes 7340032 | tf_op jit(solution)/shard_map/attend_back/pallas_call | solution.py:320
  440.2 13.2 %attend_back.7 = (bf16[1,2,128,1024]{3,2,1,0:T(8,128)(2,1)S(1)}, bf16[1,16,256,256]{3,2,1,0:T(8,128)(2,1)S(1)}, f32[512,256]{1,0:T(8,128)S(1)}, f32[512,256]{1,0:T(8,128)S(1)}) custom-call(s32[35]{0:T(128)S(1)} %copy-done.30, bf16[1,2,1024,128]{3,2,1,0:T(8,128)(2,1)} %copy-done.55, ...), custom_call_target="tpu_custom_call", output_to_operand_aliasing={{0}: (10, {})} | custom-call | flops 10737418240 | bytes 7340032 | tf_op jit(solution)/shard_map/attend_back/pallas_call | solution.py:320
  458.0 11.3 %collective-permute-done.50 = bf16[1,4,256,256]{3,2,1,0:T(8,128)(2,1)S(1)} collective-permute-done((bf16[1,4,256,256]{3,2,1,0:T(8,128)(2,1)S(1)}, bf16[1,4,256,256]{3,2,1,0:T(8,128)(2,1)S(1)}, u32[]{:S(2)}, u32[]{:S(2)}) %collective-permute-start.50) | collective-permute-done | bytes 524320 | tf_op jit(solution)/shard_map/ppermute | solution.py:896
  481.5 9.0 %collective-permute-done.52 = bf16[1,128,1024]{2,1,0:T(8,128)(2,1)S(1)} collective-permute-done((bf16[1,128,1024]{2,1,0:T(8,128)(2,1)S(1)}, bf16[1,128,1024]{2,1,0:T(8,128)(2,1)S(1)}, u32[]{:S(2)}, u32[]{:S(2)}) %collective-permute-start.52) | collective-permute-done | bytes 262176 | tf_op jit(solution)/shard_map/ppermute | solution.py:890
  514.8 12.5 %collective-permute-done.58 = bf16[1,1,256,256]{3,2,1,0:T(8,128)(2,1)S(1)} collective-permute-done((bf16[1,1,256,256]{3,2,1,0:T(8,128)(2,1)S(1)}, bf16[1,1,256,256]{3,2,1,0:T(8,128)(2,1)S(1)}, u32[]{:S(2)}, u32[]{:S(2)}) %collective-permute-start.58) | collective-permute-done | bytes 131104 | tf_op jit(solution)/shard_map/ppermute | solution.py:896
  543.4 12.1 %collective-permute-done.64 = bf16[128,2176]{1,0:T(8,128)(2,1)S(1)} collective-permute-done((bf16[128,2176]{1,0:T(8,128)(2,1)S(1)}, bf16[128,2176]{1,0:T(8,128)(2,1)S(1)}, u32[]{:S(2)}, u32[]{:S(2)}) %collective-permute-start.64) | collective-permute-done | bytes 557088 | tf_op jit(solution)/shard_map/ppermute | solution.py:896
  557.9 15.3 %collective-permute-done.65 = bf16[64,2176]{1,0:T(8,128)(2,1)S(1)} collective-permute-done((bf16[64,2176]{1,0:T(8,128)(2,1)S(1)}, bf16[64,2176]{1,0:T(8,128)(2,1)S(1)}, u32[]{:S(2)}, u32[]{:S(2)}) %collective-permute-start.65) | collective-permute-done | bytes 278560 | tf_op jit(solution)/shard_map/ppermute | solution.py:896
  (570 shorter events, 314.3 us)
Async XLA Ops:
  33.0 23.9 %collective-permute-start.6 = (bf16[1,4,256,256]{3,2,1,0:T(8,128)(2,1)S(1)}, bf16[1,4,256,256]{3,2,1,0:T(8,128)(2,1)}, u32[]{:S(2)}, u32[]{:S(2)}) collective-permute-start(bf16[1,4,256,256]{3,2,1,0:T(8,128)(2,1)S(1)} %pad_maximum_fusion.11), channel_id=1, source_target_pairs={{0,4},{2,6},{4,0},{6,2},{8,12},{10,14},{12,8},{14,10},{16,20},{18,... | collective-permute-start | bytes 1572872 | tf_op jit(solution)/shard_map/ppermute | solution.py:896
  70.8 25.6 %collective-permute-start.9 = (bf16[1,128,1024]{2,1,0:T(8,128)(2,1)S(1)}, bf16[1,128,1024]{2,1,0:T(8,128)(2,1)S(1)}, u32[]{:S(2)}, u32[]{:S(2)}) collective-permute-start(bf16[1,128,1024]{2,1,0:T(8,128)(2,1)S(1)} %get-tuple-element.546), channel_id=1, source_target_pairs={{0,30},{2,28},{4,26},{6,24},{8,22},{10,20},{12,18},{14,16},{16,14}... | collective-permute-start | bytes 786440 | tf_op jit(solution)/shard_map/ppermute | solution.py:890
  83.3 28.4 %collective-permute-start.12 = (bf16[256,1024]{1,0:T(8,128)(2,1)S(1)}, bf16[256,1024]{1,0:T(8,128)(2,1)S(1)}, u32[]{:S(2)}, u32[]{:S(2)}) collective-permute-start(bf16[256,1024]{1,0:T(8,128)(2,1)S(1)} %bitcast.357), channel_id=1, source_target_pairs={{0,1},{1,0},{2,3},{3,2},{4,5},{5,4},{6,7},{7,6},{8,9},{9,8},{10,11... | collective-permute-start | bytes 1572872 | tf_op jit(solution)/shard_map/ppermute | solution.py:893
  171.4 104.7 %collective-permute-start.24 = (bf16[256,1024]{1,0:T(8,128)(2,1)}, bf16[256,1024]{1,0:T(8,128)(2,1)S(1)}, u32[]{:S(2)}, u32[]{:S(2)}) collective-permute-start(bf16[256,1024]{1,0:T(8,128)(2,1)} %bitcast.44.heads.refs_6_), channel_id=1, source_target_pairs={{0,1},{1,0},{2,3},{3,2},{4,5},{5,4},{6,7},{7,6},{8,9},{9,8},{10,11... | collective-permute-start | bytes 1572872 | tf_op jit(solution)/shard_map/ppermute | solution.py:893
  235.7 37.3 %collective-permute-start.22 = (bf16[1,8,256,256]{3,2,1,0:T(8,128)(2,1)}, bf16[1,8,256,256]{3,2,1,0:T(8,128)(2,1)}, u32[]{:S(2)}, u32[]{:S(2)}) collective-permute-start(bf16[1,8,256,256]{3,2,1,0:T(8,128)(2,1)} %get-tuple-element.478), channel_id=1, source_target_pairs={{0,2},{2,0},{4,6},{6,4},{8,10},{10,8},{12,14},{14,12},{16,18},{18,... | collective-permute-start | bytes 3145736 | tf_op jit(solution)/shard_map/ppermute | solution.py:896
  261.3 26.2 %collective-permute-start.28 = (bf16[256,1024]{1,0:T(8,128)(2,1)S(1)}, bf16[256,1024]{1,0:T(8,128)(2,1)S(1)}, u32[]{:S(2)}, u32[]{:S(2)}) collective-permute-start(bf16[256,1024]{1,0:T(8,128)(2,1)S(1)} %bitcast.360), channel_id=1, source_target_pairs={{0,1},{1,0},{2,3},{3,2},{4,5},{5,4},{6,7},{7,6},{8,9},{9,8},{10,11... | collective-permute-start | bytes 1572872 | tf_op jit(solution)/shard_map/ppermute | solution.py:893
  273.0 33.2 %collective-permute-start.31 = (bf16[16,64,256]{2,1,0:T(8,128)(2,1)}, bf16[16,64,256]{2,1,0:T(8,128)(2,1)S(1)}, u32[]{:S(2)}, u32[]{:S(2)}) collective-permute-start(bf16[16,64,256]{2,1,0:T(8,128)(2,1)} %pad_maximum_fusion.16), channel_id=1, source_target_pairs={{0,1},{1,0},{2,3},{3,2},{4,5},{5,4},{6,7},{7,6},{8,9},{9,8},{10,11... | collective-permute-start | bytes 1572872 | tf_op jit(solution)/shard_map/ppermute | solution.py:893
  311.7 24.8 %collective-permute-start.35 = (bf16[256,3840]{1,0:T(8,128)(2,1)S(1)}, bf16[256,3840]{1,0:T(8,128)(2,1)}, u32[]{:S(2)}, u32[]{:S(2)}) collective-permute-start(bf16[256,3840]{1,0:T(8,128)(2,1)S(1)} %get-tuple-element.324), channel_id=1, source_target_pairs={{0,2},{2,0},{4,6},{6,4},{8,10},{10,8},{12,14},{14,12},{16,18},{18,... | collective-permute-start | bytes 5898248 | tf_op jit(solution)/shard_map/ppermute | solution.py:896
  339.4 44.4 %collective-permute-start.39 = (bf16[128,3840]{1,0:T(8,128)(2,1)}, bf16[128,3840]{1,0:T(8,128)(2,1)S(1)}, u32[]{:S(2)}, u32[]{:S(2)}) collective-permute-start(bf16[128,3840]{1,0:T(8,128)(2,1)} %get-tuple-element.464), channel_id=1, source_target_pairs={{0,8},{2,10},{4,12},{6,14},{8,0},{10,2},{12,4},{14,6},{16,24},{18,... | collective-permute-start | bytes 2949128 | tf_op jit(solution)/shard_map/ppermute | solution.py:896
  345.3 42.4 %collective-permute-start.38 = (bf16[128,5632]{1,0:T(8,128)(2,1)}, bf16[128,5632]{1,0:T(8,128)(2,1)S(1)}, u32[]{:S(2)}, u32[]{:S(2)}) collective-permute-start(bf16[128,5632]{1,0:T(8,128)(2,1)} %get-tuple-element.460), channel_id=1, source_target_pairs={{0,4},{2,6},{4,0},{6,2},{8,12},{10,14},{12,8},{14,10},{16,20},{18,... | collective-permute-start | bytes 4325384 | tf_op jit(solution)/shard_map/ppermute | solution.py:896
  386.4 42.0 %collective-permute-start.47 = (bf16[128,2176]{1,0:T(8,128)(2,1)S(1)}, bf16[128,2176]{1,0:T(8,128)(2,1)S(1)}, u32[]{:S(2)}, u32[]{:S(2)}) collective-permute-start(bf16[128,2176]{1,0:T(8,128)(2,1)S(1)} %get-tuple-element.472), channel_id=1, source_target_pairs={{0,4},{2,6},{4,0},{6,2},{8,12},{10,14},{12,8},{14,10},{16,20},{18,... | collective-permute-start | bytes 1671176 | tf_op jit(solution)/shard_map/ppermute | solution.py:896
  398.4 31.0 %collective-permute-start.46 = (bf16[32,3840]{1,0:T(8,128)(2,1)S(1)}, bf16[32,3840]{1,0:T(8,128)(2,1)S(1)}, u32[]{:S(2)}, u32[]{:S(2)}) collective-permute-start(bf16[32,3840]{1,0:T(8,128)(2,1)S(1)} %get-tuple-element.508), channel_id=1, source_target_pairs={{0,16},{2,18},{4,20},{6,22},{8,24},{10,26},{12,28},{14,30},{16,0},... | collective-permute-start | bytes 737288 | tf_op jit(solution)/shard_map/ppermute | solution.py:896
  410.1 43.6 %collective-permute-start.45 = (bf16[32,5632]{1,0:T(8,128)(2,1)S(1)}, bf16[32,5632]{1,0:T(8,128)(2,1)S(1)}, u32[]{:S(2)}, u32[]{:S(2)}) collective-permute-start(bf16[32,5632]{1,0:T(8,128)(2,1)S(1)} %get-tuple-element.490), channel_id=1, source_target_pairs={{0,16},{2,18},{4,20},{6,22},{8,24},{10,26},{12,28},{14,30},{16,0},... | collective-permute-start | bytes 1081352 | tf_op jit(solution)/shard_map/ppermute | solution.py:896
  411.5 66.0 %collective-permute-start.48 = (bf16[128,3840]{1,0:T(8,128)(2,1)}, bf16[128,3840]{1,0:T(8,128)(2,1)}, u32[]{:S(2)}, u32[]{:S(2)}) collective-permute-start(bf16[128,3840]{1,0:T(8,128)(2,1)} %get-tuple-element.462), channel_id=1, source_target_pairs={{0,8},{2,10},{4,12},{6,14},{8,0},{10,2},{12,4},{14,6},{16,24},{18,... | collective-permute-start | bytes 2949128 | tf_op jit(solution)/shard_map/ppermute | solution.py:896
  413.8 88.1 %collective-permute-start.55 = (bf16[128,5632]{1,0:T(8,128)(2,1)S(1)}, bf16[128,5632]{1,0:T(8,128)(2,1)S(1)}, u32[]{:S(2)}, u32[]{:S(2)}) collective-permute-start(bf16[128,5632]{1,0:T(8,128)(2,1)S(1)} %get-tuple-element.458), channel_id=1, source_target_pairs={{0,4},{2,6},{4,0},{6,2},{8,12},{10,14},{12,8},{14,10},{16,20},{18,... | collective-permute-start | bytes 4325384 | tf_op jit(solution)/shard_map/ppermute | solution.py:896
  429.4 24.6 %collective-permute-start.49 = (bf16[1,8,256,256]{3,2,1,0:T(8,128)(2,1)S(1)}, bf16[1,8,256,256]{3,2,1,0:T(8,128)(2,1)S(1)}, u32[]{:S(2)}, u32[]{:S(2)}) collective-permute-start(bf16[1,8,256,256]{3,2,1,0:T(8,128)(2,1)S(1)} %get-tuple-element.474), channel_id=1, source_target_pairs={{0,2},{2,0},{4,6},{6,4},{8,10},{10,8},{12,14},{14,12},{16,18},{18,... | collective-permute-start | bytes 3145736 | tf_op jit(solution)/shard_map/ppermute | solution.py:896
  431.1 22.9 %collective-permute-start.67 = (bf16[64,2176]{1,0:T(8,128)(2,1)}, bf16[64,2176]{1,0:T(8,128)(2,1)}, u32[]{:S(2)}, u32[]{:S(2)}) collective-permute-start(bf16[64,2176]{1,0:T(8,128)(2,1)} %get-tuple-element.494), channel_id=1, source_target_pairs={{0,8},{2,10},{4,12},{6,14},{8,0},{10,2},{12,4},{14,6},{16,24},{18,... | collective-permute-start | bytes 835592 | tf_op jit(solution)/shard_map/ppermute | solution.py:896
  456.7 36.7 %collective-permute-start.56 = (bf16[1,4,256,256]{3,2,1,0:T(8,128)(2,1)S(1)}, bf16[1,4,256,256]{3,2,1,0:T(8,128)(2,1)S(1)}, u32[]{:S(2)}, u32[]{:S(2)}) collective-permute-start(bf16[1,4,256,256]{3,2,1,0:T(8,128)(2,1)S(1)} %get-tuple-element.497), channel_id=1, source_target_pairs={{0,4},{2,6},{4,0},{6,2},{8,12},{10,14},{12,8},{14,10},{16,20},{18,... | collective-permute-start | bytes 1572872 | tf_op jit(solution)/shard_map/ppermute | solution.py:896
  490.5 39.3 %collective-permute-start.70 = (bf16[64,3840]{1,0:T(8,128)(2,1)S(1)}, bf16[64,3840]{1,0:T(8,128)(2,1)S(1)}, u32[]{:S(2)}, u32[]{:S(2)}) collective-permute-start(bf16[64,3840]{1,0:T(8,128)(2,1)S(1)} %get-tuple-element.484), channel_id=1, source_target_pairs={{0,4},{2,6},{4,0},{6,2},{8,12},{10,14},{12,8},{14,10},{16,20},{18,... | collective-permute-start | bytes 1474568 | tf_op jit(solution)/shard_map/ppermute | solution.py:896
  491.5 22.5 %collective-permute-start.62 = (bf16[16,64,256]{2,1,0:T(8,128)(2,1)S(1)}, bf16[16,64,256]{2,1,0:T(8,128)(2,1)S(1)}, u32[]{:S(2)}, u32[]{:S(2)}) collective-permute-start(bf16[16,64,256]{2,1,0:T(8,128)(2,1)S(1)} %pad_maximum_fusion.19), channel_id=1, source_target_pairs={{0,1},{1,0},{2,3},{3,2},{4,5},{5,4},{6,7},{7,6},{8,9},{9,8},{10,11... | collective-permute-start | bytes 1572872 | tf_op jit(solution)/shard_map/ppermute | solution.py:893
  501.8 28.6 %collective-permute-start.60 = (bf16[256,1024]{1,0:T(8,128)(2,1)S(1)}, bf16[256,1024]{1,0:T(8,128)(2,1)S(1)}, u32[]{:S(2)}, u32[]{:S(2)}) collective-permute-start(bf16[256,1024]{1,0:T(8,128)(2,1)S(1)} %bitcast.338), channel_id=1, source_target_pairs={{0,1},{1,0},{2,3},{3,2},{4,5},{5,4},{6,7},{7,6},{8,9},{9,8},{10,11... | collective-permute-start | bytes 1572872 | tf_op jit(solution)/shard_map/ppermute | solution.py:893
  506.3 34.4 %collective-permute-start.72 = (bf16[64,5632]{1,0:T(8,128)(2,1)S(1)}, bf16[64,5632]{1,0:T(8,128)(2,1)S(1)}, u32[]{:S(2)}, u32[]{:S(2)}) collective-permute-start(bf16[64,5632]{1,0:T(8,128)(2,1)S(1)} %get-tuple-element.466), channel_id=1, source_target_pairs={{0,8},{2,10},{4,12},{6,14},{8,0},{10,2},{12,4},{14,6},{16,24},{18,... | collective-permute-start | bytes 2162696 | tf_op jit(solution)/shard_map/ppermute | solution.py:896
  536.5 36.9 %collective-permute-start.71 = (bf16[32,3840]{1,0:T(8,128)(2,1)S(1)}, bf16[32,3840]{1,0:T(8,128)(2,1)S(1)}, u32[]{:S(2)}, u32[]{:S(2)}) collective-permute-start(bf16[32,3840]{1,0:T(8,128)(2,1)S(1)} %get-tuple-element.505), channel_id=1, source_target_pairs={{0,16},{2,18},{4,20},{6,22},{8,24},{10,26},{12,28},{14,30},{16,0},... | collective-permute-start | bytes 737288 | tf_op jit(solution)/shard_map/ppermute | solution.py:896
  541.5 31.9 %collective-permute-start.73 = (bf16[32,5632]{1,0:T(8,128)(2,1)S(1)}, bf16[32,5632]{1,0:T(8,128)(2,1)S(1)}, u32[]{:S(2)}, u32[]{:S(2)}) collective-permute-start(bf16[32,5632]{1,0:T(8,128)(2,1)S(1)} %get-tuple-element.487), channel_id=1, source_target_pairs={{0,16},{2,18},{4,20},{6,22},{8,24},{10,26},{12,28},{14,30},{16,0},... | collective-permute-start | bytes 1081352 | tf_op jit(solution)/shard_map/ppermute | solution.py:896
  (149 other events, 1551.4 us)
